TPU v7x, 128 devices: a whole 4x4x4 slice. The times are simulated.
128 devices in a mesh: rows: 8 (over z, core), cols: 16 (over x, y).
Axes of the slice: x: 4, y: 4, z: 4, core: 2. Of those that a mesh axis runs over, the one named last changes fastest.
Arguments:
- embeddings: bfloat16 [917504, 1024], P(('rows', 'cols'))
- factor_cols: bfloat16 [917504, 512], P(('rows', 'cols')), may hold values from -0.12 to 0.12, as said below
- solved: int32 [917504], P(('rows', 'cols')), may hold values from 0 to 16
- pivots: int32 [256], replicated, may hold values from 0 to 917503, as said below
Outputs:
- new_cols: bfloat16 [917504, 256], P(('rows', 'cols'))
- gains: float32 [917504], P(('rows', 'cols'))
- best_gain: float32 [], replicated
Inputs may be any that keep to these rules, and one draw needn't show every extreme that they name: `pivots`: 256 distinct row numbers in increasing order; the 7168 consecutive rows of one device hold at most 16 of them, and some device holds exactly 16. `factor_cols`: the pivots' factor rows F satisfy: every eigenvalue of F F^T is below 1.
All inputs are finite; a program needn't handle non-finite values.
Results may differ from a plain program's by a relative error of at most 0.001.
Values may be sent and summed in bfloat16 or wider, within the bound.
No kernel may reach another device: no remote copies, remote signals or barrier semaphores. Data moves between devices by JAX's collectives and lax.ppermute only.
A program may use at most 128 MiB of HBM per device.

v0:
```python
import jax
import jax.numpy as jnp
from jax import lax
from jax.sharding import PartitionSpec as P

PMAX = 16


EPS = 1e-06
TAU = 6.0
RIDGE = 1.0


def learn(counts):
    c = counts.astype(jnp.float32)
    return (c * (16.0 - c) + 8.0) / 72.0


def scales(emb):
    x = emb.astype(jnp.float32)
    return jnp.sqrt(jnp.mean(x * x, axis=1) + EPS)


def kernel_panel(
    left_emb, left_fac, left_q, left_norm, left_ids, piv_emb, piv_fac, piv_q, piv_norm, pivots
):
    dims = (((1,), (1,)), ((), ()))
    dots = lax.dot_general(left_emb, piv_emb, dims, preferred_element_type=jnp.float32)
    width = left_emb.shape[1] * 1.0
    cosine = dots / (width * left_norm[:, None] * piv_norm[None, :])
    similar = jnp.exp(TAU * (cosine - 1.0))
    ridge = jnp.where(left_ids[:, None] == pivots[None, :], RIDGE, 0.0)
    shared = lax.dot_general(left_fac, piv_fac, dims, preferred_element_type=jnp.float32)
    return left_q[:, None] * piv_q[None, :] * similar + ridge - shared


def body(embeddings, factor_cols, solved, pivots):
    rows_here = embeddings.shape[0]
    total = pivots.shape[0]
    device = lax.axis_index(("rows", "cols"))
    first_row = device * rows_here
    owner = pivots // rows_here
    before = jnp.sum((owner < device).astype(jnp.int32))
    mine = jnp.sum((owner == device).astype(jnp.int32))
    ranks = jnp.arange(PMAX, dtype=jnp.int32)
    valid = ranks < mine
    position = jnp.clip(before + ranks, 0, total - 1)
    local_idx = jnp.clip(pivots[position] - first_row, 0, rows_here - 1)
    keep = valid[:, None]
    own_emb = jnp.where(keep, embeddings[local_idx], 0)
    own_fac = jnp.where(keep, factor_cols[local_idx], 0)
    own_count = jnp.where(valid, solved[local_idx], 0).astype(jnp.bfloat16)
    place = (
        (jnp.arange(total, dtype=jnp.int32)[:, None] == (before + ranks)[None, :]) & valid[None, :]
    ).astype(jnp.float32)
    highest = lax.Precision.HIGHEST
    all_emb, all_fac, all_count = (
        lax.all_gather(own_emb, ("rows", "cols"), axis=0, tiled=True),
        lax.all_gather(own_fac, ("rows", "cols"), axis=0, tiled=True),
        lax.all_gather(own_count, ("rows", "cols"), axis=0, tiled=True),
    )
    earlier = jnp.sum((owner[None, :] < owner[:, None]).astype(jnp.int32), axis=1)
    slot_index = owner * PMAX + jnp.arange(total, dtype=jnp.int32) - earlier
    piv_emb = all_emb[slot_index]
    piv_fac = all_fac[slot_index]
    piv_count = all_count[slot_index].astype(jnp.float32)
    row_q = learn(solved)
    piv_q = learn(piv_count)
    piv_norm = scales(piv_emb)
    row_ids = first_row + jnp.arange(rows_here, dtype=jnp.int32)
    panel = kernel_panel(
        embeddings,
        factor_cols,
        row_q,
        scales(embeddings),
        row_ids,
        piv_emb,
        piv_fac,
        piv_q,
        piv_norm,
        pivots,
    )
    own_rows = jnp.where(keep, panel[local_idx], 0.0)
    block = lax.psum(jnp.dot(place, own_rows, precision=highest), ("rows", "cols"))
    lower = jnp.linalg.cholesky(block)
    full = jax.scipy.linalg.solve_triangular(lower, panel.T, lower=True).T
    facf = factor_cols.astype(jnp.float32)
    gains = row_q * row_q + RIDGE - jnp.sum(facf * facf, axis=1) - jnp.sum(full * full, axis=1)
    best = lax.pmax(jnp.max(gains), ("rows", "cols"))
    return (full.astype(jnp.bfloat16), gains, best)


def solution(mesh):
    in_specs = (P(("rows", "cols"), None), P(("rows", "cols"), None), P(("rows", "cols")), P())
    out_specs = (P(("rows", "cols"), None), P(("rows", "cols")), P())
    return jax.shard_map(body, mesh=mesh, in_specs=in_specs, out_specs=out_specs, check_vma=False)
```

profile of v0, /device:TPU:1, one launch (start us, length us, event | category | flops | bytes accessed | tf_op | source)
XLA Modules:
  0.0 518.1 jit_solution(16837783540909877693)
XLA Ops:
  7.2 1.3 fusion.28
  9.2 1.3 gather_fusion
  11.2 4.6 gather_fusion.5
  16.6 7.7 %gather_fusion.3 = bf16[16,1024]{1,0:T(8,128)(2,1)S(1)} fusion(bf16[7168,1024]{1,0:T(8,128)(2,1)} %param.4, s32[1024]{0:T(1024)S(1)} %pad_clamp_fusion.1), kind=kCustom, calls=%fused_computation.3 | custom fusion | bytes 65600 | tf_op jit(solution)/shard_map/gather | solution.py:50
  25.0 1.4 gather_fusion.1
  27.3 69.2 %all-reduce.1 = bf16[2048]{0:T(1024)(128)(2,1)S(1)} all-reduce(bf16[2048]{0:T(1024)(128)(2,1)S(1)} %dynamic-update-slice.11), channel_id=1, replica_groups=mesh['rows'=8,'cols'=16] {'rows','cols'}, use_global_device_ids=true, to_apply=%add.1 | all-reduce | flops 2048 | bytes 8192
  96.8 1.9 gather_fusion.2
  99.3 8.1 %multiply_reduce_fusion = f32[7168]{0:T(1024)S(1)} fusion(bf16[7168,1024]{1,0:T(8,128)(2,1)} %param.4), kind=kLoop, calls=%fused_computation.10 | loop fusion | flops 22012928 | bytes 14708736 | tf_op jit(solution)/shard_map/reduce_sum | solution.py:21
  107.5 3.1 gather_fusion.6
  110.6 42.8 %all-gather.3.cloned.1.call-done = bf16[2048,1024]{1,0:T(8,128)(2,1)} async-done(((bf16[16,1024]{1,0:T(8,128)(2,1)}), bf16[2048,1024]{1,0:T(8,128)(2,1)}) %all-gather.3.cloned.1.call-update) | async-done | bytes 4194320 | tf_op jit(solution)/shard_map/all_gather | solution.py:58
  153.4 4.3 gather_fusion.4
  157.7 16.8 %fusion.34 = f32[256,7168]{1,0:T(8,128)} fusion(bf16[256,1024]{1,0:T(8,128)(2,1)S(1)} %gather_fusion.4, bf16[7168,1024]{1,0:T(8,128)(2,1)} %param.4), kind=kOutput, calls=%fused_computation.90 | convolution fusion | flops 3758096384 | bytes 22544384 | tf_op jit(solution)/shard_map/dot_general | solution.py:28
  174.7 25.6 %add_subtract_fusion = (f32[256,7168]{1,0:T(8,128)}, f32[256,7168]{1,0:T(8,128)}) fusion(f32[256,7168]{1,0:T(8,128)} %fusion.34, s32[7168]{0:T(1024)S(1)} %iota_add_fusion, f32[256]{0:T(256)S(1)} %add_sqrt_fusion, f32[7168]{0:T(1024)S(1)} %get-tuple-element.44, f32[256]{0:T(256)S(1)} %fusion.26, f32[7168]{0:T(1024)S(1)} %get-tuple-element.43, ...), kind=kOutput, calls=%fused_computation.22 | convolution fusion | flops 1897398272 | bytes 29711360 | tf_op jit(solution)/shard_map/dot_general | solution.py:33
  200.3 7.2 %bitcast_subtract_fusion = f32[7168,256]{0,1:T(8,128)} fusion(f32[256,7168]{1,0:T(8,128)} %get-tuple-element.40, f32[256,7168]{1,0:T(8,128)S(1)} %bitcast.60, s32[7168]{0:T(1024)S(1)} %iota_add_fusion, f32[256]{0:T(256)S(1)} %add_sqrt_fusion, f32[7168]{0:T(1024)S(1)} %get-tuple-element.44, f32[256]{0:T(256)S(1)} %fusion.26, f32[7168]{0:T(1024)S(1)} %get-tuple-element.43, ...), kind=kLoop, calls=%fused_computation.14 | loop fusion | flops 18350080 | bytes 22109184 | tf_op jit(solution)/shard_map/sub | solution.py:34
  207.6 8.4 %copy.15 = f32[7168,256]{1,0:T(8,128)} copy(f32[7168,256]{0,1:T(8,128)} %bitcast_subtract_fusion) | data formatting | bytes 14680064 | tf_op jit(solution)/shard_map/sub | solution.py:34
  215.9 3.7 gather_fusion.7
  220.7 4.6 multiply_reduce_fusion.1
  225.3 135.9 %all-reduce.4.cloned.1.call-done = f32[256,256]{0,1:T(8,128)} async-done(((f32[256,256]{0,1:T(8,128)}), f32[256,256]{0,1:T(8,128)}) %all-reduce.4.cloned.1.call-update) | async-done | bytes 262160 | tf_op jit(solution)/shard_map/psum | solution.py:84
  363.3 11.7 %cholesky.50 = f32[128,128]{1,0:T(8,128)S(1)} custom-call(f32[128,128]{1,0:T(8,128)S(1)} %cholesky.118), custom_call_target="Cholesky" | custom-call | tf_op jit(solution)/shard_map/jit(cholesky)/cholesky | solution.py:85
  375.1 9.8 %custom-call.15 = f32[1,128,128]{1,2,0:T(8,128)S(1)} custom-call(f32[1,128,128]{2,1,0:T(8,128)S(1)} %get-tuple-element.38), custom_call_target="InvertDiagBlocksLowerTriangular" | custom-call | tf_op jit(solution)/shard_map/jit(cholesky)/cholesky | solution.py:85
  385.4 11.7 %cholesky.105 = f32[128,128]{1,0:T(8,128)S(1)} custom-call(f32[128,128]{1,0:T(8,128)S(1)} %convolution_subtract_fusion.1), custom_call_target="Cholesky" | custom-call | tf_op jit(solution)/shard_map/jit(cholesky)/cholesky | solution.py:85
  399.8 4.0 while.1
  400.4 1.4 bitcast_dynamic-update-slice_fusion.2
  402.4 1.4 bitcast_dynamic-update-slice_fusion.2
  403.8 19.9 %custom-call.16 = f32[2,128,128]{1,2,0:T(8,128)S(1)} custom-call(f32[2,128,128]{2,1,0:T(8,128)S(1)} %get-tuple-element.10), custom_call_target="InvertDiagBlocksLowerTriangular" | custom-call | tf_op jit(solution)/shard_map/jit(_solve_triangular)/triangular_solve | solution.py:86
  423.7 5.5 %fusion.7 = f32[128,7168]{1,0:T(8,128)S(1)} fusion(f32[256,7168]{1,0:T(8,128)} %get-tuple-element.39, f32[2,128,128]{1,2,0:T(8,128)S(1)} %custom-call.16), kind=kOutput, calls=%fused_computation.25 | convolution fusion | flops 1409286144 | bytes 7405568 | tf_op jit(solution)/shard_map/jit(_solve_triangular)/triangular_solve | solution.py:86
  429.2 5.3 %convolution_subtract_fusion = f32[128,7168]{1,0:T(8,128)S(1)} fusion(f32[128,7168]{1,0:T(8,128)S(1)} %fusion.7, f32[256,7168]{1,0:T(8,128)} %get-tuple-element.39, f32[256,256]{1,0:T(8,128)S(1)} %get-tuple-element.94), kind=kOutput, calls=%fused_computation.12 | convolution fusion | flops 1410203648 | bytes 11075584 | tf_op jit(solution)/shard_map/jit(_solve_triangular)/triangular_solve | solution.py:86
  434.5 3.5 fusion.14
  438.6 2.3 fusion.6
  440.9 1.2 fusion.32
  442.1 63.3 %pmax.7 = f32[]{:T(128)} all-reduce(f32[]{:T(128)} %get-tuple-element.30), channel_id=1, replica_groups=mesh['rows'=8,'cols'=16] {'rows','cols'}, use_global_device_ids=true, to_apply=%region_13.14 | all-reduce | flops 1 | bytes 8 | tf_op jit(solution)/shard_map/pmax | solution.py:89
  505.4 5.9 %copy.18 = bf16[7168,256]{1,0:T(8,128)(2,1)} copy(bf16[7168,256]{0,1:T(8,128)(2,1)} %fusion.6) | data formatting | bytes 7340032
  (55 shorter events, 11.7 us)
Async XLA Ops:
  7.2 100.4 %all-gather.5.cloned.1.call-start = ((), (), s32[]{:S(2)}) async-start(), calls=%async_computation.1 | async-start | bytes 2113536 | tf_op jit(solution)/shard_map/all_gather | solution.py:59
  16.5 136.8 %all-gather.3.cloned.1.call-start = ((), (), s32[]{:S(2)}) async-start(), calls=%async_computation | async-start | bytes 4227072 | tf_op jit(solution)/shard_map/all_gather | solution.py:58
  25.0 336.2 %all-reduce.4.cloned.1.call-start = ((), (), s32[]{:S(2)}) async-start(), calls=%async_computation.2 | async-start | bytes 524288 | tf_op jit(solution)/shard_map/psum | solution.py:84
  99.3 8.1 %copy-start.1 = (s32[7168]{0:T(1024)S(1)}, s32[7168]{0:T(1024)}, u32[]{:S(2)}) copy-start(s32[7168]{0:T(1024)} %param.6) | copy-start | bytes 86020
  157.7 17.0 %copy-start = (s32[256]{0:T(256)S(1)}, s32[256]{0:T(256)}, u32[]{:S(2)}) copy-start(s32[256]{0:T(256)} %param.7) | copy-start | bytes 3076
  174.5 25.9 %slice-start = ((s8[7340032]{0:T(1024)(128)(4,1)}), s8[4194304]{0:T(1024)(128)(4,1)S(1)}, s32[]{:S(2)}) async-start(s8[7340032]{0:T(1024)(128)(4,1)} %bitcast.59), calls=%async_computation.3 | async-start | bytes 8388608
  174.7 25.7 %slice-start.1 = ((s8[7340032]{0:T(1024)(128)(4,1)}), s8[3145728]{0:T(1024)(128)(4,1)S(1)}, s32[]{:S(2)}) async-start(s8[7340032]{0:T(1024)(128)(4,1)} %bitcast.59), calls=%async_computation.4 | async-start | bytes 6291456
Sparse Core Ops, SparseCore 0:
  16.6 69.0 all-gather.4
  89.4 63.9 all-gather.2
  220.8 140.3 all-reduce.3
where the time goes:
time: 522 us; the launch traced here: 518 us
  waiting for transfers between devices  179 us (34%)
  blocking collectives  133 us (25%)
  other arithmetic  85.1 us (16%)
  matrix products  58.3 us (11%)
  local copies, waits for them, and re-layouts  47.7 us (9%)
  between operations  15.6 us (3%)
    psum x1, waiting for transfers between devices, body(): lax.psum(jnp.dot(place, own_rows, precision=highest), ('rows', 'cols'))  136 us
    unnamed x1, blocking collectives  69.2 us
    pmax x1, blocking collectives, body(): best = lax.pmax(jnp.max(gains), ('rows', 'cols'))  63.3 us
    all_gather x1, waiting for transfers between devices, body(): lax.all_gather(own_emb, ('rows', 'cols'), axis=0, tiled=True)  42.8 us
    another operation x7, other arithmetic, body(): lower = jnp.linalg.cholesky(block)  34.6 us
    dot_general x1, matrix products, kernel_panel(): lax.dot_general(left_fac, piv_fac, dims, preferred_element_type=jnp.float32)  25.6 us
    another operation x3, other arithmetic, body(): full = jax.scipy.linalg.solve_triangular(lower, panel.T, lower=True).T  19.9 us
    dot_general x1, matrix products, kernel_panel(): lax.dot_general(left_emb, piv_emb, dims, preferred_element_type=jnp.float32)  16.8 us
  transfers between devices with their start and end apart: 3, of which 2 were waited for; matrix products, arithmetic and copies ran while one was open for 6% of the time, Pallas kernels for 0%

commit v1 on v0

v1 whole, which is shorter than its diff:
```python
import functools

import jax
import jax.numpy as jnp
from jax import lax
from jax.experimental import pallas as pl
from jax.experimental.pallas import tpu as pltpu
from jax.sharding import PartitionSpec as P

PMAX = 16
EPS = 1e-06
TAU = 6.0
RIDGE = 1.0
AXES = ("rows", "cols")
NDEV = 128
TILES = 8
BS = 32
F32 = jnp.float32
BF16 = jnp.bfloat16


def iota(shape, dim):
    return lax.broadcasted_iota(jnp.int32, shape, dim)


def learn(c):
    return (c * (16.0 - c) + 8.0) / 72.0


def gather_kernel(dev_ref, piv_s, piv_v, solved_ref, emb_ref, fac_ref, out_ref, ebuf, fbuf, sem):
    rows_here = emb_ref.shape[0]
    total = piv_s.shape[0]
    dim = emb_ref.shape[1]
    first = dev_ref[0] * rows_here
    pv = piv_v[...]
    before = jnp.sum((pv < first).astype(F32)).astype(jnp.int32)
    upto = jnp.sum((pv < first + rows_here).astype(F32)).astype(jnp.int32)
    mine = upto - before
    idx = []
    copies = []
    for s in range(PMAX):
        p = piv_s[jnp.minimum(before + s, total - 1)]
        i = jnp.clip(p - first, 0, rows_here - 1)
        idx.append(i)
        base = pl.multiple_of((i // 16) * 16, 16)
        c1 = pltpu.make_async_copy(
            emb_ref.at[pl.ds(base, 16), :], ebuf.at[pl.ds(16 * s, 16), :], sem.at[0, s]
        )
        c2 = pltpu.make_async_copy(
            fac_ref.at[pl.ds(base, 16), :], fbuf.at[pl.ds(16 * s, 16), :], sem.at[1, s]
        )
        c1.start()
        c2.start()
        copies += [c1, c2]
    r = iota((NDEV, 16 * PMAX), 0)
    q = iota((NDEV, 16 * PMAX), 1)
    rc = iota((NDEV, 128), 0)
    hot = jnp.zeros((NDEV, 16 * PMAX), F32)
    cnt = jnp.zeros((NDEV, 128), F32)
    for s in range(PMAX):
        home = jnp.where(s < mine, lax.rem(before + s, NDEV), -1)
        col = 16 * s + lax.rem(idx[s], 16)
        hot = jnp.where((r == home) & (q == col), 1.0, hot)
        c = solved_ref[idx[s] // 128, lax.rem(idx[s], 128)].astype(F32)
        cnt = jnp.where(rc == home, c, cnt)
    hot = hot.astype(BF16)
    for c in copies:
        c.wait()
    out_ref[:, 0:dim] = jnp.dot(hot, ebuf[...], preferred_element_type=F32).astype(BF16)
    out_ref[:, dim : dim + fbuf.shape[1]] = jnp.dot(
        hot, fbuf[...], preferred_element_type=F32
    ).astype(BF16)
    out_ref[:, dim + fbuf.shape[1] :] = cnt.astype(BF16)


def split3(x):
    h = x.astype(BF16)
    r = x - h.astype(F32)
    m = r.astype(BF16)
    l = (r - m.astype(F32)).astype(BF16)
    return h, m, l


def main_kernel(
    dev_ref, piv_ref, recv_ref, solved_ref, emb_ref, fac_ref,
    out_ref, gains_ref, best_ref,
    pivt, pvec, ar, minv, mt, panel, base,
):
    i = pl.program_id(0)
    tile = emb_ref.shape[0]
    dim = emb_ref.shape[1]
    k0 = fac_ref.shape[1]
    n = recv_ref.shape[0]
    half = n // 2
    nchunk = tile // 128
    tdims = (((0,), (0,)), ((), ()))

    @pl.when(i == 0)
    def _():
        jj = iota((n, n), 0)
        qq = iota((n, n), 1)
        perm = (qq == 2 * lax.rem(jj, half) + jj // half).astype(BF16)
        piv = jnp.dot(perm, recv_ref[...], preferred_element_type=F32)
        pt = piv.T
        pivt[...] = pt[0 : dim + k0, :].astype(BF16)
        ps = jnp.sqrt(jnp.sum(pt[0:dim, :] * pt[0:dim, :], axis=0, keepdims=True) / dim + EPS)
        pq = learn(pt[dim + k0 : dim + k0 + 1, :])
        pvec[0:1, :] = TAU / (dim * ps)
        pvec[1:2, :] = pq
        cs = jnp.sqrt(jnp.sum(piv[:, 0:dim] * piv[:, 0:dim], axis=1, keepdims=True) / dim + EPS)
        cq = learn(piv[:, dim + k0 : dim + k0 + 1])
        pb = piv.astype(BF16)
        dots = jnp.dot(pb[:, 0:dim], pivt[0:dim, :], preferred_element_type=F32)
        shared = jnp.dot(pb[:, dim : dim + k0], pivt[dim : dim + k0, :], preferred_element_type=F32)
        similar = jnp.exp(dots * (1.0 / cs) * pvec[0:1, :] - TAU)
        eye = (jj == qq).astype(F32)
        ar[:, 0:n] = similar * cq * pq + RIDGE * eye - shared
        ar[:, n : 2 * n] = eye

    @pl.when(i < TILES)
    def _():
        x = emb_ref[...]
        f = fac_ref[...]
        xf = x.astype(F32)
        ff = f.astype(F32)
        rs = jnp.sqrt(jnp.sum(xf * xf, axis=1, keepdims=True) / dim + EPS)
        fs = jnp.sum(ff * ff, axis=1, keepdims=True)
        st = solved_ref[pl.ds(i * nchunk, nchunk), :].astype(F32)
        ey = iota((128, 128), 0) == iota((128, 128), 1)
        cols = []
        for c in range(nchunk):
            b = jnp.broadcast_to(st[c : c + 1, :], (128, 128))
            cols.append(jnp.sum(jnp.where(ey, b, 0.0), axis=1, keepdims=True))
        q = learn(jnp.concatenate(cols, axis=0))
        base[pl.ds(pl.multiple_of(i * tile, tile), tile), :] = jnp.broadcast_to(
            q * q + RIDGE - fs, (tile, 128)
        )
        dots = jnp.dot(x, pivt[0:dim, :], preferred_element_type=F32)
        shared = jnp.dot(f, pivt[dim : dim + k0, :], preferred_element_type=F32)
        similar = jnp.exp(dots * (1.0 / rs) * pvec[0:1, :] - TAU)
        ids = dev_ref[0] * (tile * TILES) + i * tile + iota((tile, n), 0)
        ridge = jnp.where(ids == piv_ref[...], RIDGE, 0.0)
        p = similar * (q * pvec[1:2, :]) + ridge - shared
        ph = p.astype(BF16)
        plo = (p - ph.astype(F32)).astype(BF16)
        o = pl.ds(pl.multiple_of(i * tile, tile), tile)
        panel[o, 0:n] = ph
        panel[o, n : 2 * n] = plo

        rows = pl.ds(pl.multiple_of(i * BS, BS), BS)
        shift = lax.rem(n - i * BS, n)
        a = pltpu.roll(ar[rows, 0:n], shift, 1)
        w = jnp.concatenate([a, ar[rows, n : 2 * n]], axis=1)
        groups = [w[8 * g : 8 * g + 8, :] for g in range(BS // 8)]
        sub = iota((8, 1), 0)
        for k in range(BS):
            g0 = k // 8
            row = groups[g0][k % 8 : k % 8 + 1, :]
            inv = 1.0 / row[:, k : k + 1]
            srow = row * inv
            for g in range(g0, BS // 8):
                col = groups[g][:, k : k + 1]
                if g == g0:
                    if k % 8 == 7:
                        continue
                    col = jnp.where(sub > k % 8, col, 0.0)
                groups[g] = groups[g] - col * srow
        w = jnp.concatenate(groups, axis=0)
        d = jnp.sum(
            jnp.where(iota((BS, 128), 0) == iota((BS, 128), 1), w[:, 0:128], 0.0),
            axis=1, keepdims=True,
        )
        w = w * (1.0 / jnp.sqrt(d))
        u = pltpu.roll(w[:, 0:n], i * BS, 1)
        m = w[:, n : 2 * n]
        minv[rows, :] = m
        uh, um, ul = split3(u)
        mh, mm, ml = split3(m)
        left = jnp.concatenate([uh, uh, um, uh, ul, um], axis=0)
        r_a = jnp.concatenate([uh, um, uh, ul, uh, um], axis=0)
        r_m = jnp.concatenate([mh, mm, mh, ml, mh, mm], axis=0)
        ar[:, 0:n] -= lax.dot_general(left, r_a, tdims, preferred_element_type=F32)
        ar[:, n : 2 * n] -= lax.dot_general(left, r_m, tdims, preferred_element_type=F32)

    @pl.when(i == TILES)
    def _():
        t = minv[...].T
        h = t.astype(BF16)
        mt[0:n, :] = h
        mt[n : 2 * n, :] = h
        mt[2 * n : 3 * n, :] = (t - h.astype(F32)).astype(BF16)
        best_ref[...] = jnp.full(best_ref.shape, -jnp.inf, F32)

    @pl.when(i >= TILES)
    def _():
        t = i - TILES
        o = pl.ds(pl.multiple_of(t * tile, tile), tile)
        full = jnp.dot(panel[o, :], mt[0 : 2 * n, :], preferred_element_type=F32)
        full += jnp.dot(panel[o, 0:n], mt[2 * n : 3 * n, :], preferred_element_type=F32)
        out_ref[...] = full.astype(BF16)
        g = base[o, :] - jnp.sum(full * full, axis=1, keepdims=True)
        ey = iota((128, 128), 0) == iota((128, 128), 1)
        lines = []
        for c in range(nchunk):
            lines.append(
                jnp.sum(jnp.where(ey, g[128 * c : 128 * c + 128, :], 0.0), axis=0, keepdims=True)
            )
        gains_ref[pl.ds(t * nchunk, nchunk), :] = jnp.concatenate(lines, axis=0)
        best_ref[...] = jnp.maximum(best_ref[...], jnp.max(g))


def body(embeddings, factor_cols, solved, pivots):
    rows_here, dim = embeddings.shape
    k0 = factor_cols.shape[1]
    total = pivots.shape[0]
    width = dim + k0 + 128
    tile = rows_here // TILES
    device = lax.axis_index(AXES).astype(jnp.int32)
    dev = device.reshape(1)
    solved2 = solved.reshape(rows_here // 128, 128)
    piv2 = pivots.reshape(total // 128, 128)
    smem = pl.BlockSpec(memory_space=pltpu.SMEM)
    vmem = pl.BlockSpec(memory_space=pltpu.VMEM)
    hbm = pl.BlockSpec(memory_space=pl.ANY)
    send = pl.pallas_call(
        gather_kernel,
        out_shape=jax.ShapeDtypeStruct((NDEV, width), BF16),
        in_specs=[smem, smem, vmem, smem, hbm, hbm],
        out_specs=vmem,
        scratch_shapes=[
            pltpu.VMEM((16 * PMAX, dim), BF16),
            pltpu.VMEM((16 * PMAX, k0), BF16),
            pltpu.SemaphoreType.DMA((2, PMAX)),
        ],
        compiler_params=pltpu.CompilerParams(vmem_limit_bytes=8 << 20),
        name="own_rows",
    )(dev, pivots, piv2, solved2, embeddings, factor_cols)
    got = lax.all_to_all(send.reshape(NDEV, 1, width), AXES, 0, 0)
    owner = pivots // rows_here
    pair = [
        lax.dynamic_slice(got, (owner[device + NDEV * t], 0, 0), (1, 1, width))
        for t in range(total // NDEV)
    ]
    pair = jnp.concatenate(pair, axis=1)
    recv = lax.all_to_all(
        jnp.broadcast_to(pair, (NDEV, total // NDEV, width)), AXES, 0, 0
    ).reshape(total, width)
    new_cols, gains, best = pl.pallas_call(
        main_kernel,
        grid=(2 * TILES,),
        out_shape=(
            jax.ShapeDtypeStruct((rows_here, total), BF16),
            jax.ShapeDtypeStruct((rows_here // 128, 128), F32),
            jax.ShapeDtypeStruct((NDEV, 128), F32),
        ),
        in_specs=[
            smem, vmem, vmem, vmem,
            pl.BlockSpec((tile, dim), lambda i: (jnp.minimum(i, TILES - 1), 0)),
            pl.BlockSpec((tile, k0), lambda i: (jnp.minimum(i, TILES - 1), 0)),
        ],
        out_specs=(
            pl.BlockSpec((tile, total), lambda i: (jnp.maximum(i - TILES, 0), 0)),
            pl.BlockSpec((rows_here // 128, 128), lambda i: (0, 0)),
            pl.BlockSpec((NDEV, 128), lambda i: (0, 0)),
        ),
        scratch_shapes=[
            pltpu.VMEM((dim + k0, total), BF16),
            pltpu.VMEM((8, total), F32),
            pltpu.VMEM((total, 2 * total), F32),
            pltpu.VMEM((total, total), F32),
            pltpu.VMEM((3 * total, total), BF16),
            pltpu.VMEM((rows_here, 2 * total), BF16),
            pltpu.VMEM((rows_here, 128), F32),
        ],
        compiler_params=pltpu.CompilerParams(
            dimension_semantics=("arbitrary",), vmem_limit_bytes=48 << 20
        ),
        name="panel_factor",
    )(dev, pivots.reshape(1, total), recv, solved2, embeddings, factor_cols)
    peers = lax.all_to_all(best.reshape(NDEV, 1, 128), AXES, 0, 0)
    return new_cols, gains.reshape(rows_here), jnp.max(peers)


def solution(mesh):
    in_specs = (P(AXES, None), P(AXES, None), P(AXES), P())
    out_specs = (P(AXES, None), P(AXES), P())
    return jax.shard_map(body, mesh=mesh, in_specs=in_specs, out_specs=out_specs, check_vma=False)
```

time: 522 us -> 117 us (0.22)
  waiting for transfers between devices: 179 us -> 8.41 us
  blocking collectives: 133 us -> 35 us
  other arithmetic: 85.1 us -> 1.66 us
  matrix products: 58.3 us -> 0 us
  Pallas kernels: 0 us -> 42.5 us
  local copies, waits for them, and re-layouts: 47.7 us -> 13.4 us
  starting transfers between devices: 0.12 us -> 11.5 us
  between operations: 15.6 us -> 4.36 us
    psum x1 -> x0, waiting for transfers between devices: 136 us -> none  [body(): lax.psum(jnp.dot(place, own_rows, precision=highest), ('rows', 'cols'))]
    unnamed x1 -> x0, blocking collectives: 69.2 us -> none
    pmax x1 -> x0, blocking collectives: 63.3 us -> none  [body(): best = lax.pmax(jnp.max(gains), ('rows', 'cols'))]
    another operation x10 -> x0, other arithmetic: 54.5 us -> none  [the longest x7 34.6 us: body(): lower = jnp.linalg.cholesky(block)]
    dot_general x3 -> x0, matrix products: 43.5 us -> none  [the longest x1 25.6 us: kernel_panel(): lax.dot_general(left_fac, piv_fac, dims, preferred_element_type=jnp.float32)]
    all_gather x2 -> x0, waiting for transfers between devices: 42.8 us -> none  [the longest x1 42.8 us: body(): lax.all_gather(own_emb, ('rows', 'cols'), axis=0, tiled=True)]
    pallas_call x0 -> x2, Pallas kernels: none -> 42.5 us  [the longest x1 39.2 us: body(): pl.pallas_call(main_kernel, grid=(2 * TILES,), out_shape=(jax.ShapeDtypeS...]
    all_to_all x0 -> x2, blocking collectives: none -> 35 us  [the longest x1 21.1 us: body(): lax.all_to_all(jnp.broadcast_to(pair, (NDEV, total // NDEV, width)), AXES...]
  transfers between devices with their start and end apart: 3 -> 1, of which waited for: 2 -> 1; matrix products, arithmetic and copies ran while one was open for 6% -> 1% of each run, Pallas kernels for 0% -> 0%
where the time goes in v1:
time: 117 us
  Pallas kernels  42.5 us (36%)
  blocking collectives  35 us (30%)
  local copies, waits for them, and re-layouts  13.4 us (11%)
  starting transfers between devices  11.5 us (10%)
  waiting for transfers between devices  8.41 us (7%)
  between operations  4.36 us (4%)
  other arithmetic  1.66 us (1%)
    pallas_call x1, Pallas kernels, body(): pl.pallas_call(main_kernel, grid=(2 * TILES,), out_shape=(jax.ShapeDtypeS...  39.2 us
    all_to_all x1, blocking collectives, body(): lax.all_to_all(jnp.broadcast_to(pair, (NDEV, total // NDEV, width)), AXES...  21.1 us
    all_to_all x1, blocking collectives, body(): peers = lax.all_to_all(best.reshape(NDEV, 1, 128), AXES, 0, 0)  13.9 us
    all_to_all x1, starting transfers between devices, body(): got = lax.all_to_all(send.reshape(NDEV, 1, width), AXES, 0, 0)  11.5 us
    unnamed x14, local copies, waits for them, and re-layouts  11.5 us
    all_to_all x1, waiting for transfers between devices, body(): got = lax.all_to_all(send.reshape(NDEV, 1, width), AXES, 0, 0)  8.41 us
    pallas_call x1, Pallas kernels, body(): pl.pallas_call(gather_kernel, out_shape=jax.ShapeDtypeStruct((NDEV, width...  3.3 us
  transfers between devices with their start and end apart: 1, of which 1 were waited for; matrix products, arithmetic and copies ran while one was open for 1% of the time, Pallas kernels for 0%

profile of v1, /device:TPU:1, one launch (start us, length us, event | category | flops | bytes accessed | tf_op | source)
XLA Modules:
  0.0 116.9 jit_solution(15327983355505493008)
XLA Ops:
  0.6 0.0 copy-start
  0.6 5.2 %copy-done = bf16[7168,1024]{1,0:T(8,128)(2,1)S(1)} copy-done((bf16[7168,1024]{1,0:T(8,128)(2,1)S(1)}, bf16[7168,1024]{1,0:T(8,128)(2,1)}, u32[]{:S(2)}) %copy-start) | copy-done | bytes 14680088
  5.8 0.0 copy-start.1
  5.8 3.1 %copy-done.1 = bf16[7168,512]{1,0:T(8,128)(2,1)S(1)} copy-done((bf16[7168,512]{1,0:T(8,128)(2,1)S(1)}, bf16[7168,512]{1,0:T(8,128)(2,1)}, u32[]{:S(2)}) %copy-start.1) | copy-done | bytes 7340056
  8.9 0.0 copy-start.2
  8.9 0.7 copy-done.2
  9.6 0.0 copy-start.4
  9.6 0.7 copy-done.4
  10.3 0.0 copy-start.5
  10.3 3.3 %own_rows.1 = bf16[128,1664]{1,0:T(8,128)(2,1)S(1)} custom-call(s32[1]{0:T(128)} %bitcast.dev_ref, s32[256]{0:T(256)S(1)} %copy-done.4, s32[2,128]{1,0:T(2,128)S(1)} %bitcast.17, s32[56,128]{1,0:T(8,128)S(1)} %bitcast.14, bf16[7168,1024]{1,0:T(8,128)(2,1)S(1)} %copy-done, bf16[7168,512]{1,0:T(8,128)(2,1)S(1)} %copy-done.1), custom_call_target="tpu_custom_call" | custom-call | tf_op jit(solution)/shard_map/own_rows/pallas_call | solution.py:225
  13.6 0.0 copy-start.3
  13.6 0.5 broadcast.1
  14.2 0.9 reduce
  15.1 1.2 %reshape.38 = bf16[128,2,832]{2,1,0:T(2,128)(2,1)} reshape(bf16[128,1664]{1,0:T(8,128)(2,1)S(1)} %reduce) | data formatting | bytes 851968
  16.2 11.5 %all-to-all-start = ((bf16[128,2,832]{2,1,0:T(2,128)(2,1)}), bf16[128,2,832]{2,1,0:T(2,128)(2,1)S(1)}, u32[]{:S(2)}, u32[]{:S(2)}) async-start(bf16[128,2,832]{2,1,0:T(2,128)(2,1)} %reshape.38), calls=%async_computation | async-start | bytes 917504 | tf_op jit(solution)/shard_map/all_to_all | solution.py:238
  27.7 0.0 copy-done.5
  27.8 0.6 fusion
  32.0 8.4 %all-to-all-done = bf16[128,2,832]{2,1,0:T(2,128)(2,1)S(1)} async-done(((bf16[128,2,832]{2,1,0:T(2,128)(2,1)}), bf16[128,2,832]{2,1,0:T(2,128)(2,1)S(1)}, u32[]{:S(2)}, u32[]{:S(2)}) %all-to-all-start) | async-done | bytes 426016 | tf_op jit(solution)/shard_map/all_to_all | solution.py:238
  40.4 0.6 reshape.39
  41.0 0.4 broadcast_in_dim.8
  41.5 21.1 %all_to_all.15 = bf16[128,2,1664]{2,1,0:T(2,128)(2,1)S(1)} all-to-all(bf16[128,2,1664]{2,1,0:T(2,128)(2,1)S(1)} %broadcast_in_dim.8), channel_id=1, replica_groups=mesh['rows'=8,'cols'=16] {'rows','cols'}, dimensions={0} | all-to-all | bytes 1703936 | tf_op jit(solution)/shard_map/all_to_all | solution.py:245
  62.6 0.3 reshape.35.recv_ref
  63.0 0.0 copy-done.3
  63.0 39.2 %panel_factor.1 = (bf16[7168,256]{1,0:T(8,128)(2,1)}, f32[56,128]{1,0:T(8,128)}, f32[128,128]{1,0:T(8,128)S(1)}) custom-call(s32[1]{0:T(128)} %bitcast.dev_ref, s32[1,256]{1,0:T(1,128)S(1)} %bitcast.18, bf16[256,1664]{1,0:T(8,128)(2,1)S(1)} %reshape.35.recv_ref, s32[56,128]{1,0:T(8,128)S(1)} %bitcast.15, bf16[7168,1024]{1,0:T(8,128)(2,1)} %emb_ref.3, ...), custom_call_target="tpu_custom_call" | custom-call | tf_op jit(solution)/shard_map/panel_factor/pallas_call | solution.py:248
  102.2 13.9 %all_to_all.16 = f32[128,1,128]{2,1,0:T(1,128)S(1)} all-to-all(f32[128,1,128]{2,1,0:T(1,128)S(1)} %bitcast.16), channel_id=1, replica_groups=mesh['rows'=8,'cols'=16] {'rows','cols'}, dimensions={0} | all-to-all | bytes 131072 | tf_op jit(solution)/shard_map/all_to_all | solution.py:280
  116.1 0.7 reduce_max.9
  (3 shorter events, 0.1 us)
Async XLA Ops:
  0.6 5.2 %copy-start = (bf16[7168,1024]{1,0:T(8,128)(2,1)S(1)}, bf16[7168,1024]{1,0:T(8,128)(2,1)}, u32[]{:S(2)}) copy-start(bf16[7168,1024]{1,0:T(8,128)(2,1)} %emb_ref.3) | copy-start | bytes 44040196
  5.8 3.1 %copy-start.1 = (bf16[7168,512]{1,0:T(8,128)(2,1)S(1)}, bf16[7168,512]{1,0:T(8,128)(2,1)}, u32[]{:S(2)}) copy-start(bf16[7168,512]{1,0:T(8,128)(2,1)} %fac_ref.3) | copy-start | bytes 22020100
  8.9 0.7 copy-start.2
  9.6 0.7 copy-start.4
  10.3 17.4 %copy-start.5 = (s32[256]{0:T(256)S(1)}, s32[256]{0:T(256)}, u32[]{:S(2)}) copy-start(s32[256]{0:T(256)} %piv_s.1) | copy-start | bytes 3076
  13.6 49.3 %copy-start.3 = (s32[7168]{0:T(1024)S(1)}, s32[7168]{0:T(1024)}, u32[]{:S(2)}) copy-start(s32[7168]{0:T(1024)} %param.6) | copy-start | bytes 86020
  16.2 24.2 %all-to-all-start = ((bf16[128,2,832]{2,1,0:T(2,128)(2,1)}), bf16[128,2,832]{2,1,0:T(2,128)(2,1)S(1)}, u32[]{:S(2)}, u32[]{:S(2)}) async-start(bf16[128,2,832]{2,1,0:T(2,128)(2,1)} %reshape.38), calls=%async_computation | async-start | bytes 917504 | tf_op jit(solution)/shard_map/all_to_all | solution.py:238

commit v2 on v1

v2 whole, which is shorter than its diff:
```python
import functools

import jax
import jax.numpy as jnp
from jax import lax
from jax.experimental import pallas as pl
from jax.experimental.pallas import tpu as pltpu
from jax.sharding import PartitionSpec as P

PMAX = 16
EPS = 1e-06
TAU = 6.0
RIDGE = 1.0
AXES = ("rows", "cols")
NDEV = 128
CLASSES = 8
RING = 4
SUB = 4
LOG2E = 1.4426950408889634
TILES = 8
BS = 32
F32 = jnp.float32
BF16 = jnp.bfloat16


def iota(shape, dim):
    return lax.broadcasted_iota(jnp.int32, shape, dim)


def learn(c):
    return (c * (16.0 - c) + 8.0) / 72.0


def own_kernel(
    pos_ref, piv_s, piv_v, solved_ref, emb_ref, fac_ref, keep_ref, send_ref, loc_ref, ebuf, fbuf, sem
):
    rows_here, dim = emb_ref.shape
    k0 = fac_ref.shape[1]
    total = piv_s.shape[0]
    first = pos_ref[0] * rows_here
    z = pos_ref[1]
    core = pos_ref[2]
    pv = piv_v[...]
    before = jnp.sum((pv < first).astype(F32)).astype(jnp.int32)
    upto = jnp.sum((pv < first + rows_here).astype(F32)).astype(jnp.int32)
    mine = upto - before
    loc_ref[0] = before
    loc_ref[1] = mine
    idx = []
    copies = []
    for s in range(PMAX):
        p = piv_s[jnp.minimum(before + s, total - 1)]
        i = jnp.clip(p - first, 0, rows_here - 1)
        loc_ref[2 + s] = i
        idx.append(i)
        base = pl.multiple_of((i // 16) * 16, 16)
        c1 = pltpu.make_async_copy(
            emb_ref.at[pl.ds(base, 16), :], ebuf.at[pl.ds(16 * s, 16), :], sem.at[0, s]
        )
        c2 = pltpu.make_async_copy(
            fac_ref.at[pl.ds(base, 16), :], fbuf.at[pl.ds(16 * s, 16), :], sem.at[1, s]
        )
        c1.start()
        c2.start()
        copies += [c1, c2]
    r = iota((16, 16 * PMAX), 0)
    q = iota((16, 16 * PMAX), 1)
    rc = iota((16, 128), 0)
    lane = iota((16, 128), 1)
    hot = jnp.zeros((16, 16 * PMAX), F32)
    tag = jnp.zeros((16, 128), F32)
    for s in range(PMAX):
        j = before + s
        cls = lax.rem(j, CLASSES)
        row = 2 * jnp.bitwise_xor(cls // 2, z) + s // CLASSES
        row = row + jnp.where(lax.rem(cls, 2) == core, 0, 8)
        row = jnp.where(s < mine, row, -1)
        hot = jnp.where((r == row) & (q == 16 * s + lax.rem(idx[s], 16)), 1.0, hot)
        c = solved_ref[idx[s] // 128, lax.rem(idx[s], 128)].astype(F32)
        tag = jnp.where(rc == row, jnp.where(lane == 0, c, (j + 1).astype(F32)), tag)
    hot = hot.astype(BF16)
    for c in copies:
        c.wait()
    e = jnp.dot(hot, ebuf[...], preferred_element_type=F32).astype(BF16)
    f = jnp.dot(hot, fbuf[...], preferred_element_type=F32).astype(BF16)
    t = tag.astype(BF16)
    for o, ref in ((0, keep_ref), (8, send_ref)):
        ref[:, 0:dim] = e[o : o + 8, :]
        ref[:, dim : dim + k0] = f[o : o + 8, :]
        ref[:, dim + k0 :] = t[o : o + 8, :]


def split_kernel(keep_ref, recv_ref, *outs):
    both = jnp.concatenate([keep_ref[...], recv_ref[...]], axis=0)
    r = iota((8, 16), 0)
    q = iota((8, 16), 1)
    for k, out in enumerate(outs):
        want = jnp.where(r < 2, 2 * k + r, 8 + 2 * k + r - 2)
        hot = ((q == want) & (r < 4)).astype(BF16)
        out[...] = jnp.dot(hot, both, preferred_element_type=F32).astype(BF16)


def pack_kernel(*refs):
    out = refs[-1]
    data = jnp.concatenate([ref[...] for ref in refs[:-1]], axis=0)
    r = iota((16, 32), 0)
    q = iota((16, 32), 1)
    hot = (q == 8 * (r // 4) + lax.rem(r, 4)).astype(BF16)
    out[...] = jnp.dot(hot, data, preferred_element_type=F32).astype(BF16)


def slots_kernel(cls_ref, *refs):
    out = refs[-1]
    slots, width = out.shape
    data = jnp.concatenate([ref[...] for ref in refs[:-1]], axis=0)
    ids = data[:, width - 127 : width - 126].astype(F32)
    want = (CLASSES * iota((data.shape[0], slots), 1) + cls_ref[0] + 1).astype(F32)
    hot = (ids == want).astype(BF16)
    out[...] = lax.dot_general(
        hot, data, (((0,), (0,)), ((), ())), preferred_element_type=F32
    ).astype(BF16)


def norms_kernel(solved_ref, emb_ref, fac_ref, aux_ref):
    i = pl.program_id(0)
    tile, dim = emb_ref.shape
    nchunk = tile // 128
    st = solved_ref[pl.ds(i * nchunk, nchunk), :].astype(F32)
    ey = iota((128, 128), 0) == iota((128, 128), 1)
    lane = iota((128, 128), 1)
    for c in range(nchunk):
        o = slice(128 * c, 128 * c + 128)
        x = emb_ref[o, :].astype(F32)
        f = fac_ref[o, :].astype(F32)
        a = 1.0 / jnp.sqrt(jnp.sum(x * x, axis=1, keepdims=True) / dim + EPS)
        fs = jnp.sum(f * f, axis=1, keepdims=True)
        b = jnp.broadcast_to(st[c : c + 1, :], (128, 128))
        q = learn(jnp.sum(jnp.where(ey, b, 0.0), axis=1, keepdims=True))
        aux_ref[o, :] = jnp.where(lane == 0, a, jnp.where(lane == 1, q, q * q + RIDGE - fs))

def split3(x):
    h = x.astype(BF16)
    r = x - h.astype(F32)
    m = r.astype(BF16)
    l = (r - m.astype(F32)).astype(BF16)
    return h, m, l


def main_kernel(
    loc_ref, one_ref, two_ref, aux_ref, emb_ref, fac_ref,
    out_ref, gains_ref, best_ref,
    piv, pvec, ar, minv, mt, panel, base,
):
    i = pl.program_id(0)
    tile, dim = emb_ref.shape
    k0 = fac_ref.shape[1]
    n = piv.shape[0]
    nchunk = tile // 128
    sub = tile // SUB
    tdims = (((0,), (0,)), ((), ()))
    ndims = (((1,), (1,)), ((), ()))

    @pl.when(i == 0)
    def _():
        jj = iota((n, n), 0)
        qq = iota((n, n), 1)
        eye = (jj == qq).astype(F32)
        data = jnp.concatenate([one_ref[...], two_ref[...]], axis=0)
        ids = data[:, dim + k0 + 1 : dim + k0 + 2].astype(F32)
        permt = (ids == (qq + 1).astype(F32)).astype(BF16)
        v = lax.dot_general(permt, data, tdims, preferred_element_type=F32)
        pb = v.astype(BF16)
        piv[...] = pb[:, 0 : dim + k0]
        cs = 1.0 / jnp.sqrt(
            jnp.sum(v[:, 0:dim] * v[:, 0:dim], axis=1, keepdims=True) / dim + EPS
        )
        cq = learn(v[:, dim + k0 : dim + k0 + 1])
        rs = jnp.sum(eye * cs, axis=0, keepdims=True) * (TAU * LOG2E / dim)
        rq = jnp.sum(eye * cq, axis=0, keepdims=True)
        pvec[0:1, :] = rs
        pvec[1:2, :] = rq
        dots = lax.dot_general(pb[:, 0:dim], piv[:, 0:dim], ndims, preferred_element_type=F32)
        shared = lax.dot_general(
            pb[:, dim : dim + k0], piv[:, dim : dim + k0], ndims, preferred_element_type=F32
        )
        similar = jnp.exp2(dots * (cs * rs) - TAU * LOG2E)
        ar[:, 0:n] = similar * (cq * rq) + RIDGE * eye - shared
        ar[:, n : 2 * n] = eye

    @pl.when(i < TILES)
    def _():
        for c in range(SUB):
            o = slice(sub * c, sub * c + sub)
            a = aux_ref[o, 0:1]
            q = aux_ref[o, 1:2]
            dots = lax.dot_general(
                emb_ref[o, :], piv[:, 0:dim], ndims, preferred_element_type=F32
            )
            shared = lax.dot_general(
                fac_ref[o, :], piv[:, dim : dim + k0], ndims, preferred_element_type=F32
            )
            similar = jnp.exp2(dots * (a * pvec[0:1, :]) - TAU * LOG2E)
            p = similar * (q * pvec[1:2, :]) - shared
            ph = p.astype(BF16)
            w = pl.ds(pl.multiple_of(i * tile + sub * c, 16), sub)
            panel[w, 0:n] = ph
            panel[w, n : 2 * n] = (p - ph.astype(F32)).astype(BF16)
            base[w, :] = jnp.broadcast_to(aux_ref[o, 2:3], (sub, 128))

        rows = pl.ds(pl.multiple_of(i * BS, BS), BS)
        shift = lax.rem(n - i * BS, n)
        a = pltpu.roll(ar[rows, 0:n], shift, 1)
        w = jnp.concatenate([a, ar[rows, n : 2 * n]], axis=1)
        groups = [w[8 * g : 8 * g + 8, :] for g in range(BS // 8)]
        srows = iota((8, 1), 0)
        for k in range(BS):
            g0 = k // 8
            row = groups[g0][k % 8 : k % 8 + 1, :]
            srow = row * (1.0 / row[:, k : k + 1])
            for g in range(g0, BS // 8):
                col = groups[g][:, k : k + 1]
                if g == g0:
                    if k % 8 == 7:
                        continue
                    col = jnp.where(srows > k % 8, col, 0.0)
                groups[g] = groups[g] - col * srow
        w = jnp.concatenate(groups, axis=0)
        d = jnp.sum(
            jnp.where(iota((BS, 128), 0) == iota((BS, 128), 1), w[:, 0:128], 0.0),
            axis=1, keepdims=True,
        )
        w = w * (1.0 / jnp.sqrt(d))
        u = pltpu.roll(w[:, 0:n], i * BS, 1)
        m = w[:, n : 2 * n]
        minv[rows, :] = m
        uh, um, ul = split3(u)
        mh, mm, ml = split3(m)
        left = jnp.concatenate([uh, uh, um, uh, ul, um], axis=0)
        r_a = jnp.concatenate([uh, um, uh, ul, uh, um], axis=0)
        r_m = jnp.concatenate([mh, mm, mh, ml, mh, mm], axis=0)
        ar[:, 0:n] -= lax.dot_general(left, r_a, tdims, preferred_element_type=F32)
        ar[:, n : 2 * n] -= lax.dot_general(left, r_m, tdims, preferred_element_type=F32)

    @pl.when(i == TILES)
    def _():
        t = minv[...].T
        h = t.astype(BF16)
        mt[0:n, :] = h
        mt[n : 2 * n, :] = h
        mt[2 * n : 3 * n, :] = (t - h.astype(F32)).astype(BF16)
        best_ref[...] = jnp.full(best_ref.shape, -jnp.inf, F32)

        def ridge(s, carry):
            at = loc_ref[2 + s]
            w = pl.ds(pl.multiple_of((at // 16) * 16, 16), 16)
            p = panel[w, 0:n].astype(F32) + panel[w, n : 2 * n].astype(F32)
            here = (iota((16, n), 0) == lax.rem(at, 16)) & (iota((16, n), 1) == loc_ref[0] + s)
            p = p + jnp.where(here, RIDGE, 0.0)
            ph = p.astype(BF16)
            panel[w, 0:n] = ph
            panel[w, n : 2 * n] = (p - ph.astype(F32)).astype(BF16)
            return carry

        lax.fori_loop(0, jnp.minimum(loc_ref[1], PMAX), ridge, 0)

    @pl.when(i >= TILES)
    def _():
        t = i - TILES
        gs = []
        for c in range(SUB):
            o = slice(sub * c, sub * c + sub)
            w = pl.ds(pl.multiple_of(t * tile + sub * c, 16), sub)
            full = jnp.dot(panel[w, :], mt[0 : 2 * n, :], preferred_element_type=F32)
            full += jnp.dot(panel[w, 0:n], mt[2 * n : 3 * n, :], preferred_element_type=F32)
            out_ref[o, :] = full.astype(BF16)
            gs.append(base[w, :] - jnp.sum(full * full, axis=1, keepdims=True))
        g = jnp.concatenate(gs, axis=0)
        ey = iota((128, 128), 0) == iota((128, 128), 1)
        lines = []
        for c in range(nchunk):
            lines.append(
                jnp.sum(jnp.where(ey, g[128 * c : 128 * c + 128, :], 0.0), axis=0, keepdims=True)
            )
        lines = jnp.concatenate(lines, axis=0)
        gains_ref[pl.ds(t * nchunk, nchunk), :] = lines
        best_ref[...] = jnp.maximum(best_ref[...], jnp.max(lines))


def ring(values, axis, pairs):
    return [lax.ppermute(v, axis, p) for v, p in zip(values, pairs)]


def body(embeddings, factor_cols, solved, pivots):
    rows_here, dim = embeddings.shape
    k0 = factor_cols.shape[1]
    total = pivots.shape[0]
    width = dim + k0 + 128
    tile = rows_here // TILES
    r = lax.axis_index("rows").astype(jnp.int32)
    c = lax.axis_index("cols").astype(jnp.int32)
    pos = jnp.stack([r * 16 + c, r // 2, r % 2])
    solved2 = solved.reshape(rows_here // 128, 128)
    piv2 = pivots.reshape(total // 128, 128)
    smem = pl.BlockSpec(memory_space=pltpu.SMEM)
    vmem = pl.BlockSpec(memory_space=pltpu.VMEM)
    hbm = pl.BlockSpec(memory_space=pltpu.HBM)
    small = pltpu.CompilerParams(vmem_limit_bytes=8 << 20)
    wide = lambda rows: jax.ShapeDtypeStruct((rows, width), BF16)
    swap = [(i, i ^ 1) for i in range(8)]
    zs = [[(i, i ^ (2 * k)) for i in range(8)] for k in range(1, RING)]
    xs = [[(i, i ^ (4 * k)) for i in range(16)] for k in range(1, RING)]
    ys = [[(i, i ^ k) for i in range(16)] for k in range(1, RING)]

    keep, send, loc = pl.pallas_call(
        own_kernel,
        out_shape=(wide(8), wide(8), jax.ShapeDtypeStruct((2 + PMAX,), jnp.int32)),
        in_specs=[smem, smem, vmem, smem, hbm, hbm],
        out_specs=(vmem, vmem, smem),
        scratch_shapes=[
            pltpu.VMEM((16 * PMAX, dim), BF16),
            pltpu.VMEM((16 * PMAX, k0), BF16),
            pltpu.SemaphoreType.DMA((2, PMAX)),
        ],
        compiler_params=small,
        name="own_rows",
    )(pos, pivots, piv2, solved2, embeddings, factor_cols)
    aux = pl.pallas_call(
        norms_kernel,
        grid=(TILES,),
        out_shape=jax.ShapeDtypeStruct((rows_here, 128), F32),
        in_specs=[
            vmem,
            pl.BlockSpec((tile, dim), lambda i: (i, 0)),
            pl.BlockSpec((tile, k0), lambda i: (i, 0)),
        ],
        out_specs=pl.BlockSpec((tile, 128), lambda i: (i, 0)),
        compiler_params=pltpu.CompilerParams(
            dimension_semantics=("arbitrary",), vmem_limit_bytes=40 << 20
        ),
        cost_estimate=pl.CostEstimate(
            flops=rows_here * (dim + k0) * 4, bytes_accessed=rows_here * (dim + k0) * 2,
            transcendentals=0,
        ),
        name="row_norms",
    )(solved2, embeddings, factor_cols)
    recv = lax.ppermute(send, "rows", swap)
    parts = pl.pallas_call(
        split_kernel, out_shape=(wide(8),) * RING, compiler_params=small, name="by_class",
    )(keep, recv)
    got = [parts[0]] + ring(parts[1:], "rows", zs)
    mine = pl.pallas_call(
        pack_kernel, out_shape=wide(16), compiler_params=small, name="pack",
    )(*got)
    got = [mine] + ring([mine] * 3, "cols", xs)
    mine = pl.pallas_call(
        slots_kernel,
        out_shape=wide(total // CLASSES),
        in_specs=[smem] + [vmem] * RING,
        out_specs=vmem,
        compiler_params=small,
        name="slots",
    )(r.reshape(1), *got)
    got = [mine] + ring([mine] * 3, "cols", ys)
    mine = got[0] + got[1] + got[2] + got[3]
    got = [mine] + ring([mine] * 3, "rows", zs)
    one = jnp.concatenate(got, axis=0)
    two = lax.ppermute(one, "rows", swap)

    new_cols, gains, best = pl.pallas_call(
        main_kernel,
        grid=(2 * TILES,),
        out_shape=(
            jax.ShapeDtypeStruct((rows_here, total), BF16),
            jax.ShapeDtypeStruct((rows_here // 128, 128), F32),
            jax.ShapeDtypeStruct((NDEV, 128), F32),
        ),
        in_specs=[
            smem, vmem, vmem,
            pl.BlockSpec((tile, 128), lambda i: (jnp.minimum(i, TILES - 1), 0)),
            pl.BlockSpec((tile, dim), lambda i: (jnp.minimum(i, TILES - 1), 0)),
            pl.BlockSpec((tile, k0), lambda i: (jnp.minimum(i, TILES - 1), 0)),
        ],
        out_specs=(
            pl.BlockSpec((tile, total), lambda i: (jnp.maximum(i - TILES, 0), 0)),
            pl.BlockSpec((rows_here // 128, 128), lambda i: (0, 0)),
            pl.BlockSpec((NDEV, 128), lambda i: (0, 0)),
        ),
        scratch_shapes=[
            pltpu.VMEM((total, dim + k0), BF16),
            pltpu.VMEM((8, total), F32),
            pltpu.VMEM((total, 2 * total), F32),
            pltpu.VMEM((total, total), F32),
            pltpu.VMEM((3 * total, total), BF16),
            pltpu.VMEM((rows_here, 2 * total), BF16),
            pltpu.VMEM((rows_here, 128), F32),
        ],
        compiler_params=pltpu.CompilerParams(
            dimension_semantics=("arbitrary",), vmem_limit_bytes=48 << 20
        ),
        name="panel_factor",
    )(loc, one, two, aux, embeddings, factor_cols)
    peers = lax.all_to_all(best.reshape(NDEV, 1, 128), AXES, 0, 0)
    return new_cols, gains.reshape(rows_here), jnp.max(peers)


def solution(mesh):
    in_specs = (P(AXES, None), P(AXES, None), P(AXES), P())
    out_specs = (P(AXES, None), P(AXES), P())
    return jax.shard_map(body, mesh=mesh, in_specs=in_specs, out_specs=out_specs, check_vma=False)
```

time: 117 us -> 119 us (1.017)
  blocking collectives: 35 us -> 14.9 us
  starting transfers between devices: 11.5 us -> 23 us
  Pallas kernels: 42.5 us -> 52.9 us
  waiting for transfers between devices: 8.41 us -> 16.2 us
  local copies, waits for them, and re-layouts: 13.4 us -> 9.69 us
  between operations: 4.36 us -> 0.73 us
    ppermute x0 -> x14, starting transfers between devices: none -> 23 us  [the longest x12 15.3 us: ring(): return [lax.ppermute(v, axis, p) for v, p in zip(values, pairs)]]
    all_to_all x1 -> x0, blocking collectives: 21.1 us -> none  [body(): lax.all_to_all(jnp.broadcast_to(pair, (NDEV, total // NDEV, width)), AXES...]
    ppermute x0 -> x14, waiting for transfers between devices: none -> 16.2 us  [the longest x12 15.4 us: ring(): return [lax.ppermute(v, axis, p) for v, p in zip(values, pairs)]]
    all_to_all x1 -> x0, starting transfers between devices: 11.5 us -> none  [body(): got = lax.all_to_all(send.reshape(NDEV, 1, width), AXES, 0, 0)]
    pallas_call x1 -> x5, Pallas kernels: 3.3 us -> 14.7 us  [the longest x1 10.6 us: body(): pl.pallas_call(norms_kernel, grid=(TILES,), out_shape=jax.ShapeDtypeStruc...]
    all_to_all x1 -> x0, waiting for transfers between devices: 8.41 us -> none  [body(): got = lax.all_to_all(send.reshape(NDEV, 1, width), AXES, 0, 0)]
    unnamed x14 -> x12, local copies, waits for them, and re-layouts: 11.5 us -> 9.69 us
  transfers between devices with their start and end apart: 1 -> 14, of which waited for: 1 -> 9; matrix products, arithmetic and copies ran while one was open for 1% -> 0% of each run, Pallas kernels for 0% -> 9%
where the time goes in v2:
time: 119 us; the launch traced here: 118 us
  Pallas kernels  52.9 us (44%)
  starting transfers between devices  23 us (19%)
  waiting for transfers between devices  16.2 us (14%)
  blocking collectives  14.9 us (13%)
  local copies, waits for them, and re-layouts  9.69 us (8%)
    pallas_call x1, Pallas kernels, body(): pl.pallas_call(main_kernel, grid=(2 * TILES,), out_shape=(jax.ShapeDtypeS...  38.2 us
    ppermute x12, waiting for transfers between devices, ring(): return [lax.ppermute(v, axis, p) for v, p in zip(values, pairs)]  15.4 us
    ppermute x12, starting transfers between devices, ring(): return [lax.ppermute(v, axis, p) for v, p in zip(values, pairs)]  15.3 us
    all_to_all x1, blocking collectives, body(): peers = lax.all_to_all(best.reshape(NDEV, 1, 128), AXES, 0, 0)  14.9 us
    pallas_call x1, Pallas kernels, body(): pl.pallas_call(norms_kernel, grid=(TILES,), out_shape=jax.ShapeDtypeStruc...  10.6 us
    unnamed x12, local copies, waits for them, and re-layouts  9.69 us
    ppermute x1, starting transfers between devices, body(): two = lax.ppermute(one, 'rows', swap)  6.29 us
    pallas_call x1, Pallas kernels, body(): pl.pallas_call(own_kernel, out_shape=(wide(8), wide(8), jax.ShapeDtypeStr...  3.55 us
  transfers between devices with their start and end apart: 14, of which 9 were waited for; matrix products, arithmetic and copies ran while one was open for 0% of the time, Pallas kernels for 9%

profile of v2, /device:TPU:1, one launch (start us, length us, event | category | flops | bytes accessed | tf_op | source)
XLA Modules:
  0.0 118.3 jit_solution(7116624423171793132)
XLA Ops:
  0.7 5.2 %copy-done = bf16[7168,1024]{1,0:T(8,128)(2,1)S(1)} copy-done((bf16[7168,1024]{1,0:T(8,128)(2,1)S(1)}, bf16[7168,1024]{1,0:T(8,128)(2,1)}, u32[]{:S(2)}) %copy-start) | copy-done | bytes 14680088
  5.9 3.1 %copy-done.1 = bf16[7168,512]{1,0:T(8,128)(2,1)S(1)} copy-done((bf16[7168,512]{1,0:T(8,128)(2,1)S(1)}, bf16[7168,512]{1,0:T(8,128)(2,1)}, u32[]{:S(2)}) %copy-start.1) | copy-done | bytes 7340056
  9.0 0.7 copy-done.3
  9.7 0.7 copy-done.5
  10.4 3.5 %own_rows.1 = (bf16[8,1664]{1,0:T(8,128)(2,1)S(1)}, bf16[8,1664]{1,0:T(8,128)(2,1)S(1)}, s32[18]{0:T(128)S(1)}) custom-call(s32[3]{0:T(128)S(1)} %pad_add_fusion.pos_ref, s32[256]{0:T(256)S(1)} %copy-done.5, s32[2,128]{1,0:T(2,128)S(1)} %bitcast.13, s32[56,128]{1,0:T(8,128)S(1)} %bitcast.10, bf16[7168,1024]{1,0:T(8,128)(2,1)S(1)} %copy-done, ...), custom_call_target="tpu_custom_call" | custom-call | tf_op jit(solution)/shard_map/own_rows/pallas_call | solution.py:314
  14.0 1.5 %collective-permute-start = (bf16[8,1664]{1,0:T(8,128)(2,1)S(1)}, bf16[8,1664]{1,0:T(8,128)(2,1)S(1)}, u32[]{:S(2)}, u32[]{:S(2)}) collective-permute-start(bf16[8,1664]{1,0:T(8,128)(2,1)S(1)} %get-tuple-element.15), channel_id=1, source_target_pairs={{0,16},{16,0},{32,48},{48,32},{64,80},{80,64},{96,112},{112,96},{1... | collective-permute-start | bytes 79880 | tf_op jit(solution)/shard_map/ppermute | solution.py:346
  15.4 0.9 collective-permute-done.recv_ref
  16.3 0.2 by_class.1
  16.5 1.8 %collective-permute-start.1 = (bf16[8,1664]{1,0:T(8,128)(2,1)S(1)}, bf16[8,1664]{1,0:T(8,128)(2,1)S(1)}, u32[]{:S(2)}, u32[]{:S(2)}) collective-permute-start(bf16[8,1664]{1,0:T(8,128)(2,1)S(1)} %get-tuple-element.17), channel_id=1, source_target_pairs={{0,32},{16,48},{32,0},{48,16},{64,96},{80,112},{96,64},{112,80},{1... | collective-permute-start | bytes 79880 | tf_op jit(solution)/shard_map/ppermute | solution.py:290
  18.3 3.3 %collective-permute-start.2 = (bf16[8,1664]{1,0:T(8,128)(2,1)S(1)}, bf16[8,1664]{1,0:T(8,128)(2,1)S(1)}, u32[]{:S(2)}, u32[]{:S(2)}) collective-permute-start(bf16[8,1664]{1,0:T(8,128)(2,1)S(1)} %get-tuple-element.18), channel_id=1, source_target_pairs={{0,64},{16,80},{32,96},{48,112},{64,0},{80,16},{96,32},{112,48},{1... | collective-permute-start | bytes 79880 | tf_op jit(solution)/shard_map/ppermute | solution.py:290
  21.6 1.5 %collective-permute-done.2.refs_2_ = bf16[8,1664]{1,0:T(8,128)(2,1)S(1)} collective-permute-done((bf16[8,1664]{1,0:T(8,128)(2,1)S(1)}, bf16[8,1664]{1,0:T(8,128)(2,1)S(1)}, u32[]{:S(2)}, u32[]{:S(2)}) %collective-permute-start.2) | collective-permute-done | bytes 26656 | tf_op jit(solution)/shard_map/ppermute | solution.py:290
  23.1 2.4 %collective-permute-done.3.refs_3_ = bf16[8,1664]{1,0:T(8,128)(2,1)S(1)} collective-permute-done((bf16[8,1664]{1,0:T(8,128)(2,1)S(1)}, bf16[8,1664]{1,0:T(8,128)(2,1)S(1)}, u32[]{:S(2)}, u32[]{:S(2)}) %collective-permute-start.3) | collective-permute-done | bytes 26656 | tf_op jit(solution)/shard_map/ppermute | solution.py:290
  25.7 2.6 %collective-permute-start.6 = (bf16[16,1664]{1,0:T(8,128)(2,1)S(1)}, bf16[16,1664]{1,0:T(8,128)(2,1)S(1)}, u32[]{:S(2)}, u32[]{:S(2)}) collective-permute-start(bf16[16,1664]{1,0:T(8,128)(2,1)S(1)} %pack.1.refs_0_), channel_id=1, source_target_pairs={{0,12},{1,13},{2,14},{3,15},{4,8},{5,9},{6,10},{7,11},{8,4},{9,5},... | collective-permute-start | bytes 159752 | tf_op jit(solution)/shard_map/ppermute | solution.py:290
  28.2 0.5 collective-permute-start.5
  28.7 0.3 collective-permute-start.4
  29.0 0.9 collective-permute-done.6.refs_3_
  29.9 2.9 %collective-permute-done.5.refs_2_ = bf16[16,1664]{1,0:T(8,128)(2,1)S(1)} collective-permute-done((bf16[16,1664]{1,0:T(8,128)(2,1)S(1)}, bf16[16,1664]{1,0:T(8,128)(2,1)S(1)}, u32[]{:S(2)}, u32[]{:S(2)}) %collective-permute-start.5) | collective-permute-done | bytes 53280 | tf_op jit(solution)/shard_map/ppermute | solution.py:290
  32.8 0.3 slots.1
  33.1 2.8 %collective-permute-start.9 = (bf16[32,1664]{1,0:T(8,128)(2,1)S(1)}, bf16[32,1664]{1,0:T(8,128)(2,1)S(1)}, u32[]{:S(2)}, u32[]{:S(2)}) collective-permute-start(bf16[32,1664]{1,0:T(8,128)(2,1)S(1)} %slots.1), channel_id=1, source_target_pairs={{0,3},{1,2},{2,1},{3,0},{4,7},{5,6},{6,5},{7,4},{8,11},{9,10},{10,... | collective-permute-start | bytes 319496 | tf_op jit(solution)/shard_map/ppermute | solution.py:290
  35.9 0.3 collective-permute-start.8
  36.3 0.3 collective-permute-start.7
  36.6 2.1 %collective-permute-done.9 = bf16[32,1664]{1,0:T(8,128)(2,1)S(1)} collective-permute-done((bf16[32,1664]{1,0:T(8,128)(2,1)S(1)}, bf16[32,1664]{1,0:T(8,128)(2,1)S(1)}, u32[]{:S(2)}, u32[]{:S(2)}) %collective-permute-start.9) | collective-permute-done | bytes 106528 | tf_op jit(solution)/shard_map/ppermute | solution.py:290
  38.7 2.3 %collective-permute-done.8 = bf16[32,1664]{1,0:T(8,128)(2,1)S(1)} collective-permute-done((bf16[32,1664]{1,0:T(8,128)(2,1)S(1)}, bf16[32,1664]{1,0:T(8,128)(2,1)S(1)}, u32[]{:S(2)}, u32[]{:S(2)}) %collective-permute-start.8) | collective-permute-done | bytes 106528 | tf_op jit(solution)/shard_map/ppermute | solution.py:290
  41.0 0.3 collective-permute-start.12
  41.5 2.9 %collective-permute-start.10 = (bf16[32,1664]{1,0:T(8,128)(2,1)S(1)}, bf16[32,1664]{1,0:T(8,128)(2,1)S(1)}, u32[]{:S(2)}, u32[]{:S(2)}) collective-permute-start(bf16[32,1664]{1,0:T(8,128)(2,1)S(1)} %add_add_fusion), channel_id=1, source_target_pairs={{0,32},{16,48},{32,0},{48,16},{64,96},{80,112},{96,64},{112,80},{1... | collective-permute-start | bytes 319496 | tf_op jit(solution)/shard_map/ppermute | solution.py:290
  44.4 2.7 %collective-permute-done.12 = bf16[32,1664]{1,0:T(8,128)(2,1)S(1)} collective-permute-done((bf16[32,1664]{1,0:T(8,128)(2,1)S(1)}, bf16[32,1664]{1,0:T(8,128)(2,1)S(1)}, u32[]{:S(2)}, u32[]{:S(2)}) %collective-permute-start.12) | collective-permute-done | bytes 106528 | tf_op jit(solution)/shard_map/ppermute | solution.py:290
  47.0 0.6 collective-permute-done.10
  47.6 6.3 %collective-permute-start.13 = (bf16[128,1664]{1,0:T(8,128)(2,1)S(1)}, bf16[128,1664]{1,0:T(8,128)(2,1)S(1)}, u32[]{:S(2)}, u32[]{:S(2)}) collective-permute-start(bf16[128,1664]{1,0:T(8,128)(2,1)S(1)} %pad_maximum_fusion.one_ref), channel_id=1, source_target_pairs={{0,16},{16,0},{32,48},{48,32},{64,80},{80,64},{96,112},{112,96},{1... | collective-permute-start | bytes 1277960 | tf_op jit(solution)/shard_map/ppermute | solution.py:367
  53.9 10.6 %row_norms.1.aux_ref = f32[7168,128]{1,0:T(8,128)S(1)} custom-call(s32[56,128]{1,0:T(8,128)S(1)} %bitcast.11, bf16[7168,1024]{1,0:T(8,128)(2,1)} %emb_ref.5, bf16[7168,512]{1,0:T(8,128)(2,1)S(1)} %copy-done.2), custom_call_target="tpu_custom_call" | custom-call | flops 44040192 | bytes 22020096 | tf_op jit(solution)/shard_map/row_norms/pallas_call | solution.py:327
  64.5 38.2 %panel_factor.1 = (bf16[7168,256]{1,0:T(8,128)(2,1)}, f32[56,128]{1,0:T(8,128)}, f32[128,128]{1,0:T(8,128)S(1)}) custom-call(s32[18]{0:T(128)S(1)} %get-tuple-element.13.loc_ref, bf16[128,1664]{1,0:T(8,128)(2,1)S(1)} %pad_maximum_fusion.one_ref, bf16[128,1664]{1,0:T(8,128)(2,1)S(1)} %collective-permute-done.13.two_ref, f32[7168,128]{1,0:T(8,128)S(1)} %row_norms.1.aux_ref, ...), custom_call_target="tpu_custom_call" | custom-call | tf_op jit(solution)/shard_map/panel_factor/pallas_call | solution.py:369
  102.7 14.9 %all_to_all.5 = f32[128,1,128]{2,1,0:T(1,128)S(1)} all-to-all(f32[128,1,128]{2,1,0:T(1,128)S(1)} %bitcast.12), channel_id=1, replica_groups=mesh['rows'=8,'cols'=16] {'rows','cols'}, dimensions={0} | all-to-all | bytes 131072 | tf_op jit(solution)/shard_map/all_to_all | solution.py:402
  117.6 0.7 reduce_max.9
  (19 shorter events, 0.4 us)
Async XLA Ops:
  0.7 5.2 %copy-start = (bf16[7168,1024]{1,0:T(8,128)(2,1)S(1)}, bf16[7168,1024]{1,0:T(8,128)(2,1)}, u32[]{:S(2)}) copy-start(bf16[7168,1024]{1,0:T(8,128)(2,1)} %emb_ref.5) | copy-start | bytes 44040196
  5.9 3.1 %copy-start.1 = (bf16[7168,512]{1,0:T(8,128)(2,1)S(1)}, bf16[7168,512]{1,0:T(8,128)(2,1)}, u32[]{:S(2)}) copy-start(bf16[7168,512]{1,0:T(8,128)(2,1)} %fac_ref.5) | copy-start | bytes 22020100
  9.0 0.7 copy-start.3
  9.7 0.7 copy-start.5
  10.4 43.5 %copy-start.2 = (bf16[7168,512]{1,0:T(8,128)(2,1)S(1)}, bf16[7168,512]{1,0:T(8,128)(2,1)}, u32[]{:S(2)}) copy-start(bf16[7168,512]{1,0:T(8,128)(2,1)} %fac_ref.5) | copy-start | bytes 22020100
  10.4 43.5 %copy-start.4 = (s32[7168]{0:T(1024)S(1)}, s32[7168]{0:T(1024)}, u32[]{:S(2)}) copy-start(s32[7168]{0:T(1024)} %param.6) | copy-start | bytes 86020
  14.0 2.3 %collective-permute-start = (bf16[8,1664]{1,0:T(8,128)(2,1)S(1)}, bf16[8,1664]{1,0:T(8,128)(2,1)S(1)}, u32[]{:S(2)}, u32[]{:S(2)}) collective-permute-start(bf16[8,1664]{1,0:T(8,128)(2,1)S(1)} %get-tuple-element.15), channel_id=1, source_target_pairs={{0,16},{16,0},{32,48},{48,32},{64,80},{80,64},{96,112},{112,96},{1... | collective-permute-start | bytes 79880 | tf_op jit(solution)/shard_map/ppermute | solution.py:346
  16.5 5.1 %collective-permute-start.1 = (bf16[8,1664]{1,0:T(8,128)(2,1)S(1)}, bf16[8,1664]{1,0:T(8,128)(2,1)S(1)}, u32[]{:S(2)}, u32[]{:S(2)}) collective-permute-start(bf16[8,1664]{1,0:T(8,128)(2,1)S(1)} %get-tuple-element.17), channel_id=1, source_target_pairs={{0,32},{16,48},{32,0},{48,16},{64,96},{80,112},{96,64},{112,80},{1... | collective-permute-start | bytes 79880 | tf_op jit(solution)/shard_map/ppermute | solution.py:290
  18.3 4.8 %collective-permute-start.2 = (bf16[8,1664]{1,0:T(8,128)(2,1)S(1)}, bf16[8,1664]{1,0:T(8,128)(2,1)S(1)}, u32[]{:S(2)}, u32[]{:S(2)}) collective-permute-start(bf16[8,1664]{1,0:T(8,128)(2,1)S(1)} %get-tuple-element.18), channel_id=1, source_target_pairs={{0,64},{16,80},{32,96},{48,112},{64,0},{80,16},{96,32},{112,48},{1... | collective-permute-start | bytes 79880 | tf_op jit(solution)/shard_map/ppermute | solution.py:290
  21.6 3.9 %collective-permute-start.3 = (bf16[8,1664]{1,0:T(8,128)(2,1)S(1)}, bf16[8,1664]{1,0:T(8,128)(2,1)S(1)}, u32[]{:S(2)}, u32[]{:S(2)}) collective-permute-start(bf16[8,1664]{1,0:T(8,128)(2,1)S(1)} %get-tuple-element.19), channel_id=1, source_target_pairs={{0,96},{16,112},{32,64},{48,80},{64,32},{80,48},{96,0},{112,16},{1... | collective-permute-start | bytes 79880 | tf_op jit(solution)/shard_map/ppermute | solution.py:290
  25.7 4.3 %collective-permute-start.6 = (bf16[16,1664]{1,0:T(8,128)(2,1)S(1)}, bf16[16,1664]{1,0:T(8,128)(2,1)S(1)}, u32[]{:S(2)}, u32[]{:S(2)}) collective-permute-start(bf16[16,1664]{1,0:T(8,128)(2,1)S(1)} %pack.1.refs_0_), channel_id=1, source_target_pairs={{0,12},{1,13},{2,14},{3,15},{4,8},{5,9},{6,10},{7,11},{8,4},{9,5},... | collective-permute-start | bytes 159752 | tf_op jit(solution)/shard_map/ppermute | solution.py:290
  28.2 4.6 %collective-permute-start.5 = (bf16[16,1664]{1,0:T(8,128)(2,1)S(1)}, bf16[16,1664]{1,0:T(8,128)(2,1)S(1)}, u32[]{:S(2)}, u32[]{:S(2)}) collective-permute-start(bf16[16,1664]{1,0:T(8,128)(2,1)S(1)} %pack.1.refs_0_), channel_id=1, source_target_pairs={{0,8},{1,9},{2,10},{3,11},{4,12},{5,13},{6,14},{7,15},{8,0},{9,1},... | collective-permute-start | bytes 159752 | tf_op jit(solution)/shard_map/ppermute | solution.py:290
  28.7 4.1 %collective-permute-start.4 = (bf16[16,1664]{1,0:T(8,128)(2,1)S(1)}, bf16[16,1664]{1,0:T(8,128)(2,1)S(1)}, u32[]{:S(2)}, u32[]{:S(2)}) collective-permute-start(bf16[16,1664]{1,0:T(8,128)(2,1)S(1)} %pack.1.refs_0_), channel_id=1, source_target_pairs={{0,4},{1,5},{2,6},{3,7},{4,0},{5,1},{6,2},{7,3},{8,12},{9,13},{10,... | collective-permute-start | bytes 159752 | tf_op jit(solution)/shard_map/ppermute | solution.py:290
  33.1 5.6 %collective-permute-start.9 = (bf16[32,1664]{1,0:T(8,128)(2,1)S(1)}, bf16[32,1664]{1,0:T(8,128)(2,1)S(1)}, u32[]{:S(2)}, u32[]{:S(2)}) collective-permute-start(bf16[32,1664]{1,0:T(8,128)(2,1)S(1)} %slots.1), channel_id=1, source_target_pairs={{0,3},{1,2},{2,1},{3,0},{4,7},{5,6},{6,5},{7,4},{8,11},{9,10},{10,... | collective-permute-start | bytes 319496 | tf_op jit(solution)/shard_map/ppermute | solution.py:290
  35.9 5.1 %collective-permute-start.8 = (bf16[32,1664]{1,0:T(8,128)(2,1)S(1)}, bf16[32,1664]{1,0:T(8,128)(2,1)S(1)}, u32[]{:S(2)}, u32[]{:S(2)}) collective-permute-start(bf16[32,1664]{1,0:T(8,128)(2,1)S(1)} %slots.1), channel_id=1, source_target_pairs={{0,2},{1,3},{2,0},{3,1},{4,6},{5,7},{6,4},{7,5},{8,10},{9,11},{10,... | collective-permute-start | bytes 319496 | tf_op jit(solution)/shard_map/ppermute | solution.py:290
  36.3 4.7 %collective-permute-start.7 = (bf16[32,1664]{1,0:T(8,128)(2,1)S(1)}, bf16[32,1664]{1,0:T(8,128)(2,1)S(1)}, u32[]{:S(2)}, u32[]{:S(2)}) collective-permute-start(bf16[32,1664]{1,0:T(8,128)(2,1)S(1)} %slots.1), channel_id=1, source_target_pairs={{0,1},{1,0},{2,3},{3,2},{4,5},{5,4},{6,7},{7,6},{8,9},{9,8},{10,11... | collective-permute-start | bytes 319496 | tf_op jit(solution)/shard_map/ppermute | solution.py:290
  41.0 6.0 %collective-permute-start.12 = (bf16[32,1664]{1,0:T(8,128)(2,1)S(1)}, bf16[32,1664]{1,0:T(8,128)(2,1)S(1)}, u32[]{:S(2)}, u32[]{:S(2)}) collective-permute-start(bf16[32,1664]{1,0:T(8,128)(2,1)S(1)} %add_add_fusion), channel_id=1, source_target_pairs={{0,96},{16,112},{32,64},{48,80},{64,32},{80,48},{96,0},{112,16},{1... | collective-permute-start | bytes 319496 | tf_op jit(solution)/shard_map/ppermute | solution.py:290
  41.4 5.7 %collective-permute-start.11 = (bf16[32,1664]{1,0:T(8,128)(2,1)S(1)}, bf16[32,1664]{1,0:T(8,128)(2,1)S(1)}, u32[]{:S(2)}, u32[]{:S(2)}) collective-permute-start(bf16[32,1664]{1,0:T(8,128)(2,1)S(1)} %add_add_fusion), channel_id=1, source_target_pairs={{0,64},{16,80},{32,96},{48,112},{64,0},{80,16},{96,32},{112,48},{1... | collective-permute-start | bytes 319496 | tf_op jit(solution)/shard_map/ppermute | solution.py:290
  41.5 6.1 %collective-permute-start.10 = (bf16[32,1664]{1,0:T(8,128)(2,1)S(1)}, bf16[32,1664]{1,0:T(8,128)(2,1)S(1)}, u32[]{:S(2)}, u32[]{:S(2)}) collective-permute-start(bf16[32,1664]{1,0:T(8,128)(2,1)S(1)} %add_add_fusion), channel_id=1, source_target_pairs={{0,32},{16,48},{32,0},{48,16},{64,96},{80,112},{96,64},{112,80},{1... | collective-permute-start | bytes 319496 | tf_op jit(solution)/shard_map/ppermute | solution.py:290
  47.6 16.9 %collective-permute-start.13 = (bf16[128,1664]{1,0:T(8,128)(2,1)S(1)}, bf16[128,1664]{1,0:T(8,128)(2,1)S(1)}, u32[]{:S(2)}, u32[]{:S(2)}) collective-permute-start(bf16[128,1664]{1,0:T(8,128)(2,1)S(1)} %pad_maximum_fusion.one_ref), channel_id=1, source_target_pairs={{0,16},{16,0},{32,48},{48,32},{64,80},{80,64},{96,112},{112,96},{1... | collective-permute-start | bytes 1277960 | tf_op jit(solution)/shard_map/ppermute | solution.py:367

commit v3 on v2

--- a/solution.py
+++ b/solution.py
@@ -16,6 +16,7 @@
 CLASSES = 8
 RING = 4
 SUB = 4
+GRANT = 58 << 20
 LOG2E = 1.4426950408889634
 TILES = 8
 BS = 32
@@ -121,8 +122,9 @@
     ).astype(BF16)
 
 
-def norms_kernel(solved_ref, emb_ref, fac_ref, aux_ref):
-    i = pl.program_id(0)
+def norms_kernel(first, solved_ref, emb_ref, fac_ref, *refs):
+    aux_ref = refs[-1]
+    i = pl.program_id(0) + first
     tile, dim = emb_ref.shape
     nchunk = tile // 128
     st = solved_ref[pl.ds(i * nchunk, nchunk), :].astype(F32)
@@ -286,87 +288,14 @@
         best_ref[...] = jnp.maximum(best_ref[...], jnp.max(lines))
 
 
-def ring(values, axis, pairs):
-    return [lax.ppermute(v, axis, p) for v, p in zip(values, pairs)]
-
-
-def body(embeddings, factor_cols, solved, pivots):
+def main_call(loc, one, two, aux, embeddings, factor_cols):
     rows_here, dim = embeddings.shape
     k0 = factor_cols.shape[1]
-    total = pivots.shape[0]
-    width = dim + k0 + 128
+    total = one.shape[0] + two.shape[0]
     tile = rows_here // TILES
-    r = lax.axis_index("rows").astype(jnp.int32)
-    c = lax.axis_index("cols").astype(jnp.int32)
-    pos = jnp.stack([r * 16 + c, r // 2, r % 2])
-    solved2 = solved.reshape(rows_here // 128, 128)
-    piv2 = pivots.reshape(total // 128, 128)
     smem = pl.BlockSpec(memory_space=pltpu.SMEM)
     vmem = pl.BlockSpec(memory_space=pltpu.VMEM)
-    hbm = pl.BlockSpec(memory_space=pltpu.HBM)
-    small = pltpu.CompilerParams(vmem_limit_bytes=8 << 20)
-    wide = lambda rows: jax.ShapeDtypeStruct((rows, width), BF16)
-    swap = [(i, i ^ 1) for i in range(8)]
-    zs = [[(i, i ^ (2 * k)) for i in range(8)] for k in range(1, RING)]
-    xs = [[(i, i ^ (4 * k)) for i in range(16)] for k in range(1, RING)]
-    ys = [[(i, i ^ k) for i in range(16)] for k in range(1, RING)]
-
-    keep, send, loc = pl.pallas_call(
-        own_kernel,
-        out_shape=(wide(8), wide(8), jax.ShapeDtypeStruct((2 + PMAX,), jnp.int32)),
-        in_specs=[smem, smem, vmem, smem, hbm, hbm],
-        out_specs=(vmem, vmem, smem),
-        scratch_shapes=[
-            pltpu.VMEM((16 * PMAX, dim), BF16),
-            pltpu.VMEM((16 * PMAX, k0), BF16),
-            pltpu.SemaphoreType.DMA((2, PMAX)),
-        ],
-        compiler_params=small,
-        name="own_rows",
-    )(pos, pivots, piv2, solved2, embeddings, factor_cols)
-    aux = pl.pallas_call(
-        norms_kernel,
-        grid=(TILES,),
-        out_shape=jax.ShapeDtypeStruct((rows_here, 128), F32),
-        in_specs=[
-            vmem,
-            pl.BlockSpec((tile, dim), lambda i: (i, 0)),
-            pl.BlockSpec((tile, k0), lambda i: (i, 0)),
-        ],
-        out_specs=pl.BlockSpec((tile, 128), lambda i: (i, 0)),
-        compiler_params=pltpu.CompilerParams(
-            dimension_semantics=("arbitrary",), vmem_limit_bytes=40 << 20
-        ),
-        cost_estimate=pl.CostEstimate(
-            flops=rows_here * (dim + k0) * 4, bytes_accessed=rows_here * (dim + k0) * 2,
-            transcendentals=0,
-        ),
-        name="row_norms",
-    )(solved2, embeddings, factor_cols)
-    recv = lax.ppermute(send, "rows", swap)
-    parts = pl.pallas_call(
-        split_kernel, out_shape=(wide(8),) * RING, compiler_params=small, name="by_class",
-    )(keep, recv)
-    got = [parts[0]] + ring(parts[1:], "rows", zs)
-    mine = pl.pallas_call(
-        pack_kernel, out_shape=wide(16), compiler_params=small, name="pack",
-    )(*got)
-    got = [mine] + ring([mine] * 3, "cols", xs)
-    mine = pl.pallas_call(
-        slots_kernel,
-        out_shape=wide(total // CLASSES),
-        in_specs=[smem] + [vmem] * RING,
-        out_specs=vmem,
-        compiler_params=small,
-        name="slots",
-    )(r.reshape(1), *got)
-    got = [mine] + ring([mine] * 3, "cols", ys)
-    mine = got[0] + got[1] + got[2] + got[3]
-    got = [mine] + ring([mine] * 3, "rows", zs)
-    one = jnp.concatenate(got, axis=0)
-    two = lax.ppermute(one, "rows", swap)
-
-    new_cols, gains, best = pl.pallas_call(
+    return pl.pallas_call(
         main_kernel,
         grid=(2 * TILES,),
         out_shape=(
@@ -395,10 +324,114 @@
             pltpu.VMEM((rows_here, 128), F32),
         ],
         compiler_params=pltpu.CompilerParams(
-            dimension_semantics=("arbitrary",), vmem_limit_bytes=48 << 20
+            dimension_semantics=("arbitrary",), vmem_limit_bytes=GRANT
         ),
         name="panel_factor",
     )(loc, one, two, aux, embeddings, factor_cols)
+
+
+def norms_part(solved2, embeddings, factor_cols, first, last, aux):
+    rows_here, dim = embeddings.shape
+    k0 = factor_cols.shape[1]
+    tile = rows_here // TILES
+    rows = (last - first) * tile
+    specs = [
+        pl.BlockSpec(memory_space=pltpu.VMEM),
+        pl.BlockSpec((tile, dim), lambda i: (i + first, 0)),
+        pl.BlockSpec((tile, k0), lambda i: (i + first, 0)),
+    ]
+    args = (solved2, embeddings, factor_cols)
+    if aux is not None:
+        specs.append(pl.BlockSpec(memory_space=pl.ANY))
+        args += (aux,)
+    return pl.pallas_call(
+        functools.partial(norms_kernel, first),
+        grid=(last - first,),
+        out_shape=jax.ShapeDtypeStruct((rows_here, 128), F32),
+        in_specs=specs,
+        out_specs=pl.BlockSpec((tile, 128), lambda i: (i + first, 0)),
+        input_output_aliases={} if aux is None else {3: 0},
+        compiler_params=pltpu.CompilerParams(
+            dimension_semantics=("arbitrary",), vmem_limit_bytes=GRANT
+        ),
+        cost_estimate=pl.CostEstimate(
+            flops=rows * (dim + k0) * 4, bytes_accessed=rows * (dim + k0) * 2, transcendentals=0
+        ),
+        name="row_norms",
+    )(*args)
+
+
+def ring(values, axis, pairs):
+    return [lax.ppermute(v, axis, p) for v, p in zip(values, pairs)]
+
+
+def body(embeddings, factor_cols, solved, pivots):
+    rows_here, dim = embeddings.shape
+    k0 = factor_cols.shape[1]
+    total = pivots.shape[0]
+    width = dim + k0 + 128
+    tile = rows_here // TILES
+    r = lax.axis_index("rows").astype(jnp.int32)
+    c = lax.axis_index("cols").astype(jnp.int32)
+    pos = jnp.stack([r * 16 + c, r // 2, r % 2])
+    solved2 = solved.reshape(rows_here // 128, 128)
+    piv2 = pivots.reshape(total // 128, 128)
+    smem = pl.BlockSpec(memory_space=pltpu.SMEM)
+    vmem = pl.BlockSpec(memory_space=pltpu.VMEM)
+    hbm = pl.BlockSpec(memory_space=pltpu.HBM)
+    small = pltpu.CompilerParams(vmem_limit_bytes=8 << 20)
+    wide = lambda rows: jax.ShapeDtypeStruct((rows, width), BF16)
+    swap = [(i, i ^ 1) for i in range(8)]
+    zs = [[(i, i ^ (2 * k)) for i in range(8)] for k in range(1, RING)]
+    xs = [[(i, i ^ (4 * k)) for i in range(16)] for k in range(1, RING)]
+    ys = [[(i, i ^ k) for i in range(16)] for k in range(1, RING)]
+
+    keep, send, loc = pl.pallas_call(
+        own_kernel,
+        out_shape=(wide(8), wide(8), jax.ShapeDtypeStruct((2 + PMAX,), jnp.int32)),
+        in_specs=[smem, smem, vmem, smem, hbm, hbm],
+        out_specs=(vmem, vmem, smem),
+        scratch_shapes=[
+            pltpu.VMEM((16 * PMAX, dim), BF16),
+            pltpu.VMEM((16 * PMAX, k0), BF16),
+            pltpu.SemaphoreType.DMA((2, PMAX)),
+        ],
+        compiler_params=pltpu.CompilerParams(vmem_limit_bytes=GRANT),
+        name="own_rows",
+    )(pos, pivots, piv2, solved2, embeddings, factor_cols)
+    recv = lax.ppermute(send, "rows", swap)
+    parts = pl.pallas_call(
+        split_kernel, out_shape=(wide(8),) * RING, compiler_params=small, name="by_class",
+    )(keep, recv)
+    got = [parts[0]] + ring(parts[1:], "rows", zs)
+    mine = pl.pallas_call(
+        pack_kernel, out_shape=wide(16), compiler_params=small, name="pack",
+    )(*got)
+    counts, mine = lax.optimization_barrier((solved2, mine))
+    got = [mine] + ring([mine] * 3, "cols", xs)
+    aux = norms_part(counts, embeddings, factor_cols, 0, 3, None)
+    aux, *got = lax.optimization_barrier((aux, *got))
+    mine = pl.pallas_call(
+        slots_kernel,
+        out_shape=wide(total // CLASSES),
+        in_specs=[smem] + [vmem] * RING,
+        out_specs=vmem,
+        compiler_params=small,
+        name="slots",
+    )(r.reshape(1), *got)
+    counts, mine = lax.optimization_barrier((solved2, mine))
+    got = [mine] + ring([mine] * 3, "cols", ys)
+    aux = norms_part(counts, embeddings, factor_cols, 3, 6, aux)
+    aux, *got = lax.optimization_barrier((aux, *got))
+    mine = got[0] + got[1] + got[2] + got[3]
+    counts, mine = lax.optimization_barrier((solved2, mine))
+    got = [mine] + ring([mine] * 3, "rows", zs)
+    aux = norms_part(counts, embeddings, factor_cols, 6, TILES, aux)
+    aux, *got = lax.optimization_barrier((aux, *got))
+    one = jnp.concatenate(got, axis=0)
+    two = lax.ppermute(one, "rows", swap)
+
+    new_cols, gains, best = main_call(loc, one, two, aux, embeddings, factor_cols)
     peers = lax.all_to_all(best.reshape(NDEV, 1, 128), AXES, 0, 0)
     return new_cols, gains.reshape(rows_here), jnp.max(peers)
 

time: 119 us -> 110 us (0.924)
  waiting for transfers between devices: 16.2 us -> 6.39 us
  local copies, waits for them, and re-layouts: 9.69 us -> 1.58 us
  Pallas kernels: 52.9 us -> 60.9 us
  blocking collectives: 14.9 us -> 17 us
  starting transfers between devices: 23 us -> 21.3 us
    ppermute x12, waiting for transfers between devices: 15.4 us -> 3.93 us  [ring(): return [lax.ppermute(v, axis, p) for v, p in zip(values, pairs)]]
    unnamed x12 -> x9, local copies, waits for them, and re-layouts: 9.69 us -> 1.56 us
    pallas_call x2 -> x4, Pallas kernels: 48.7 us -> 56 us  [the longest x1 38.9 us: main_call(): pl.pallas_call(main_kernel, grid=(2 * TILES,), out_shape=(jax.ShapeDtypeS...]
    all_to_all x1, blocking collectives: 14.9 us -> 17 us  [body(): peers = lax.all_to_all(best.reshape(NDEV, 1, 128), AXES, 0, 0)]
    ppermute x1, starting transfers between devices: 6.29 us -> 4.51 us  [body(): two = lax.ppermute(one, 'rows', swap)]
    ppermute x1, waiting for transfers between devices: 0.01 us -> 1.4 us  [body(): two = lax.ppermute(one, 'rows', swap)]
  transfers between devices with their start and end apart: 14 -> 14, of which waited for: 9 -> 4; matrix products, arithmetic and copies ran while one was open for 0% -> 0% of each run, Pallas kernels for 9% -> 16%
where the time goes in v3:
time: 110 us; the launch traced here: 109 us
  Pallas kernels  60.9 us (55%)
  starting transfers between devices  21.3 us (19%)
  blocking collectives  17 us (15%)
  waiting for transfers between devices  6.39 us (6%)
  local copies, waits for them, and re-layouts  1.58 us (1%)
  other arithmetic  1.32 us (1%)
    pallas_call x1, Pallas kernels, main_call(): pl.pallas_call(main_kernel, grid=(2 * TILES,), out_shape=(jax.ShapeDtypeS...  38.9 us
    pallas_call x3, Pallas kernels, norms_part(): pl.pallas_call(functools.partial(norms_kernel, first), grid=(last - first...  17.1 us
    all_to_all x1, blocking collectives, body(): peers = lax.all_to_all(best.reshape(NDEV, 1, 128), AXES, 0, 0)  17 us
    ppermute x12, starting transfers between devices, ring(): return [lax.ppermute(v, axis, p) for v, p in zip(values, pairs)]  15.3 us
    ppermute x1, starting transfers between devices, body(): two = lax.ppermute(one, 'rows', swap)  4.51 us
    pallas_call x1, Pallas kernels, body(): pl.pallas_call(own_kernel, out_shape=(wide(8), wide(8), jax.ShapeDtypeStr...  4.31 us
    ppermute x12, waiting for transfers between devices, ring(): return [lax.ppermute(v, axis, p) for v, p in zip(values, pairs)]  3.93 us
  transfers between devices with their start and end apart: 14, of which 4 were waited for; matrix products, arithmetic and copies ran while one was open for 0% of the time, Pallas kernels for 16%

profile of v3, /device:TPU:1, one launch (start us, length us, event | category | flops | bytes accessed | tf_op | source)
XLA Modules:
  0.0 109.2 jit_solution(2210606771826344557)
XLA Ops:
  0.7 0.6 pad_add_fusion.pos_ref
  1.2 4.3 %own_rows.1 = (bf16[8,1664]{1,0:T(8,128)(2,1)}, bf16[8,1664]{1,0:T(8,128)(2,1)}, s32[18]{0:T(128)}) custom-call(s32[3]{0:T(128)} %pad_add_fusion.pos_ref, s32[256]{0:T(256)} %piv_s.1, s32[2,128]{1,0:T(2,128)} %bitcast.15, s32[56,128]{1,0:T(8,128)} %bitcast.10, bf16[7168,1024]{1,0:T(8,128)(2,1)} %emb_ref.9, bf16[7168,512]{1,0:T(8,128)(2,1)} %fac_ref.9), custom_call_target="tpu_custom_call" | custom-call | tf_op jit(solution)/shard_map/own_rows/pallas_call | solution.py:389
  5.5 1.5 %collective-permute-start = (bf16[8,1664]{1,0:T(8,128)(2,1)}, bf16[8,1664]{1,0:T(8,128)(2,1)S(1)}, u32[]{:S(2)}, u32[]{:S(2)}) collective-permute-start(bf16[8,1664]{1,0:T(8,128)(2,1)} %get-tuple-element.36), channel_id=1, source_target_pairs={{0,16},{16,0},{32,48},{48,32},{64,80},{80,64},{96,112},{112,96},{1... | collective-permute-start | bytes 79880 | tf_op jit(solution)/shard_map/ppermute | solution.py:402
  7.0 1.1 collective-permute-done.recv_ref
  8.1 0.7 copy-done
  8.8 0.2 by_class.1
  9.0 1.8 %collective-permute-start.1 = (bf16[8,1664]{1,0:T(8,128)(2,1)S(1)}, bf16[8,1664]{1,0:T(8,128)(2,1)S(1)}, u32[]{:S(2)}, u32[]{:S(2)}) collective-permute-start(bf16[8,1664]{1,0:T(8,128)(2,1)S(1)} %get-tuple-element.38), channel_id=1, source_target_pairs={{0,32},{16,48},{32,0},{48,16},{64,96},{80,112},{96,64},{112,80},{1... | collective-permute-start | bytes 79880 | tf_op jit(solution)/shard_map/ppermute | solution.py:365
  10.8 3.4 %collective-permute-start.2 = (bf16[8,1664]{1,0:T(8,128)(2,1)S(1)}, bf16[8,1664]{1,0:T(8,128)(2,1)S(1)}, u32[]{:S(2)}, u32[]{:S(2)}) collective-permute-start(bf16[8,1664]{1,0:T(8,128)(2,1)S(1)} %get-tuple-element.39), channel_id=1, source_target_pairs={{0,64},{16,80},{32,96},{48,112},{64,0},{80,16},{96,32},{112,48},{1... | collective-permute-start | bytes 79880 | tf_op jit(solution)/shard_map/ppermute | solution.py:365
  14.1 0.0 collective-permute-done.1.refs_1_
  14.1 1.5 %collective-permute-done.2.refs_2_ = bf16[8,1664]{1,0:T(8,128)(2,1)S(1)} collective-permute-done((bf16[8,1664]{1,0:T(8,128)(2,1)S(1)}, bf16[8,1664]{1,0:T(8,128)(2,1)S(1)}, u32[]{:S(2)}, u32[]{:S(2)}) %collective-permute-start.2) | collective-permute-done | bytes 26656 | tf_op jit(solution)/shard_map/ppermute | solution.py:365
  15.7 2.4 %collective-permute-done.3.refs_3_ = bf16[8,1664]{1,0:T(8,128)(2,1)S(1)} collective-permute-done((bf16[8,1664]{1,0:T(8,128)(2,1)S(1)}, bf16[8,1664]{1,0:T(8,128)(2,1)S(1)}, u32[]{:S(2)}, u32[]{:S(2)}) %collective-permute-start.3) | collective-permute-done | bytes 26656 | tf_op jit(solution)/shard_map/ppermute | solution.py:365
  18.1 0.1 pack.1.refs_0_
  18.2 2.3 %collective-permute-start.6 = (bf16[16,1664]{1,0:T(8,128)(2,1)S(1)}, bf16[16,1664]{1,0:T(8,128)(2,1)S(1)}, u32[]{:S(2)}, u32[]{:S(2)}) collective-permute-start(bf16[16,1664]{1,0:T(8,128)(2,1)S(1)} %pack.1.refs_0_), channel_id=1, source_target_pairs={{0,12},{1,13},{2,14},{3,15},{4,8},{5,9},{6,10},{7,11},{8,4},{9,5},... | collective-permute-start | bytes 159752 | tf_op jit(solution)/shard_map/ppermute | solution.py:365
  20.5 0.8 collective-permute-start.5
  21.2 0.3 collective-permute-start.4
  21.5 6.7 %row_norms.3.refs_0_ = f32[7168,128]{1,0:T(8,128)} custom-call(s32[56,128]{1,0:T(8,128)} %bitcast.11, bf16[7168,1024]{1,0:T(8,128)(2,1)} %emb_ref.9, bf16[7168,512]{1,0:T(8,128)(2,1)} %fac_ref.9), custom_call_target="tpu_custom_call" | custom-call | flops 16515072 | bytes 8257536 | tf_op jit(solution)/shard_map/row_norms/pallas_call | solution.py:347
  28.2 0.0 collective-permute-done.5.refs_2_
  28.2 0.3 slots.1
  28.5 2.8 %collective-permute-start.9 = (bf16[32,1664]{1,0:T(8,128)(2,1)S(1)}, bf16[32,1664]{1,0:T(8,128)(2,1)S(1)}, u32[]{:S(2)}, u32[]{:S(2)}) collective-permute-start(bf16[32,1664]{1,0:T(8,128)(2,1)S(1)} %slots.1), channel_id=1, source_target_pairs={{0,3},{1,2},{2,1},{3,0},{4,7},{5,6},{6,5},{7,4},{8,11},{9,10},{10,... | collective-permute-start | bytes 319496 | tf_op jit(solution)/shard_map/ppermute | solution.py:365
  31.3 0.3 collective-permute-start.8
  31.6 0.3 collective-permute-start.7
  32.0 6.2 %row_norms.4.refs_0_ = f32[7168,128]{1,0:T(8,128)} custom-call(s32[56,128]{1,0:T(8,128)} %bitcast.12, bf16[7168,1024]{1,0:T(8,128)(2,1)} %emb_ref.9, bf16[7168,512]{1,0:T(8,128)(2,1)} %fac_ref.9, f32[7168,128]{1,0:T(8,128)} %row_norms.3.refs_0_), custom_call_target="tpu_custom_call", output_to_operand_aliasing={{}: (3, {})} | custom-call | flops 16515072 | bytes 8257536 | tf_op jit(solution)/shard_map/row_norms/pallas_call | solution.py:347
  38.3 0.4 collective-permute-start.12
  38.6 0.1 collective-permute-start.11
  38.7 2.9 %collective-permute-start.10 = (bf16[32,1664]{1,0:T(8,128)(2,1)S(1)}, bf16[32,1664]{1,0:T(8,128)(2,1)S(1)}, u32[]{:S(2)}, u32[]{:S(2)}) collective-permute-start(bf16[32,1664]{1,0:T(8,128)(2,1)S(1)} %add_add_fusion), channel_id=1, source_target_pairs={{0,32},{16,48},{32,0},{48,16},{64,96},{80,112},{96,64},{112,80},{1... | collective-permute-start | bytes 319496 | tf_op jit(solution)/shard_map/ppermute | solution.py:365
  41.6 4.2 %row_norms.5.aux_ref = f32[7168,128]{1,0:T(8,128)} custom-call(s32[56,128]{1,0:T(8,128)} %bitcast.13, bf16[7168,1024]{1,0:T(8,128)(2,1)} %emb_ref.9, bf16[7168,512]{1,0:T(8,128)(2,1)} %fac_ref.9, f32[7168,128]{1,0:T(8,128)} %row_norms.4.refs_0_), custom_call_target="tpu_custom_call", output_to_operand_aliasing={{}: (3, {})} | custom-call | flops 11010048 | bytes 5505024 | tf_op jit(solution)/shard_map/row_norms/pallas_call | solution.py:347
  45.9 4.5 %collective-permute-start.13 = (bf16[128,1664]{1,0:T(8,128)(2,1)S(1)}, bf16[128,1664]{1,0:T(8,128)(2,1)S(1)}, u32[]{:S(2)}, u32[]{:S(2)}) collective-permute-start(bf16[128,1664]{1,0:T(8,128)(2,1)S(1)} %constant_dynamic-update-slice_fusion.one_ref), channel_id=1, source_target_pairs={{0,16},{16,0},{32,48},{48,32},{64,80},{80,64},{96,112},{112,96},{1... | collective-permute-start | bytes 1277960 | tf_op jit(solution)/shard_map/ppermute | solution.py:432
  50.4 1.4 %collective-permute-done.13.two_ref = bf16[128,1664]{1,0:T(8,128)(2,1)S(1)} collective-permute-done((bf16[128,1664]{1,0:T(8,128)(2,1)S(1)}, bf16[128,1664]{1,0:T(8,128)(2,1)S(1)}, u32[]{:S(2)}, u32[]{:S(2)}) %collective-permute-start.13) | collective-permute-done | bytes 426016 | tf_op jit(solution)/shard_map/ppermute | solution.py:432
  51.8 0.8 copy-done.2
  52.6 38.9 %panel_factor.1 = (bf16[7168,256]{1,0:T(8,128)(2,1)}, f32[56,128]{1,0:T(8,128)}, f32[128,128]{1,0:T(8,128)}) custom-call(s32[18]{0:T(128)} %get-tuple-element.34.loc_ref, bf16[128,1664]{1,0:T(8,128)(2,1)} %copy-done.1, bf16[128,1664]{1,0:T(8,128)(2,1)} %copy-done.2, f32[7168,128]{1,0:T(8,128)} %row_norms.5.aux_ref, bf16[7168,1024]{1,0:T(8,128)(2,1)} %emb_ref.9, ...), custom_call_target="tpu_custom_call" | custom-call | tf_op jit(solution)/shard_map/panel_factor/pallas_call | solution.py:298
  91.5 17.0 %all_to_all.5 = f32[128,1,128]{2,1,0:T(1,128)S(1)} all-to-all(f32[128,1,128]{2,1,0:T(1,128)} %bitcast.14), channel_id=1, replica_groups=mesh['rows'=8,'cols'=16] {'rows','cols'}, dimensions={0} | all-to-all | bytes 131072 | tf_op jit(solution)/shard_map/all_to_all | solution.py:435
  108.5 0.7 reduce_max.9
  (18 shorter events, 0.1 us)
Async XLA Ops:
  5.5 2.6 %collective-permute-start = (bf16[8,1664]{1,0:T(8,128)(2,1)}, bf16[8,1664]{1,0:T(8,128)(2,1)S(1)}, u32[]{:S(2)}, u32[]{:S(2)}) collective-permute-start(bf16[8,1664]{1,0:T(8,128)(2,1)} %get-tuple-element.36), channel_id=1, source_target_pairs={{0,16},{16,0},{32,48},{48,32},{64,80},{80,64},{96,112},{112,96},{1... | collective-permute-start | bytes 79880 | tf_op jit(solution)/shard_map/ppermute | solution.py:402
  8.1 0.7 copy-start
  9.0 5.1 %collective-permute-start.1 = (bf16[8,1664]{1,0:T(8,128)(2,1)S(1)}, bf16[8,1664]{1,0:T(8,128)(2,1)S(1)}, u32[]{:S(2)}, u32[]{:S(2)}) collective-permute-start(bf16[8,1664]{1,0:T(8,128)(2,1)S(1)} %get-tuple-element.38), channel_id=1, source_target_pairs={{0,32},{16,48},{32,0},{48,16},{64,96},{80,112},{96,64},{112,80},{1... | collective-permute-start | bytes 79880 | tf_op jit(solution)/shard_map/ppermute | solution.py:365
  10.8 4.9 %collective-permute-start.2 = (bf16[8,1664]{1,0:T(8,128)(2,1)S(1)}, bf16[8,1664]{1,0:T(8,128)(2,1)S(1)}, u32[]{:S(2)}, u32[]{:S(2)}) collective-permute-start(bf16[8,1664]{1,0:T(8,128)(2,1)S(1)} %get-tuple-element.39), channel_id=1, source_target_pairs={{0,64},{16,80},{32,96},{48,112},{64,0},{80,16},{96,32},{112,48},{1... | collective-permute-start | bytes 79880 | tf_op jit(solution)/shard_map/ppermute | solution.py:365
  14.1 3.9 %collective-permute-start.3 = (bf16[8,1664]{1,0:T(8,128)(2,1)S(1)}, bf16[8,1664]{1,0:T(8,128)(2,1)S(1)}, u32[]{:S(2)}, u32[]{:S(2)}) collective-permute-start(bf16[8,1664]{1,0:T(8,128)(2,1)S(1)} %get-tuple-element.40), channel_id=1, source_target_pairs={{0,96},{16,112},{32,64},{48,80},{64,32},{80,48},{96,0},{112,16},{1... | collective-permute-start | bytes 79880 | tf_op jit(solution)/shard_map/ppermute | solution.py:365
  18.2 10.0 %collective-permute-start.6 = (bf16[16,1664]{1,0:T(8,128)(2,1)S(1)}, bf16[16,1664]{1,0:T(8,128)(2,1)S(1)}, u32[]{:S(2)}, u32[]{:S(2)}) collective-permute-start(bf16[16,1664]{1,0:T(8,128)(2,1)S(1)} %pack.1.refs_0_), channel_id=1, source_target_pairs={{0,12},{1,13},{2,14},{3,15},{4,8},{5,9},{6,10},{7,11},{8,4},{9,5},... | collective-permute-start | bytes 159752 | tf_op jit(solution)/shard_map/ppermute | solution.py:365
  20.5 7.7 %collective-permute-start.5 = (bf16[16,1664]{1,0:T(8,128)(2,1)S(1)}, bf16[16,1664]{1,0:T(8,128)(2,1)S(1)}, u32[]{:S(2)}, u32[]{:S(2)}) collective-permute-start(bf16[16,1664]{1,0:T(8,128)(2,1)S(1)} %pack.1.refs_0_), channel_id=1, source_target_pairs={{0,8},{1,9},{2,10},{3,11},{4,12},{5,13},{6,14},{7,15},{8,0},{9,1},... | collective-permute-start | bytes 159752 | tf_op jit(solution)/shard_map/ppermute | solution.py:365
  21.2 7.0 %collective-permute-start.4 = (bf16[16,1664]{1,0:T(8,128)(2,1)S(1)}, bf16[16,1664]{1,0:T(8,128)(2,1)S(1)}, u32[]{:S(2)}, u32[]{:S(2)}) collective-permute-start(bf16[16,1664]{1,0:T(8,128)(2,1)S(1)} %pack.1.refs_0_), channel_id=1, source_target_pairs={{0,4},{1,5},{2,6},{3,7},{4,0},{5,1},{6,2},{7,3},{8,12},{9,13},{10,... | collective-permute-start | bytes 159752 | tf_op jit(solution)/shard_map/ppermute | solution.py:365
  28.5 9.7 %collective-permute-start.9 = (bf16[32,1664]{1,0:T(8,128)(2,1)S(1)}, bf16[32,1664]{1,0:T(8,128)(2,1)S(1)}, u32[]{:S(2)}, u32[]{:S(2)}) collective-permute-start(bf16[32,1664]{1,0:T(8,128)(2,1)S(1)} %slots.1), channel_id=1, source_target_pairs={{0,3},{1,2},{2,1},{3,0},{4,7},{5,6},{6,5},{7,4},{8,11},{9,10},{10,... | collective-permute-start | bytes 319496 | tf_op jit(solution)/shard_map/ppermute | solution.py:365
  31.3 6.9 %collective-permute-start.8 = (bf16[32,1664]{1,0:T(8,128)(2,1)S(1)}, bf16[32,1664]{1,0:T(8,128)(2,1)S(1)}, u32[]{:S(2)}, u32[]{:S(2)}) collective-permute-start(bf16[32,1664]{1,0:T(8,128)(2,1)S(1)} %slots.1), channel_id=1, source_target_pairs={{0,2},{1,3},{2,0},{3,1},{4,6},{5,7},{6,4},{7,5},{8,10},{9,11},{10,... | collective-permute-start | bytes 319496 | tf_op jit(solution)/shard_map/ppermute | solution.py:365
  31.6 6.6 %collective-permute-start.7 = (bf16[32,1664]{1,0:T(8,128)(2,1)S(1)}, bf16[32,1664]{1,0:T(8,128)(2,1)S(1)}, u32[]{:S(2)}, u32[]{:S(2)}) collective-permute-start(bf16[32,1664]{1,0:T(8,128)(2,1)S(1)} %slots.1), channel_id=1, source_target_pairs={{0,1},{1,0},{2,3},{3,2},{4,5},{5,4},{6,7},{7,6},{8,9},{9,8},{10,11... | collective-permute-start | bytes 319496 | tf_op jit(solution)/shard_map/ppermute | solution.py:365
  38.3 7.5 %collective-permute-start.12 = (bf16[32,1664]{1,0:T(8,128)(2,1)S(1)}, bf16[32,1664]{1,0:T(8,128)(2,1)S(1)}, u32[]{:S(2)}, u32[]{:S(2)}) collective-permute-start(bf16[32,1664]{1,0:T(8,128)(2,1)S(1)} %add_add_fusion), channel_id=1, source_target_pairs={{0,96},{16,112},{32,64},{48,80},{64,32},{80,48},{96,0},{112,16},{1... | collective-permute-start | bytes 319496 | tf_op jit(solution)/shard_map/ppermute | solution.py:365
  38.6 7.1 %collective-permute-start.11 = (bf16[32,1664]{1,0:T(8,128)(2,1)S(1)}, bf16[32,1664]{1,0:T(8,128)(2,1)S(1)}, u32[]{:S(2)}, u32[]{:S(2)}) collective-permute-start(bf16[32,1664]{1,0:T(8,128)(2,1)S(1)} %add_add_fusion), channel_id=1, source_target_pairs={{0,64},{16,80},{32,96},{48,112},{64,0},{80,16},{96,32},{112,48},{1... | collective-permute-start | bytes 319496 | tf_op jit(solution)/shard_map/ppermute | solution.py:365
  38.7 7.0 %collective-permute-start.10 = (bf16[32,1664]{1,0:T(8,128)(2,1)S(1)}, bf16[32,1664]{1,0:T(8,128)(2,1)S(1)}, u32[]{:S(2)}, u32[]{:S(2)}) collective-permute-start(bf16[32,1664]{1,0:T(8,128)(2,1)S(1)} %add_add_fusion), channel_id=1, source_target_pairs={{0,32},{16,48},{32,0},{48,16},{64,96},{80,112},{96,64},{112,80},{1... | collective-permute-start | bytes 319496 | tf_op jit(solution)/shard_map/ppermute | solution.py:365
  45.9 5.9 %copy-start.1 = (bf16[128,1664]{1,0:T(8,128)(2,1)}, bf16[128,1664]{1,0:T(8,128)(2,1)S(1)}, u32[]{:S(2)}) copy-start(bf16[128,1664]{1,0:T(8,128)(2,1)S(1)} %constant_dynamic-update-slice_fusion.one_ref) | copy-start | bytes 1277956
  45.9 5.9 %collective-permute-start.13 = (bf16[128,1664]{1,0:T(8,128)(2,1)S(1)}, bf16[128,1664]{1,0:T(8,128)(2,1)S(1)}, u32[]{:S(2)}, u32[]{:S(2)}) collective-permute-start(bf16[128,1664]{1,0:T(8,128)(2,1)S(1)} %constant_dynamic-update-slice_fusion.one_ref), channel_id=1, source_target_pairs={{0,16},{16,0},{32,48},{48,32},{64,80},{80,64},{96,112},{112,96},{1... | collective-permute-start | bytes 1277960 | tf_op jit(solution)/shard_map/ppermute | solution.py:432
  51.8 0.8 copy-start.2

commit v4 on v3

--- a/solution.py
+++ b/solution.py
@@ -130,12 +130,16 @@
     st = solved_ref[pl.ds(i * nchunk, nchunk), :].astype(F32)
     ey = iota((128, 128), 0) == iota((128, 128), 1)
     lane = iota((128, 128), 1)
+    ndims = (((1,), (1,)), ((), ()))
     for c in range(nchunk):
         o = slice(128 * c, 128 * c + 128)
-        x = emb_ref[o, :].astype(F32)
-        f = fac_ref[o, :].astype(F32)
-        a = 1.0 / jnp.sqrt(jnp.sum(x * x, axis=1, keepdims=True) / dim + EPS)
-        fs = jnp.sum(f * f, axis=1, keepdims=True)
+        x = emb_ref[o, :]
+        f = fac_ref[o, :]
+        xx = lax.dot_general(x, x, ndims, preferred_element_type=F32)
+        ff = lax.dot_general(f, f, ndims, preferred_element_type=F32)
+        ss = jnp.sum(jnp.where(ey, xx, 0.0), axis=1, keepdims=True)
+        fs = jnp.sum(jnp.where(ey, ff, 0.0), axis=1, keepdims=True)
+        a = 1.0 / jnp.sqrt(ss / dim + EPS)
         b = jnp.broadcast_to(st[c : c + 1, :], (128, 128))
         q = learn(jnp.sum(jnp.where(ey, b, 0.0), axis=1, keepdims=True))
         aux_ref[o, :] = jnp.where(lane == 0, a, jnp.where(lane == 1, q, q * q + RIDGE - fs))
@@ -146,6 +150,67 @@
     m = r.astype(BF16)
     l = (r - m.astype(F32)).astype(BF16)
     return h, m, l
+
+
+def lanes(x, k):
+    return jnp.broadcast_to(x[:, k : k + 1], x.shape)
+
+
+def sublanes(x, k):
+    return jnp.broadcast_to(x[k : k + 1, :], x.shape)
+
+
+def eliminate(w):
+    rows, width = w.shape
+    groups = [
+        [w[8 * g : 8 * g + 8, 128 * v : 128 * v + 128] for v in range(width // 128)]
+        for g in range(rows // 8)
+    ]
+    srow = iota((8, 128), 0)
+    done = []
+    for t in range(rows // 8):
+        cols = [lanes(groups[t][0], 8 * t + k) for k in range(8)]
+        e = [[sublanes(cols[k], i) for k in range(i + 1)] for i in range(8)]
+        below = {
+            g: [lanes(groups[g][0], 8 * t + k) for k in range(8)]
+            for g in range(t + 1, rows // 8)
+        }
+        tops = [[sublanes(x, j) for x in groups[t]] for j in range(8)]
+        m = [[None] * 8 for _ in range(8)]
+        n = [[None] * 8 for _ in range(8)]
+        for k in range(8):
+            inv = 1.0 / e[k][k]
+            for i in range(k + 1, 8):
+                m[i][k] = e[i][k] * inv
+                for j in range(k + 1, i + 1):
+                    e[i][j] = e[i][j] - m[i][k] * e[j][k]
+            for j in range(k):
+                acc = m[k][j]
+                for l in range(j + 1, k):
+                    acc = acc + m[k][l] * n[l][j]
+                n[k][j] = -acc
+        root = [1.0 / jnp.sqrt(e[k][k]) for k in range(8)]
+        inv = [[root[i] * n[i][j] for j in range(i)] + [root[i]] for i in range(8)]
+        cols = []
+        for j in range(8):
+            c = jnp.where(srow == j, inv[j][j], 0.0)
+            for i in range(j + 1, 8):
+                c = jnp.where(srow == i, inv[i][j], c)
+            cols.append(c)
+        out = []
+        for v in range(width // 128):
+            acc = cols[0] * tops[0][v]
+            for j in range(1, 8):
+                acc = acc + cols[j] * tops[j][v]
+            out.append(acc)
+        for g in range(t + 1, rows // 8):
+            for j in range(8):
+                c = below[g][0] * inv[j][0]
+                for k in range(1, j + 1):
+                    c = c + below[g][k] * inv[j][k]
+                groups[g] = [x - c * sublanes(o, j) for x, o in zip(groups[g], out)]
+        done.append(jnp.concatenate(out, axis=1))
+    return jnp.concatenate(done, axis=0)
 
 
 def main_kernel(
@@ -212,26 +277,7 @@
         rows = pl.ds(pl.multiple_of(i * BS, BS), BS)
         shift = lax.rem(n - i * BS, n)
         a = pltpu.roll(ar[rows, 0:n], shift, 1)
-        w = jnp.concatenate([a, ar[rows, n : 2 * n]], axis=1)
-        groups = [w[8 * g : 8 * g + 8, :] for g in range(BS // 8)]
-        srows = iota((8, 1), 0)
-        for k in range(BS):
-            g0 = k // 8
-            row = groups[g0][k % 8 : k % 8 + 1, :]
-            srow = row * (1.0 / row[:, k : k + 1])
-            for g in range(g0, BS // 8):
-                col = groups[g][:, k : k + 1]
-                if g == g0:
-                    if k % 8 == 7:
-                        continue
-                    col = jnp.where(srows > k % 8, col, 0.0)
-                groups[g] = groups[g] - col * srow
-        w = jnp.concatenate(groups, axis=0)
-        d = jnp.sum(
-            jnp.where(iota((BS, 128), 0) == iota((BS, 128), 1), w[:, 0:128], 0.0),
-            axis=1, keepdims=True,
-        )
-        w = w * (1.0 / jnp.sqrt(d))
+        w = eliminate(jnp.concatenate([a, ar[rows, n : 2 * n]], axis=1))
         u = pltpu.roll(w[:, 0:n], i * BS, 1)
         m = w[:, n : 2 * n]
         minv[rows, :] = m

time: 110 us -> 96.9 us (0.88)
  Pallas kernels: 60.9 us -> 48.1 us
    pallas_call x1, Pallas kernels: 38.9 us -> 25.7 us  [main_call(): pl.pallas_call(main_kernel, grid=(2 * TILES,), out_shape=(jax.ShapeDtypeS...]
  transfers between devices with their start and end apart: 14 -> 14, of which waited for: 4 -> 4; matrix products, arithmetic and copies ran while one was open for 0% -> 0% of each run, Pallas kernels for 16% -> 18%
where the time goes in v4:
time: 96.9 us; the launch traced here: 96.3 us
  Pallas kernels  48.1 us (50%)
  starting transfers between devices  21.5 us (22%)
  blocking collectives  16.7 us (17%)
  waiting for transfers between devices  6.39 us (7%)
  local copies, waits for them, and re-layouts  1.58 us (2%)
  other arithmetic  1.32 us (1%)
    pallas_call x1, Pallas kernels, main_call(): pl.pallas_call(main_kernel, grid=(2 * TILES,), out_shape=(jax.ShapeDtypeS...  25.7 us
    pallas_call x3, Pallas kernels, norms_part(): pl.pallas_call(functools.partial(norms_kernel, first), grid=(last - first...  17.7 us
    all_to_all x1, blocking collectives, body(): peers = lax.all_to_all(best.reshape(NDEV, 1, 128), AXES, 0, 0)  16.7 us
    ppermute x12, starting transfers between devices, ring(): return [lax.ppermute(v, axis, p) for v, p in zip(values, pairs)]  15.2 us
    ppermute x1, starting transfers between devices, body(): two = lax.ppermute(one, 'rows', swap)  4.62 us
    pallas_call x1, Pallas kernels, body(): pl.pallas_call(own_kernel, out_shape=(wide(8), wide(8), jax.ShapeDtypeStr...  4.16 us
    ppermute x12, waiting for transfers between devices, ring(): return [lax.ppermute(v, axis, p) for v, p in zip(values, pairs)]  3.93 us
  transfers between devices with their start and end apart: 14, of which 4 were waited for; matrix products, arithmetic and copies ran while one was open for 0% of the time, Pallas kernels for 18%

profile of v4, /device:TPU:1, one launch (start us, length us, event | category | flops | bytes accessed | tf_op | source)
XLA Modules:
  0.0 96.3 jit_solution(11166482844111594430)
XLA Ops:
  0.7 0.6 pad_add_fusion.pos_ref
  1.2 4.2 %own_rows.1 = (bf16[8,1664]{1,0:T(8,128)(2,1)}, bf16[8,1664]{1,0:T(8,128)(2,1)}, s32[18]{0:T(128)}) custom-call(s32[3]{0:T(128)} %pad_add_fusion.pos_ref, s32[256]{0:T(256)} %piv_s.1, s32[2,128]{1,0:T(2,128)} %bitcast.15, s32[56,128]{1,0:T(8,128)} %bitcast.10, bf16[7168,1024]{1,0:T(8,128)(2,1)} %emb_ref.9, bf16[7168,512]{1,0:T(8,128)(2,1)} %fac_ref.9), custom_call_target="tpu_custom_call" | custom-call | tf_op jit(solution)/shard_map/own_rows/pallas_call | solution.py:435
  5.4 1.7 %collective-permute-start = (bf16[8,1664]{1,0:T(8,128)(2,1)}, bf16[8,1664]{1,0:T(8,128)(2,1)S(1)}, u32[]{:S(2)}, u32[]{:S(2)}) collective-permute-start(bf16[8,1664]{1,0:T(8,128)(2,1)} %get-tuple-element.36), channel_id=1, source_target_pairs={{0,16},{16,0},{32,48},{48,32},{64,80},{80,64},{96,112},{112,96},{1... | collective-permute-start | bytes 79880 | tf_op jit(solution)/shard_map/ppermute | solution.py:448
  7.0 1.1 %collective-permute-done.recv_ref = bf16[8,1664]{1,0:T(8,128)(2,1)S(1)} collective-permute-done((bf16[8,1664]{1,0:T(8,128)(2,1)}, bf16[8,1664]{1,0:T(8,128)(2,1)S(1)}, u32[]{:S(2)}, u32[]{:S(2)}) %collective-permute-start) | collective-permute-done | bytes 26656 | tf_op jit(solution)/shard_map/ppermute | solution.py:448
  8.1 0.7 copy-done
  8.8 0.2 by_class.1
  9.0 1.8 %collective-permute-start.1 = (bf16[8,1664]{1,0:T(8,128)(2,1)S(1)}, bf16[8,1664]{1,0:T(8,128)(2,1)S(1)}, u32[]{:S(2)}, u32[]{:S(2)}) collective-permute-start(bf16[8,1664]{1,0:T(8,128)(2,1)S(1)} %get-tuple-element.38), channel_id=1, source_target_pairs={{0,32},{16,48},{32,0},{48,16},{64,96},{80,112},{96,64},{112,80},{1... | collective-permute-start | bytes 79880 | tf_op jit(solution)/shard_map/ppermute | solution.py:411
  10.8 3.4 %collective-permute-start.2 = (bf16[8,1664]{1,0:T(8,128)(2,1)S(1)}, bf16[8,1664]{1,0:T(8,128)(2,1)S(1)}, u32[]{:S(2)}, u32[]{:S(2)}) collective-permute-start(bf16[8,1664]{1,0:T(8,128)(2,1)S(1)} %get-tuple-element.39), channel_id=1, source_target_pairs={{0,64},{16,80},{32,96},{48,112},{64,0},{80,16},{96,32},{112,48},{1... | collective-permute-start | bytes 79880 | tf_op jit(solution)/shard_map/ppermute | solution.py:411
  14.2 1.5 %collective-permute-done.2.refs_2_ = bf16[8,1664]{1,0:T(8,128)(2,1)S(1)} collective-permute-done((bf16[8,1664]{1,0:T(8,128)(2,1)S(1)}, bf16[8,1664]{1,0:T(8,128)(2,1)S(1)}, u32[]{:S(2)}, u32[]{:S(2)}) %collective-permute-start.2) | collective-permute-done | bytes 26656 | tf_op jit(solution)/shard_map/ppermute | solution.py:411
  15.7 2.4 %collective-permute-done.3.refs_3_ = bf16[8,1664]{1,0:T(8,128)(2,1)S(1)} collective-permute-done((bf16[8,1664]{1,0:T(8,128)(2,1)S(1)}, bf16[8,1664]{1,0:T(8,128)(2,1)S(1)}, u32[]{:S(2)}, u32[]{:S(2)}) %collective-permute-start.3) | collective-permute-done | bytes 26656 | tf_op jit(solution)/shard_map/ppermute | solution.py:411
  18.1 0.1 pack.1.refs_0_
  18.2 2.4 %collective-permute-start.6 = (bf16[16,1664]{1,0:T(8,128)(2,1)S(1)}, bf16[16,1664]{1,0:T(8,128)(2,1)S(1)}, u32[]{:S(2)}, u32[]{:S(2)}) collective-permute-start(bf16[16,1664]{1,0:T(8,128)(2,1)S(1)} %pack.1.refs_0_), channel_id=1, source_target_pairs={{0,12},{1,13},{2,14},{3,15},{4,8},{5,9},{6,10},{7,11},{8,4},{9,5},... | collective-permute-start | bytes 159752 | tf_op jit(solution)/shard_map/ppermute | solution.py:411
  20.7 0.6 collective-permute-start.5
  21.3 0.3 collective-permute-start.4
  21.6 6.8 %row_norms.3.refs_0_ = f32[7168,128]{1,0:T(8,128)} custom-call(s32[56,128]{1,0:T(8,128)} %bitcast.11, bf16[7168,1024]{1,0:T(8,128)(2,1)} %emb_ref.9, bf16[7168,512]{1,0:T(8,128)(2,1)} %fac_ref.9), custom_call_target="tpu_custom_call" | custom-call | flops 16515072 | bytes 8257536 | tf_op jit(solution)/shard_map/row_norms/pallas_call | solution.py:393
  28.4 0.0 collective-permute-done.6.refs_3_
  28.4 0.0 collective-permute-done.5.refs_2_
  28.4 0.3 slots.1
  28.7 2.7 %collective-permute-start.9 = (bf16[32,1664]{1,0:T(8,128)(2,1)S(1)}, bf16[32,1664]{1,0:T(8,128)(2,1)S(1)}, u32[]{:S(2)}, u32[]{:S(2)}) collective-permute-start(bf16[32,1664]{1,0:T(8,128)(2,1)S(1)} %slots.1), channel_id=1, source_target_pairs={{0,3},{1,2},{2,1},{3,0},{4,7},{5,6},{6,5},{7,4},{8,11},{9,10},{10,... | collective-permute-start | bytes 319496 | tf_op jit(solution)/shard_map/ppermute | solution.py:411
  31.4 0.4 collective-permute-start.8
  31.8 0.3 collective-permute-start.7
  32.1 6.4 %row_norms.4.refs_0_ = f32[7168,128]{1,0:T(8,128)} custom-call(s32[56,128]{1,0:T(8,128)} %bitcast.12, bf16[7168,1024]{1,0:T(8,128)(2,1)} %emb_ref.9, bf16[7168,512]{1,0:T(8,128)(2,1)} %fac_ref.9, f32[7168,128]{1,0:T(8,128)} %row_norms.3.refs_0_), custom_call_target="tpu_custom_call", output_to_operand_aliasing={{}: (3, {})} | custom-call | flops 16515072 | bytes 8257536 | tf_op jit(solution)/shard_map/row_norms/pallas_call | solution.py:393
  38.5 0.4 collective-permute-start.12
  38.9 0.1 collective-permute-start.11
  39.0 2.9 %collective-permute-start.10 = (bf16[32,1664]{1,0:T(8,128)(2,1)S(1)}, bf16[32,1664]{1,0:T(8,128)(2,1)S(1)}, u32[]{:S(2)}, u32[]{:S(2)}) collective-permute-start(bf16[32,1664]{1,0:T(8,128)(2,1)S(1)} %add_add_fusion), channel_id=1, source_target_pairs={{0,32},{16,48},{32,0},{48,16},{64,96},{80,112},{96,64},{112,80},{1... | collective-permute-start | bytes 319496 | tf_op jit(solution)/shard_map/ppermute | solution.py:411
  41.8 4.5 %row_norms.5.aux_ref = f32[7168,128]{1,0:T(8,128)} custom-call(s32[56,128]{1,0:T(8,128)} %bitcast.13, bf16[7168,1024]{1,0:T(8,128)(2,1)} %emb_ref.9, bf16[7168,512]{1,0:T(8,128)(2,1)} %fac_ref.9, f32[7168,128]{1,0:T(8,128)} %row_norms.4.refs_0_), custom_call_target="tpu_custom_call", output_to_operand_aliasing={{}: (3, {})} | custom-call | flops 11010048 | bytes 5505024 | tf_op jit(solution)/shard_map/row_norms/pallas_call | solution.py:393
  46.4 4.6 %collective-permute-start.13 = (bf16[128,1664]{1,0:T(8,128)(2,1)S(1)}, bf16[128,1664]{1,0:T(8,128)(2,1)S(1)}, u32[]{:S(2)}, u32[]{:S(2)}) collective-permute-start(bf16[128,1664]{1,0:T(8,128)(2,1)S(1)} %constant_dynamic-update-slice_fusion.one_ref), channel_id=1, source_target_pairs={{0,16},{16,0},{32,48},{48,32},{64,80},{80,64},{96,112},{112,96},{1... | collective-permute-start | bytes 1277960 | tf_op jit(solution)/shard_map/ppermute | solution.py:478
  51.1 1.4 %collective-permute-done.13.two_ref = bf16[128,1664]{1,0:T(8,128)(2,1)S(1)} collective-permute-done((bf16[128,1664]{1,0:T(8,128)(2,1)S(1)}, bf16[128,1664]{1,0:T(8,128)(2,1)S(1)}, u32[]{:S(2)}, u32[]{:S(2)}) %collective-permute-start.13) | collective-permute-done | bytes 426016 | tf_op jit(solution)/shard_map/ppermute | solution.py:478
  52.5 0.8 copy-done.2
  53.2 25.7 %panel_factor.1 = (bf16[7168,256]{1,0:T(8,128)(2,1)}, f32[56,128]{1,0:T(8,128)}, f32[128,128]{1,0:T(8,128)}) custom-call(s32[18]{0:T(128)} %get-tuple-element.34.loc_ref, bf16[128,1664]{1,0:T(8,128)(2,1)} %copy-done.1, bf16[128,1664]{1,0:T(8,128)(2,1)} %copy-done.2, f32[7168,128]{1,0:T(8,128)} %row_norms.5.aux_ref, bf16[7168,1024]{1,0:T(8,128)(2,1)} %emb_ref.9, ...), custom_call_target="tpu_custom_call" | custom-call | tf_op jit(solution)/shard_map/panel_factor/pallas_call | solution.py:344
  78.9 16.7 %all_to_all.5 = f32[128,1,128]{2,1,0:T(1,128)S(1)} all-to-all(f32[128,1,128]{2,1,0:T(1,128)} %bitcast.14), channel_id=1, replica_groups=mesh['rows'=8,'cols'=16] {'rows','cols'}, dimensions={0} | all-to-all | bytes 131072 | tf_op jit(solution)/shard_map/all_to_all | solution.py:481
  95.6 0.7 reduce_max.9
  (18 shorter events, 0.1 us)
Async XLA Ops:
  5.4 2.7 %collective-permute-start = (bf16[8,1664]{1,0:T(8,128)(2,1)}, bf16[8,1664]{1,0:T(8,128)(2,1)S(1)}, u32[]{:S(2)}, u32[]{:S(2)}) collective-permute-start(bf16[8,1664]{1,0:T(8,128)(2,1)} %get-tuple-element.36), channel_id=1, source_target_pairs={{0,16},{16,0},{32,48},{48,32},{64,80},{80,64},{96,112},{112,96},{1... | collective-permute-start | bytes 79880 | tf_op jit(solution)/shard_map/ppermute | solution.py:448
  8.1 0.7 copy-start
  9.0 5.1 %collective-permute-start.1 = (bf16[8,1664]{1,0:T(8,128)(2,1)S(1)}, bf16[8,1664]{1,0:T(8,128)(2,1)S(1)}, u32[]{:S(2)}, u32[]{:S(2)}) collective-permute-start(bf16[8,1664]{1,0:T(8,128)(2,1)S(1)} %get-tuple-element.38), channel_id=1, source_target_pairs={{0,32},{16,48},{32,0},{48,16},{64,96},{80,112},{96,64},{112,80},{1... | collective-permute-start | bytes 79880 | tf_op jit(solution)/shard_map/ppermute | solution.py:411
  10.8 4.9 %collective-permute-start.2 = (bf16[8,1664]{1,0:T(8,128)(2,1)S(1)}, bf16[8,1664]{1,0:T(8,128)(2,1)S(1)}, u32[]{:S(2)}, u32[]{:S(2)}) collective-permute-start(bf16[8,1664]{1,0:T(8,128)(2,1)S(1)} %get-tuple-element.39), channel_id=1, source_target_pairs={{0,64},{16,80},{32,96},{48,112},{64,0},{80,16},{96,32},{112,48},{1... | collective-permute-start | bytes 79880 | tf_op jit(solution)/shard_map/ppermute | solution.py:411
  14.2 3.9 %collective-permute-start.3 = (bf16[8,1664]{1,0:T(8,128)(2,1)S(1)}, bf16[8,1664]{1,0:T(8,128)(2,1)S(1)}, u32[]{:S(2)}, u32[]{:S(2)}) collective-permute-start(bf16[8,1664]{1,0:T(8,128)(2,1)S(1)} %get-tuple-element.40), channel_id=1, source_target_pairs={{0,96},{16,112},{32,64},{48,80},{64,32},{80,48},{96,0},{112,16},{1... | collective-permute-start | bytes 79880 | tf_op jit(solution)/shard_map/ppermute | solution.py:411
  18.2 10.2 %collective-permute-start.6 = (bf16[16,1664]{1,0:T(8,128)(2,1)S(1)}, bf16[16,1664]{1,0:T(8,128)(2,1)S(1)}, u32[]{:S(2)}, u32[]{:S(2)}) collective-permute-start(bf16[16,1664]{1,0:T(8,128)(2,1)S(1)} %pack.1.refs_0_), channel_id=1, source_target_pairs={{0,12},{1,13},{2,14},{3,15},{4,8},{5,9},{6,10},{7,11},{8,4},{9,5},... | collective-permute-start | bytes 159752 | tf_op jit(solution)/shard_map/ppermute | solution.py:411
  20.7 7.7 %collective-permute-start.5 = (bf16[16,1664]{1,0:T(8,128)(2,1)S(1)}, bf16[16,1664]{1,0:T(8,128)(2,1)S(1)}, u32[]{:S(2)}, u32[]{:S(2)}) collective-permute-start(bf16[16,1664]{1,0:T(8,128)(2,1)S(1)} %pack.1.refs_0_), channel_id=1, source_target_pairs={{0,8},{1,9},{2,10},{3,11},{4,12},{5,13},{6,14},{7,15},{8,0},{9,1},... | collective-permute-start | bytes 159752 | tf_op jit(solution)/shard_map/ppermute | solution.py:411
  21.3 7.1 %collective-permute-start.4 = (bf16[16,1664]{1,0:T(8,128)(2,1)S(1)}, bf16[16,1664]{1,0:T(8,128)(2,1)S(1)}, u32[]{:S(2)}, u32[]{:S(2)}) collective-permute-start(bf16[16,1664]{1,0:T(8,128)(2,1)S(1)} %pack.1.refs_0_), channel_id=1, source_target_pairs={{0,4},{1,5},{2,6},{3,7},{4,0},{5,1},{6,2},{7,3},{8,12},{9,13},{10,... | collective-permute-start | bytes 159752 | tf_op jit(solution)/shard_map/ppermute | solution.py:411
  28.7 9.8 %collective-permute-start.9 = (bf16[32,1664]{1,0:T(8,128)(2,1)S(1)}, bf16[32,1664]{1,0:T(8,128)(2,1)S(1)}, u32[]{:S(2)}, u32[]{:S(2)}) collective-permute-start(bf16[32,1664]{1,0:T(8,128)(2,1)S(1)} %slots.1), channel_id=1, source_target_pairs={{0,3},{1,2},{2,1},{3,0},{4,7},{5,6},{6,5},{7,4},{8,11},{9,10},{10,... | collective-permute-start | bytes 319496 | tf_op jit(solution)/shard_map/ppermute | solution.py:411
  31.4 7.1 %collective-permute-start.8 = (bf16[32,1664]{1,0:T(8,128)(2,1)S(1)}, bf16[32,1664]{1,0:T(8,128)(2,1)S(1)}, u32[]{:S(2)}, u32[]{:S(2)}) collective-permute-start(bf16[32,1664]{1,0:T(8,128)(2,1)S(1)} %slots.1), channel_id=1, source_target_pairs={{0,2},{1,3},{2,0},{3,1},{4,6},{5,7},{6,4},{7,5},{8,10},{9,11},{10,... | collective-permute-start | bytes 319496 | tf_op jit(solution)/shard_map/ppermute | solution.py:411
  31.8 6.7 %collective-permute-start.7 = (bf16[32,1664]{1,0:T(8,128)(2,1)S(1)}, bf16[32,1664]{1,0:T(8,128)(2,1)S(1)}, u32[]{:S(2)}, u32[]{:S(2)}) collective-permute-start(bf16[32,1664]{1,0:T(8,128)(2,1)S(1)} %slots.1), channel_id=1, source_target_pairs={{0,1},{1,0},{2,3},{3,2},{4,5},{5,4},{6,7},{7,6},{8,9},{9,8},{10,11... | collective-permute-start | bytes 319496 | tf_op jit(solution)/shard_map/ppermute | solution.py:411
  38.5 7.8 %collective-permute-start.12 = (bf16[32,1664]{1,0:T(8,128)(2,1)S(1)}, bf16[32,1664]{1,0:T(8,128)(2,1)S(1)}, u32[]{:S(2)}, u32[]{:S(2)}) collective-permute-start(bf16[32,1664]{1,0:T(8,128)(2,1)S(1)} %add_add_fusion), channel_id=1, source_target_pairs={{0,96},{16,112},{32,64},{48,80},{64,32},{80,48},{96,0},{112,16},{1... | collective-permute-start | bytes 319496 | tf_op jit(solution)/shard_map/ppermute | solution.py:411
  38.9 7.5 %collective-permute-start.11 = (bf16[32,1664]{1,0:T(8,128)(2,1)S(1)}, bf16[32,1664]{1,0:T(8,128)(2,1)S(1)}, u32[]{:S(2)}, u32[]{:S(2)}) collective-permute-start(bf16[32,1664]{1,0:T(8,128)(2,1)S(1)} %add_add_fusion), channel_id=1, source_target_pairs={{0,64},{16,80},{32,96},{48,112},{64,0},{80,16},{96,32},{112,48},{1... | collective-permute-start | bytes 319496 | tf_op jit(solution)/shard_map/ppermute | solution.py:411
  39.0 7.4 %collective-permute-start.10 = (bf16[32,1664]{1,0:T(8,128)(2,1)S(1)}, bf16[32,1664]{1,0:T(8,128)(2,1)S(1)}, u32[]{:S(2)}, u32[]{:S(2)}) collective-permute-start(bf16[32,1664]{1,0:T(8,128)(2,1)S(1)} %add_add_fusion), channel_id=1, source_target_pairs={{0,32},{16,48},{32,0},{48,16},{64,96},{80,112},{96,64},{112,80},{1... | collective-permute-start | bytes 319496 | tf_op jit(solution)/shard_map/ppermute | solution.py:411
  46.4 6.0 %copy-start.1 = (bf16[128,1664]{1,0:T(8,128)(2,1)}, bf16[128,1664]{1,0:T(8,128)(2,1)S(1)}, u32[]{:S(2)}) copy-start(bf16[128,1664]{1,0:T(8,128)(2,1)S(1)} %constant_dynamic-update-slice_fusion.one_ref) | copy-start | bytes 1277956
  46.4 6.0 %collective-permute-start.13 = (bf16[128,1664]{1,0:T(8,128)(2,1)S(1)}, bf16[128,1664]{1,0:T(8,128)(2,1)S(1)}, u32[]{:S(2)}, u32[]{:S(2)}) collective-permute-start(bf16[128,1664]{1,0:T(8,128)(2,1)S(1)} %constant_dynamic-update-slice_fusion.one_ref), channel_id=1, source_target_pairs={{0,16},{16,0},{32,48},{48,32},{64,80},{80,64},{96,112},{112,96},{1... | collective-permute-start | bytes 1277960 | tf_op jit(solution)/shard_map/ppermute | solution.py:478
  52.5 0.8 copy-start.2

commit v5 on v4

v5 whole, which is shorter than its diff:
```python
import functools

import jax
import jax.numpy as jnp
from jax import lax
from jax.experimental import pallas as pl
from jax.experimental.pallas import tpu as pltpu
from jax.sharding import PartitionSpec as P

PMAX = 16
EPS = 1e-06
TAU = 6.0
RIDGE = 1.0
AXES = ("rows", "cols")
NDEV = 128
CLASSES = 8
RING = 4
SUB = 4
NORM_TILES = 14
SOLVE_SUB = 4
GRANT = 58 << 20
LOG2E = 1.4426950408889634
TILES = 8
BS = 32
F32 = jnp.float32
BF16 = jnp.bfloat16


def iota(shape, dim):
    return lax.broadcasted_iota(jnp.int32, shape, dim)


def learn(c):
    return (c * (16.0 - c) + 8.0) / 72.0


def own_kernel(
    dev_ref, piv_s, piv_v, solved_ref, emb_ref, fac_ref, send_ref, loc_ref, ebuf, fbuf, sem
):
    rows_here, dim = emb_ref.shape
    k0 = fac_ref.shape[1]
    total = piv_s.shape[0]
    first = dev_ref[0] * rows_here
    pv = piv_v[...]
    before = jnp.sum((pv < first).astype(F32)).astype(jnp.int32)
    upto = jnp.sum((pv < first + rows_here).astype(F32)).astype(jnp.int32)
    mine = upto - before
    loc_ref[0] = before
    loc_ref[1] = mine
    idx = []
    copies = []
    for s in range(PMAX):
        p = piv_s[jnp.minimum(before + s, total - 1)]
        i = jnp.clip(p - first, 0, rows_here - 1)
        loc_ref[2 + s] = i
        idx.append(i)
        base = pl.multiple_of((i // 16) * 16, 16)
        c1 = pltpu.make_async_copy(
            emb_ref.at[pl.ds(base, 16), :], ebuf.at[pl.ds(16 * s, 16), :], sem.at[0, s]
        )
        c2 = pltpu.make_async_copy(
            fac_ref.at[pl.ds(base, 16), :], fbuf.at[pl.ds(16 * s, 16), :], sem.at[1, s]
        )
        c1.start()
        c2.start()
        copies += [c1, c2]
    r = iota((16, 16 * PMAX), 0)
    q = iota((16, 16 * PMAX), 1)
    rc = iota((16, 128), 0)
    lane = iota((16, 128), 1)
    hot = jnp.zeros((16, 16 * PMAX), F32)
    tag = jnp.zeros((16, 128), F32)
    for s in range(PMAX):
        j = before + s
        row = jnp.where(s < mine, 2 * lax.rem(j, CLASSES) + s // CLASSES, -1)
        hot = jnp.where((r == row) & (q == 16 * s + lax.rem(idx[s], 16)), 1.0, hot)
        c = solved_ref[idx[s] // 128, lax.rem(idx[s], 128)].astype(F32)
        tag = jnp.where(rc == row, jnp.where(lane == 0, c, (j + 1).astype(F32)), tag)
    hot = hot.astype(BF16)
    for c in copies:
        c.wait()
    send_ref[:, 0:dim] = jnp.dot(hot, ebuf[...], preferred_element_type=F32).astype(BF16)
    send_ref[:, dim : dim + k0] = jnp.dot(hot, fbuf[...], preferred_element_type=F32).astype(BF16)
    send_ref[:, dim + k0 :] = tag.astype(BF16)


def slots_kernel(cls_ref, *refs):
    out = refs[-1]
    slots, width = out.shape
    data = jnp.concatenate([ref[...] for ref in refs[:-1]], axis=0)
    ids = data[:, width - 127 : width - 126].astype(F32)
    want = (CLASSES * iota((data.shape[0], slots), 1) + cls_ref[0] + 1).astype(F32)
    hot = (ids == want).astype(BF16)
    out[...] = lax.dot_general(
        hot, data, (((0,), (0,)), ((), ())), preferred_element_type=F32
    ).astype(BF16)


def norms_kernel(first, solved_ref, emb_ref, fac_ref, *refs):
    aux_ref = refs[-1]
    i = pl.program_id(0) + first
    tile, dim = emb_ref.shape
    nchunk = tile // 128
    st = solved_ref[pl.ds(i * nchunk, nchunk), :].astype(F32)
    ey = iota((128, 128), 0) == iota((128, 128), 1)
    lane = iota((128, 128), 1)
    ndims = (((1,), (1,)), ((), ()))
    for c in range(nchunk):
        o = slice(128 * c, 128 * c + 128)
        x = emb_ref[o, :].astype(F32)
        f = fac_ref[o, :]
        ff = lax.dot_general(f, f, ndims, preferred_element_type=F32)
        ss = jnp.sum(x * x, axis=1, keepdims=True)
        fs = jnp.sum(jnp.where(ey, ff, 0.0), axis=1, keepdims=True)
        a = 1.0 / jnp.sqrt(ss / dim + EPS)
        b = jnp.broadcast_to(st[c : c + 1, :], (128, 128))
        q = learn(jnp.sum(jnp.where(ey, b, 0.0), axis=1, keepdims=True))
        aux_ref[o, :] = jnp.where(lane == 0, q * q + RIDGE - fs, jnp.where(lane == 1, a, q))

def split3(x):
    h = x.astype(BF16)
    r = x - h.astype(F32)
    m = r.astype(BF16)
    l = (r - m.astype(F32)).astype(BF16)
    return h, m, l


def lanes(x, k):
    return jnp.broadcast_to(x[:, k : k + 1], x.shape)


def sublanes(x, k):
    return jnp.broadcast_to(x[k : k + 1, :], x.shape)


def eliminate(w):
    rows, width = w.shape
    groups = [
        [w[8 * g : 8 * g + 8, 128 * v : 128 * v + 128] for v in range(width // 128)]
        for g in range(rows // 8)
    ]
    srow = iota((8, 128), 0)
    done = []
    for t in range(rows // 8):
        cols = [lanes(groups[t][0], 8 * t + k) for k in range(8)]
        e = [[sublanes(cols[k], i) for k in range(i + 1)] for i in range(8)]
        below = {
            g: [lanes(groups[g][0], 8 * t + k) for k in range(8)]
            for g in range(t + 1, rows // 8)
        }
        tops = [[sublanes(x, j) for x in groups[t]] for j in range(8)]
        m = [[None] * 8 for _ in range(8)]
        n = [[None] * 8 for _ in range(8)]
        for k in range(8):
            inv = 1.0 / e[k][k]
            for i in range(k + 1, 8):
                m[i][k] = e[i][k] * inv
                for j in range(k + 1, i + 1):
                    e[i][j] = e[i][j] - m[i][k] * e[j][k]
            for j in range(k):
                acc = m[k][j]
                for l in range(j + 1, k):
                    acc = acc + m[k][l] * n[l][j]
                n[k][j] = -acc
        root = [1.0 / jnp.sqrt(e[k][k]) for k in range(8)]
        inv = [[root[i] * n[i][j] for j in range(i)] + [root[i]] for i in range(8)]
        cols = []
        for j in range(8):
            c = jnp.where(srow == j, inv[j][j], 0.0)
            for i in range(j + 1, 8):
                c = jnp.where(srow == i, inv[i][j], c)
            cols.append(c)
        out = []
        for v in range(width // 128):
            acc = cols[0] * tops[0][v]
            for j in range(1, 8):
                acc = acc + cols[j] * tops[j][v]
            out.append(acc)
        for g in range(t + 1, rows // 8):
            for j in range(8):
                c = below[g][0] * inv[j][0]
                for k in range(1, j + 1):
                    c = c + below[g][k] * inv[j][k]
                groups[g] = [x - c * sublanes(o, j) for x, o in zip(groups[g], out)]
        done.append(jnp.concatenate(out, axis=1))
    return jnp.concatenate(done, axis=0)


def main_kernel(
    loc_ref, one_ref, two_ref, aux_hbm, emb_hbm, fac_hbm,
    out_hbm, gains_ref, best_ref,
    piv, pvec, ar, minv, mt, panel, aux_ref, emb_ref, fac_ref, out_ref, sem, out_sem,
):
    rows_here, dim = emb_ref.shape
    tile = rows_here // TILES
    k0 = fac_ref.shape[1]
    n = piv.shape[0]

    def fetch(t):
        w = pl.ds(pl.multiple_of(t * tile, tile), tile)
        return [
            pltpu.make_async_copy(src.at[w, :], dst.at[w, :], sem.at[k, t])
            for k, (src, dst) in enumerate(
                ((aux_hbm, aux_ref), (emb_hbm, emb_ref), (fac_hbm, fac_ref))
            )
        ]

    for t in range(TILES):
        for c in fetch(t):
            c.start()

    nchunk = tile // 128
    sub = tile // SUB
    tdims = (((0,), (0,)), ((), ()))
    ndims = (((1,), (1,)), ((), ()))

    jj = iota((n, n), 0)
    qq = iota((n, n), 1)
    eye = (jj == qq).astype(F32)
    data = jnp.concatenate([one_ref[...], two_ref[...]], axis=0)
    ids = data[:, dim + k0 + 1 : dim + k0 + 2].astype(F32)
    permt = (ids == (qq + 1).astype(F32)).astype(BF16)
    v = lax.dot_general(permt, data, tdims, preferred_element_type=F32)
    pb = v.astype(BF16)
    piv[...] = pb[:, 0 : dim + k0]
    cs = 1.0 / jnp.sqrt(
        jnp.sum(v[:, 0:dim] * v[:, 0:dim], axis=1, keepdims=True) / dim + EPS
    )
    cq = learn(v[:, dim + k0 : dim + k0 + 1])
    rs = jnp.sum(eye * cs, axis=0, keepdims=True) * (TAU * LOG2E / dim)
    rq = jnp.sum(eye * cq, axis=0, keepdims=True)
    pvec[0:1, :] = rs
    pvec[1:2, :] = rq
    dots = lax.dot_general(pb[:, 0:dim], piv[:, 0:dim], ndims, preferred_element_type=F32)
    shared = lax.dot_general(
        pb[:, dim : dim + k0], piv[:, dim : dim + k0], ndims, preferred_element_type=F32
    )
    similar = jnp.exp2(dots * (cs * rs) - TAU * LOG2E)
    ar[:, 0:n] = similar * (cq * rq) + RIDGE * eye - shared
    ar[:, n : 2 * n] = eye

    def step(i, carry):
        for c in fetch(i):
            c.wait()
        for c in range(SUB):
            w = pl.ds(pl.multiple_of(i * tile + sub * c, 16), sub)
            a = aux_ref[w, 1:2]
            q = aux_ref[w, 2:3]
            dots = lax.dot_general(
                emb_ref[w, :], piv[:, 0:dim], ndims, preferred_element_type=F32
            )
            shared = lax.dot_general(
                fac_ref[w, :], piv[:, dim : dim + k0], ndims, preferred_element_type=F32
            )
            similar = jnp.exp2(dots * (a * pvec[0:1, :]) - TAU * LOG2E)
            p = similar * (q * pvec[1:2, :]) - shared
            ph = p.astype(BF16)
            panel[w, 0:n] = ph
            panel[w, n : 2 * n] = (p - ph.astype(F32)).astype(BF16)

        rows = pl.ds(pl.multiple_of(i * BS, BS), BS)
        shift = lax.rem(n - i * BS, n)
        a = pltpu.roll(ar[rows, 0:n], shift, 1)
        w = eliminate(jnp.concatenate([a, ar[rows, n : 2 * n]], axis=1))
        u = pltpu.roll(w[:, 0:n], i * BS, 1)
        m = w[:, n : 2 * n]
        minv[rows, :] = m
        uh, um, ul = split3(u)
        mh, mm, ml = split3(m)
        left = jnp.concatenate([uh, uh, um, uh, ul, um], axis=0)
        r_a = jnp.concatenate([uh, um, uh, ul, uh, um], axis=0)
        r_m = jnp.concatenate([mh, mm, mh, ml, mh, mm], axis=0)
        ar[:, 0:n] -= lax.dot_general(left, r_a, tdims, preferred_element_type=F32)
        ar[:, n : 2 * n] -= lax.dot_general(left, r_m, tdims, preferred_element_type=F32)
        return carry

    lax.fori_loop(0, TILES, step, 0)

    t = minv[...].T
    h = t.astype(BF16)
    mt[0:n, :] = h
    mt[n : 2 * n, :] = h
    mt[2 * n : 3 * n, :] = (t - h.astype(F32)).astype(BF16)
    best_ref[...] = jnp.full(best_ref.shape, -jnp.inf, F32)

    def ridge(s, carry):
        at = loc_ref[2 + s]
        w = pl.ds(pl.multiple_of((at // 16) * 16, 16), 16)
        p = panel[w, 0:n].astype(F32) + panel[w, n : 2 * n].astype(F32)
        here = (iota((16, n), 0) == lax.rem(at, 16)) & (iota((16, n), 1) == loc_ref[0] + s)
        p = p + jnp.where(here, RIDGE, 0.0)
        ph = p.astype(BF16)
        panel[w, 0:n] = ph
        panel[w, n : 2 * n] = (p - ph.astype(F32)).astype(BF16)
        return carry

    lax.fori_loop(0, jnp.minimum(loc_ref[1], PMAX), ridge, 0)

    def store(t):
        w = pl.ds(pl.multiple_of(t * tile, tile), tile)
        return pltpu.make_async_copy(out_ref.at[w, :], out_hbm.at[w, :], out_sem.at[t])

    def solve(t, carry):
        gs = []
        part = tile // SOLVE_SUB
        for c in range(SOLVE_SUB):
            w = pl.ds(pl.multiple_of(t * tile + part * c, 16), part)
            both = jnp.concatenate([panel[w, :], panel[w, 0:n]], axis=1)
            full = jnp.dot(both, mt[...], preferred_element_type=F32)
            out_ref[w, :] = full.astype(BF16)
            gs.append(aux_ref[w, 0:1] - jnp.sum(full * full, axis=1, keepdims=True))
        g = jnp.concatenate(gs, axis=0)
        ey = iota((128, 128), 0) == iota((128, 128), 1)
        lines = []
        for c in range(nchunk):
            b = jnp.broadcast_to(g[128 * c : 128 * c + 128, :], (128, 128))
            lines.append(jnp.sum(jnp.where(ey, b, 0.0), axis=0, keepdims=True))
        lines = jnp.concatenate(lines, axis=0)
        gains_ref[pl.ds(t * nchunk, nchunk), :] = lines
        best_ref[...] = jnp.maximum(best_ref[...], jnp.max(lines))
        store(t).start()
        return carry

    lax.fori_loop(0, TILES, solve, 0)
    for t in range(TILES):
        store(t).wait()


def main_call(loc, one, two, aux, embeddings, factor_cols):
    rows_here, dim = embeddings.shape
    k0 = factor_cols.shape[1]
    total = one.shape[0] + two.shape[0]
    tile = rows_here // TILES
    smem = pl.BlockSpec(memory_space=pltpu.SMEM)
    vmem = pl.BlockSpec(memory_space=pltpu.VMEM)
    hbm = pl.BlockSpec(memory_space=pltpu.HBM)
    return pl.pallas_call(
        main_kernel,
        out_shape=(
            jax.ShapeDtypeStruct((rows_here, total), BF16),
            jax.ShapeDtypeStruct((rows_here // 128, 128), F32),
            jax.ShapeDtypeStruct((NDEV, 128), F32),
        ),
        in_specs=[smem, vmem, vmem, hbm, hbm, hbm],
        out_specs=(hbm, vmem, vmem),
        scratch_shapes=[
            pltpu.VMEM((total, dim + k0), BF16),
            pltpu.VMEM((8, total), F32),
            pltpu.VMEM((total, 2 * total), F32),
            pltpu.VMEM((total, total), F32),
            pltpu.VMEM((3 * total, total), BF16),
            pltpu.VMEM((rows_here, 2 * total), BF16),
            pltpu.VMEM((rows_here, 128), F32),
            pltpu.VMEM((rows_here, dim), BF16),
            pltpu.VMEM((rows_here, k0), BF16),
            pltpu.VMEM((rows_here, total), BF16),
            pltpu.SemaphoreType.DMA((3, TILES)),
            pltpu.SemaphoreType.DMA((TILES,)),
        ],
        compiler_params=pltpu.CompilerParams(vmem_limit_bytes=GRANT),
        name="panel_factor",
    )(loc, one, two, aux, embeddings, factor_cols)


def norms_part(solved2, embeddings, factor_cols, first, last, aux):
    rows_here, dim = embeddings.shape
    k0 = factor_cols.shape[1]
    tile = rows_here // NORM_TILES
    rows = (last - first) * tile
    specs = [
        pl.BlockSpec(memory_space=pltpu.VMEM),
        pl.BlockSpec((tile, dim), lambda i: (i + first, 0)),
        pl.BlockSpec((tile, k0), lambda i: (i + first, 0)),
    ]
    args = (solved2, embeddings, factor_cols)
    if aux is not None:
        specs.append(pl.BlockSpec(memory_space=pl.ANY))
        args += (aux,)
    return pl.pallas_call(
        functools.partial(norms_kernel, first),
        grid=(last - first,),
        out_shape=jax.ShapeDtypeStruct((rows_here, 128), F32),
        in_specs=specs,
        out_specs=pl.BlockSpec((tile, 128), lambda i: (i + first, 0)),
        input_output_aliases={} if aux is None else {3: 0},
        compiler_params=pltpu.CompilerParams(
            dimension_semantics=("arbitrary",), vmem_limit_bytes=GRANT
        ),
        cost_estimate=pl.CostEstimate(
            flops=rows * (dim + k0) * 4, bytes_accessed=rows * (dim + k0) * 2, transcendentals=0
        ),
        name="row_norms",
    )(*args)


def ring(values, axis, pairs):
    return [lax.ppermute(v, axis, p) for v, p in zip(values, pairs)]


def body(embeddings, factor_cols, solved, pivots):
    rows_here, dim = embeddings.shape
    k0 = factor_cols.shape[1]
    total = pivots.shape[0]
    width = dim + k0 + 128
    tile = rows_here // TILES
    r = lax.axis_index("rows").astype(jnp.int32)
    c = lax.axis_index("cols").astype(jnp.int32)
    dev = (r * 16 + c).reshape(1)
    solved2 = solved.reshape(rows_here // 128, 128)
    piv2 = pivots.reshape(total // 128, 128)
    smem = pl.BlockSpec(memory_space=pltpu.SMEM)
    vmem = pl.BlockSpec(memory_space=pltpu.VMEM)
    hbm = pl.BlockSpec(memory_space=pltpu.HBM)
    small = pltpu.CompilerParams(vmem_limit_bytes=8 << 20)
    wide = lambda rows: jax.ShapeDtypeStruct((rows, width), BF16)
    swap = [(i, i ^ 1) for i in range(8)]
    zs = [[(i, i ^ (2 * k)) for i in range(8)] for k in range(1, RING)]
    xs = [[(i, i ^ (4 * k)) for i in range(16)] for k in range(1, RING)]
    ys = [[(i, i ^ k) for i in range(16)] for k in range(1, RING)]

    send, loc = pl.pallas_call(
        own_kernel,
        out_shape=(wide(16), jax.ShapeDtypeStruct((2 + PMAX,), jnp.int32)),
        in_specs=[smem, smem, vmem, smem, hbm, hbm],
        out_specs=(vmem, smem),
        scratch_shapes=[
            pltpu.VMEM((16 * PMAX, dim), BF16),
            pltpu.VMEM((16 * PMAX, k0), BF16),
            pltpu.SemaphoreType.DMA((2, PMAX)),
        ],
        compiler_params=pltpu.CompilerParams(vmem_limit_bytes=GRANT),
        name="own_rows",
    )(dev, pivots, piv2, solved2, embeddings, factor_cols)
    mine = lax.all_to_all(send.reshape(CLASSES, 2, width), "rows", 0, 0).reshape(16, width)
    counts, mine = lax.optimization_barrier((solved2, mine))
    got = [mine] + ring([mine] * 3, "cols", xs)
    aux = norms_part(counts, embeddings, factor_cols, 0, 5, None)
    aux, *got = lax.optimization_barrier((aux, *got))
    mine = pl.pallas_call(
        slots_kernel,
        out_shape=wide(total // CLASSES),
        in_specs=[smem] + [vmem] * RING,
        out_specs=vmem,
        compiler_params=small,
        name="slots",
    )(r.reshape(1), *got)
    counts, mine = lax.optimization_barrier((solved2, mine))
    got = [mine] + ring([mine] * 3, "cols", ys)
    aux = norms_part(counts, embeddings, factor_cols, 5, 10, aux)
    aux, *got = lax.optimization_barrier((aux, *got))
    mine = got[0] + got[1] + got[2] + got[3]
    counts, mine = lax.optimization_barrier((solved2, mine))
    got = [mine] + ring([mine] * 3, "rows", zs)
    aux = norms_part(counts, embeddings, factor_cols, 10, NORM_TILES, aux)
    aux, *got = lax.optimization_barrier((aux, *got))
    one = jnp.concatenate(got, axis=0)
    two = lax.ppermute(one, "rows", swap)

    new_cols, gains, best = main_call(loc, one, two, aux, embeddings, factor_cols)
    peers = lax.all_to_all(best.reshape(NDEV, 1, 128), AXES, 0, 0)
    return new_cols, gains.reshape(rows_here), jnp.max(peers)


def solution(mesh):
    in_specs = (P(AXES, None), P(AXES, None), P(AXES), P())
    out_specs = (P(AXES, None), P(AXES), P())
    return jax.shard_map(body, mesh=mesh, in_specs=in_specs, out_specs=out_specs, check_vma=False)
```

time: 96.9 us -> 95.9 us (0.990)
  blocking collectives: 16.7 us -> 28.6 us
  starting transfers between devices: 21.5 us -> 13.4 us
  waiting for transfers between devices: 6.39 us -> 1.42 us
    all_to_all x0 -> x1, blocking collectives: none -> 11.5 us  [body(): lax.all_to_all(send.reshape(CLASSES, 2, width), 'rows', 0, 0)]
    ppermute x12 -> x9, starting transfers between devices: 15.2 us -> 10.3 us  [ring(): return [lax.ppermute(v, axis, p) for v, p in zip(values, pairs)]]
    ppermute x12 -> x9, waiting for transfers between devices: 3.93 us -> 0.02 us  [ring(): return [lax.ppermute(v, axis, p) for v, p in zip(values, pairs)]]
    ppermute x1 -> x0, starting transfers between devices: 1.66 us -> none  [body(): recv = lax.ppermute(send, 'rows', swap)]
    ppermute x1, starting transfers between devices: 4.62 us -> 3.08 us  [body(): two = lax.ppermute(one, 'rows', swap)]
    ppermute x1 -> x0, waiting for transfers between devices: 1.06 us -> none  [body(): recv = lax.ppermute(send, 'rows', swap)]
    pallas_call x4 -> x2, Pallas kernels: 30.1 us -> 30.2 us  [the longest x1 26.1 us: main_call(): pl.pallas_call(main_kernel, out_shape=(jax.ShapeDtypeStruct((rows_here, t...]
  transfers between devices with their start and end apart: 14 -> 10, of which waited for: 4 -> 1; matrix products, arithmetic and copies ran while one was open for 0% -> 0% of each run, Pallas kernels for 18% -> 19%
where the time goes in v5:
time: 95.9 us; the launch traced here: 95.2 us
  Pallas kernels  48.6 us (51%)
  blocking collectives  28.6 us (30%)
  starting transfers between devices  13.4 us (14%)
  local copies, waits for them, and re-layouts  1.68 us (2%)
  waiting for transfers between devices  1.42 us (1%)
    pallas_call x1, Pallas kernels, main_call(): pl.pallas_call(main_kernel, out_shape=(jax.ShapeDtypeStruct((rows_here, t...  26.1 us
    pallas_call x3, Pallas kernels, norms_part(): pl.pallas_call(functools.partial(norms_kernel, first), grid=(last - first...  18.1 us
    all_to_all x1, blocking collectives, body(): peers = lax.all_to_all(best.reshape(NDEV, 1, 128), AXES, 0, 0)  17.1 us
    all_to_all x1, blocking collectives, body(): lax.all_to_all(send.reshape(CLASSES, 2, width), 'rows', 0, 0)  11.5 us
    ppermute x9, starting transfers between devices, ring(): return [lax.ppermute(v, axis, p) for v, p in zip(values, pairs)]  10.3 us
    pallas_call x1, Pallas kernels, body(): pl.pallas_call(own_kernel, out_shape=(wide(16), jax.ShapeDtypeStruct((2 +...  4.11 us
    ppermute x1, starting transfers between devices, body(): two = lax.ppermute(one, 'rows', swap)  3.08 us
  transfers between devices with their start and end apart: 10, of which 1 were waited for; matrix products, arithmetic and copies ran while one was open for 0% of the time, Pallas kernels for 19%

profile of v5, /device:TPU:1, one launch (start us, length us, event | category | flops | bytes accessed | tf_op | source)
XLA Modules:
  0.0 95.2 jit_solution(12966805382537090902)
XLA Ops:
  0.6 4.1 %own_rows.1 = (bf16[16,1664]{1,0:T(8,128)(2,1)}, s32[18]{0:T(128)}) custom-call(s32[1]{0:T(128)} %bitcast.dev_ref, s32[256]{0:T(256)} %piv_s.1, s32[2,128]{1,0:T(2,128)} %bitcast.13, s32[56,128]{1,0:T(8,128)} %bitcast.8, bf16[7168,1024]{1,0:T(8,128)(2,1)} %emb_hbm.1, bf16[7168,512]{1,0:T(8,128)(2,1)} %fac_hbm.1), custom_call_target="tpu_custom_call" | custom-call | tf_op jit(solution)/shard_map/own_rows/pallas_call | solution.py:421
  4.8 0.8 reshape.34
  5.6 11.5 %all_to_all.10 = bf16[8,2,1664]{2,1,0:T(2,128)(2,1)S(1)} all-to-all(bf16[8,2,1664]{2,1,0:T(2,128)(2,1)S(1)} %reshape.34), channel_id=1, replica_groups=mesh['rows'=8,'cols'=16] {'rows'}, dimensions={0} | all-to-all | bytes 106496 | tf_op jit(solution)/shard_map/all_to_all | solution.py:434
  17.1 2.6 %collective-permute-start.2 = (bf16[16,1664]{1,0:T(8,128)(2,1)S(1)}, bf16[16,1664]{1,0:T(8,128)(2,1)S(1)}, u32[]{:S(2)}, u32[]{:S(2)}) collective-permute-start(bf16[16,1664]{1,0:T(8,128)(2,1)S(1)} %reshape.35.refs_0_), channel_id=1, source_target_pairs={{0,12},{1,13},{2,14},{3,15},{4,8},{5,9},{6,10},{7,11},{8,4},{9,5},... | collective-permute-start | bytes 159752 | tf_op jit(solution)/shard_map/ppermute | solution.py:397
  19.7 0.6 collective-permute-start.1
  20.3 0.1 collective-permute-start
  20.4 6.5 %row_norms.3.refs_0_ = f32[7168,128]{1,0:T(8,128)} custom-call(s32[56,128]{1,0:T(8,128)} %bitcast.9, bf16[7168,1024]{1,0:T(8,128)(2,1)} %emb_hbm.1, bf16[7168,512]{1,0:T(8,128)(2,1)} %fac_hbm.1), custom_call_target="tpu_custom_call" | custom-call | flops 15728640 | bytes 7864320 | tf_op jit(solution)/shard_map/row_norms/pallas_call | solution.py:379
  26.9 0.0 collective-permute-done.2.refs_3_
  26.9 0.0 collective-permute-done.1.refs_2_
  26.9 0.0 collective-permute-done.refs_1_
  26.9 0.3 slots.1
  27.2 3.0 %collective-permute-start.5 = (bf16[32,1664]{1,0:T(8,128)(2,1)S(1)}, bf16[32,1664]{1,0:T(8,128)(2,1)S(1)}, u32[]{:S(2)}, u32[]{:S(2)}) collective-permute-start(bf16[32,1664]{1,0:T(8,128)(2,1)S(1)} %slots.1), channel_id=1, source_target_pairs={{0,3},{1,2},{2,1},{3,0},{4,7},{5,6},{6,5},{7,4},{8,11},{9,10},{10,... | collective-permute-start | bytes 319496 | tf_op jit(solution)/shard_map/ppermute | solution.py:397
  30.2 0.2 collective-permute-start.4
  30.4 0.5 collective-permute-start.3
  30.9 6.5 %row_norms.4.refs_0_ = f32[7168,128]{1,0:T(8,128)} custom-call(s32[56,128]{1,0:T(8,128)} %bitcast.10, bf16[7168,1024]{1,0:T(8,128)(2,1)} %emb_hbm.1, bf16[7168,512]{1,0:T(8,128)(2,1)} %fac_hbm.1, f32[7168,128]{1,0:T(8,128)} %row_norms.3.refs_0_), custom_call_target="tpu_custom_call", output_to_operand_aliasing={{}: (3, {})} | custom-call | flops 15728640 | bytes 7864320 | tf_op jit(solution)/shard_map/row_norms/pallas_call | solution.py:379
  37.4 0.0 collective-permute-done.5
  37.4 0.0 collective-permute-done.4
  37.4 0.0 collective-permute-done.3
  37.4 1.0 %collective-permute-start.8 = (bf16[32,1664]{1,0:T(8,128)(2,1)S(1)}, bf16[32,1664]{1,0:T(8,128)(2,1)S(1)}, u32[]{:S(2)}, u32[]{:S(2)}) collective-permute-start(bf16[32,1664]{1,0:T(8,128)(2,1)S(1)} %add_add_fusion), channel_id=1, source_target_pairs={{0,96},{16,112},{32,64},{48,80},{64,32},{80,48},{96,0},{112,16},{1... | collective-permute-start | bytes 319496 | tf_op jit(solution)/shard_map/ppermute | solution.py:397
  38.4 1.2 %collective-permute-start.7 = (bf16[32,1664]{1,0:T(8,128)(2,1)S(1)}, bf16[32,1664]{1,0:T(8,128)(2,1)S(1)}, u32[]{:S(2)}, u32[]{:S(2)}) collective-permute-start(bf16[32,1664]{1,0:T(8,128)(2,1)S(1)} %add_add_fusion), channel_id=1, source_target_pairs={{0,64},{16,80},{32,96},{48,112},{64,0},{80,16},{96,32},{112,48},{1... | collective-permute-start | bytes 319496 | tf_op jit(solution)/shard_map/ppermute | solution.py:397
  39.6 1.2 %collective-permute-start.6 = (bf16[32,1664]{1,0:T(8,128)(2,1)S(1)}, bf16[32,1664]{1,0:T(8,128)(2,1)S(1)}, u32[]{:S(2)}, u32[]{:S(2)}) collective-permute-start(bf16[32,1664]{1,0:T(8,128)(2,1)S(1)} %add_add_fusion), channel_id=1, source_target_pairs={{0,32},{16,48},{32,0},{48,16},{64,96},{80,112},{96,64},{112,80},{1... | collective-permute-start | bytes 319496 | tf_op jit(solution)/shard_map/ppermute | solution.py:397
  40.7 5.2 %row_norms.5.aux_hbm = f32[7168,128]{1,0:T(8,128)} custom-call(s32[56,128]{1,0:T(8,128)} %bitcast.11, bf16[7168,1024]{1,0:T(8,128)(2,1)} %emb_hbm.1, bf16[7168,512]{1,0:T(8,128)(2,1)} %fac_hbm.1, f32[7168,128]{1,0:T(8,128)} %row_norms.4.refs_0_), custom_call_target="tpu_custom_call", output_to_operand_aliasing={{}: (3, {})} | custom-call | flops 12582912 | bytes 6291456 | tf_op jit(solution)/shard_map/row_norms/pallas_call | solution.py:379
  45.9 0.0 collective-permute-done.8
  45.9 0.0 collective-permute-done.7
  45.9 0.0 collective-permute-done.6
  46.0 3.1 %collective-permute-start.9 = (bf16[128,1664]{1,0:T(8,128)(2,1)S(1)}, bf16[128,1664]{1,0:T(8,128)(2,1)S(1)}, u32[]{:S(2)}, u32[]{:S(2)}) collective-permute-start(bf16[128,1664]{1,0:T(8,128)(2,1)S(1)} %constant_dynamic-update-slice_fusion.one_ref), channel_id=1, source_target_pairs={{0,16},{16,0},{32,48},{48,32},{64,80},{80,64},{96,112},{112,96},{1... | collective-permute-start | bytes 1277960 | tf_op jit(solution)/shard_map/ppermute | solution.py:457
  49.1 1.4 %collective-permute-done.9.two_ref = bf16[128,1664]{1,0:T(8,128)(2,1)S(1)} collective-permute-done((bf16[128,1664]{1,0:T(8,128)(2,1)S(1)}, bf16[128,1664]{1,0:T(8,128)(2,1)S(1)}, u32[]{:S(2)}, u32[]{:S(2)}) %collective-permute-start.9) | collective-permute-done | bytes 426016 | tf_op jit(solution)/shard_map/ppermute | solution.py:457
  50.5 0.0 copy-done
  50.5 0.8 copy-done.1
  51.3 26.1 %panel_factor.1 = (bf16[7168,256]{1,0:T(8,128)(2,1)}, f32[56,128]{1,0:T(8,128)}, f32[128,128]{1,0:T(8,128)}) custom-call(s32[18]{0:T(128)} %get-tuple-element.29.loc_ref, bf16[128,1664]{1,0:T(8,128)(2,1)} %copy-done, bf16[128,1664]{1,0:T(8,128)(2,1)} %copy-done.1, f32[7168,128]{1,0:T(8,128)} %row_norms.5.aux_hbm, bf16[7168,1024]{1,0:T(8,128)(2,1)} %emb_hbm.1, ...), custom_call_target="tpu_custom_call" | custom-call | tf_op jit(solution)/shard_map/panel_factor/pallas_call | solution.py:337
  77.3 17.1 %all_to_all.11 = f32[128,1,128]{2,1,0:T(1,128)S(1)} all-to-all(f32[128,1,128]{2,1,0:T(1,128)} %bitcast.12), channel_id=1, replica_groups=mesh['rows'=8,'cols'=16] {'rows','cols'}, dimensions={0} | all-to-all | bytes 131072 | tf_op jit(solution)/shard_map/all_to_all | solution.py:460
  94.5 0.7 reduce_max.9
  (8 shorter events, 0.1 us)
Async XLA Ops:
  17.1 9.8 %collective-permute-start.2 = (bf16[16,1664]{1,0:T(8,128)(2,1)S(1)}, bf16[16,1664]{1,0:T(8,128)(2,1)S(1)}, u32[]{:S(2)}, u32[]{:S(2)}) collective-permute-start(bf16[16,1664]{1,0:T(8,128)(2,1)S(1)} %reshape.35.refs_0_), channel_id=1, source_target_pairs={{0,12},{1,13},{2,14},{3,15},{4,8},{5,9},{6,10},{7,11},{8,4},{9,5},... | collective-permute-start | bytes 159752 | tf_op jit(solution)/shard_map/ppermute | solution.py:397
  19.7 7.3 %collective-permute-start.1 = (bf16[16,1664]{1,0:T(8,128)(2,1)S(1)}, bf16[16,1664]{1,0:T(8,128)(2,1)S(1)}, u32[]{:S(2)}, u32[]{:S(2)}) collective-permute-start(bf16[16,1664]{1,0:T(8,128)(2,1)S(1)} %reshape.35.refs_0_), channel_id=1, source_target_pairs={{0,8},{1,9},{2,10},{3,11},{4,12},{5,13},{6,14},{7,15},{8,0},{9,1},... | collective-permute-start | bytes 159752 | tf_op jit(solution)/shard_map/ppermute | solution.py:397
  20.3 6.6 %collective-permute-start = (bf16[16,1664]{1,0:T(8,128)(2,1)S(1)}, bf16[16,1664]{1,0:T(8,128)(2,1)S(1)}, u32[]{:S(2)}, u32[]{:S(2)}) collective-permute-start(bf16[16,1664]{1,0:T(8,128)(2,1)S(1)} %reshape.35.refs_0_), channel_id=1, source_target_pairs={{0,4},{1,5},{2,6},{3,7},{4,0},{5,1},{6,2},{7,3},{8,12},{9,13},{10,... | collective-permute-start | bytes 159752 | tf_op jit(solution)/shard_map/ppermute | solution.py:397
  27.2 10.1 %collective-permute-start.5 = (bf16[32,1664]{1,0:T(8,128)(2,1)S(1)}, bf16[32,1664]{1,0:T(8,128)(2,1)S(1)}, u32[]{:S(2)}, u32[]{:S(2)}) collective-permute-start(bf16[32,1664]{1,0:T(8,128)(2,1)S(1)} %slots.1), channel_id=1, source_target_pairs={{0,3},{1,2},{2,1},{3,0},{4,7},{5,6},{6,5},{7,4},{8,11},{9,10},{10,... | collective-permute-start | bytes 319496 | tf_op jit(solution)/shard_map/ppermute | solution.py:397
  30.2 7.2 %collective-permute-start.4 = (bf16[32,1664]{1,0:T(8,128)(2,1)S(1)}, bf16[32,1664]{1,0:T(8,128)(2,1)S(1)}, u32[]{:S(2)}, u32[]{:S(2)}) collective-permute-start(bf16[32,1664]{1,0:T(8,128)(2,1)S(1)} %slots.1), channel_id=1, source_target_pairs={{0,2},{1,3},{2,0},{3,1},{4,6},{5,7},{6,4},{7,5},{8,10},{9,11},{10,... | collective-permute-start | bytes 319496 | tf_op jit(solution)/shard_map/ppermute | solution.py:397
  30.4 7.0 %collective-permute-start.3 = (bf16[32,1664]{1,0:T(8,128)(2,1)S(1)}, bf16[32,1664]{1,0:T(8,128)(2,1)S(1)}, u32[]{:S(2)}, u32[]{:S(2)}) collective-permute-start(bf16[32,1664]{1,0:T(8,128)(2,1)S(1)} %slots.1), channel_id=1, source_target_pairs={{0,1},{1,0},{2,3},{3,2},{4,5},{5,4},{6,7},{7,6},{8,9},{9,8},{10,11... | collective-permute-start | bytes 319496 | tf_op jit(solution)/shard_map/ppermute | solution.py:397
  37.4 8.5 %collective-permute-start.8 = (bf16[32,1664]{1,0:T(8,128)(2,1)S(1)}, bf16[32,1664]{1,0:T(8,128)(2,1)S(1)}, u32[]{:S(2)}, u32[]{:S(2)}) collective-permute-start(bf16[32,1664]{1,0:T(8,128)(2,1)S(1)} %add_add_fusion), channel_id=1, source_target_pairs={{0,96},{16,112},{32,64},{48,80},{64,32},{80,48},{96,0},{112,16},{1... | collective-permute-start | bytes 319496 | tf_op jit(solution)/shard_map/ppermute | solution.py:397
  38.4 7.5 %collective-permute-start.7 = (bf16[32,1664]{1,0:T(8,128)(2,1)S(1)}, bf16[32,1664]{1,0:T(8,128)(2,1)S(1)}, u32[]{:S(2)}, u32[]{:S(2)}) collective-permute-start(bf16[32,1664]{1,0:T(8,128)(2,1)S(1)} %add_add_fusion), channel_id=1, source_target_pairs={{0,64},{16,80},{32,96},{48,112},{64,0},{80,16},{96,32},{112,48},{1... | collective-permute-start | bytes 319496 | tf_op jit(solution)/shard_map/ppermute | solution.py:397
  39.6 6.4 %collective-permute-start.6 = (bf16[32,1664]{1,0:T(8,128)(2,1)S(1)}, bf16[32,1664]{1,0:T(8,128)(2,1)S(1)}, u32[]{:S(2)}, u32[]{:S(2)}) collective-permute-start(bf16[32,1664]{1,0:T(8,128)(2,1)S(1)} %add_add_fusion), channel_id=1, source_target_pairs={{0,32},{16,48},{32,0},{48,16},{64,96},{80,112},{96,64},{112,80},{1... | collective-permute-start | bytes 319496 | tf_op jit(solution)/shard_map/ppermute | solution.py:397
  46.0 4.5 %copy-start = (bf16[128,1664]{1,0:T(8,128)(2,1)}, bf16[128,1664]{1,0:T(8,128)(2,1)S(1)}, u32[]{:S(2)}) copy-start(bf16[128,1664]{1,0:T(8,128)(2,1)S(1)} %constant_dynamic-update-slice_fusion.one_ref) | copy-start | bytes 1277956
  46.0 4.5 %collective-permute-start.9 = (bf16[128,1664]{1,0:T(8,128)(2,1)S(1)}, bf16[128,1664]{1,0:T(8,128)(2,1)S(1)}, u32[]{:S(2)}, u32[]{:S(2)}) collective-permute-start(bf16[128,1664]{1,0:T(8,128)(2,1)S(1)} %constant_dynamic-update-slice_fusion.one_ref), channel_id=1, source_target_pairs={{0,16},{16,0},{32,48},{48,32},{64,80},{80,64},{96,112},{112,96},{1... | collective-permute-start | bytes 1277960 | tf_op jit(solution)/shard_map/ppermute | solution.py:457
  50.5 0.8 copy-start.1

commit v6 on v5

--- a/solution.py
+++ b/solution.py
@@ -96,26 +96,56 @@
     ).astype(BF16)
 
 
-def norms_kernel(first, solved_ref, emb_ref, fac_ref, *refs):
-    aux_ref = refs[-1]
-    i = pl.program_id(0) + first
-    tile, dim = emb_ref.shape
+def norms_kernel(first, solved_ref, emb_hbm, fac_hbm, *refs):
+    aux_hbm, emb_ref, fac_ref, aux_ref, sem, out_sem = refs[-6:]
+    rows, dim = emb_ref.shape
+    tile = emb_hbm.shape[0] // NORM_TILES
     nchunk = tile // 128
-    st = solved_ref[pl.ds(i * nchunk, nchunk), :].astype(F32)
     ey = iota((128, 128), 0) == iota((128, 128), 1)
     lane = iota((128, 128), 1)
     ndims = (((1,), (1,)), ((), ()))
-    for c in range(nchunk):
-        o = slice(128 * c, 128 * c + 128)
-        x = emb_ref[o, :].astype(F32)
-        f = fac_ref[o, :]
-        ff = lax.dot_general(f, f, ndims, preferred_element_type=F32)
-        ss = jnp.sum(x * x, axis=1, keepdims=True)
-        fs = jnp.sum(jnp.where(ey, ff, 0.0), axis=1, keepdims=True)
-        a = 1.0 / jnp.sqrt(ss / dim + EPS)
-        b = jnp.broadcast_to(st[c : c + 1, :], (128, 128))
-        q = learn(jnp.sum(jnp.where(ey, b, 0.0), axis=1, keepdims=True))
-        aux_ref[o, :] = jnp.where(lane == 0, q * q + RIDGE - fs, jnp.where(lane == 1, a, q))
+
+    def fetch(t):
+        src = pl.ds(pl.multiple_of((first + t) * tile, tile), tile)
+        dst = pl.ds(pl.multiple_of(t * tile, tile), tile)
+        return [
+            pltpu.make_async_copy(x.at[src, :], y.at[dst, :], sem.at[k, t])
+            for k, (x, y) in enumerate(((emb_hbm, emb_ref), (fac_hbm, fac_ref)))
+        ]
+
+    def store(t):
+        src = pl.ds(pl.multiple_of(t * tile, tile), tile)
+        dst = pl.ds(pl.multiple_of((first + t) * tile, tile), tile)
+        return pltpu.make_async_copy(aux_ref.at[src, :], aux_hbm.at[dst, :], out_sem.at[t])
+
+    for t in range(rows // tile):
+        for c in fetch(t):
+            c.start()
+
+    def step(t, carry):
+        st = solved_ref[pl.ds((first + t) * nchunk, nchunk), :].astype(F32)
+        for c in fetch(t):
+            c.wait()
+        for c in range(nchunk):
+            o = pl.ds(pl.multiple_of(t * tile + 128 * c, 128), 128)
+            x = emb_ref[o, :].astype(F32)
+            f = fac_ref[o, :]
+            ff = lax.dot_general(f, f, ndims, preferred_element_type=F32)
+            ss = jnp.sum(x * x, axis=1, keepdims=True)
+            fs = jnp.sum(jnp.where(ey, ff, 0.0), axis=1, keepdims=True)
+            a = 1.0 / jnp.sqrt(ss / dim + EPS)
+            b = jnp.broadcast_to(st[c : c + 1, :], (128, 128))
+            q = learn(jnp.sum(jnp.where(ey, b, 0.0), axis=1, keepdims=True))
+            aux_ref[o, :] = jnp.where(
+                lane == 0, q * q + RIDGE - fs, jnp.where(lane == 1, a, q)
+            )
+        store(t).start()
+        return carry
+
+    lax.fori_loop(0, rows // tile, step, 0)
+    for t in range(rows // tile):
+        store(t).wait()
+
 
 def split3(x):
     h = x.astype(BF16)
@@ -367,25 +397,26 @@
     k0 = factor_cols.shape[1]
     tile = rows_here // NORM_TILES
     rows = (last - first) * tile
-    specs = [
-        pl.BlockSpec(memory_space=pltpu.VMEM),
-        pl.BlockSpec((tile, dim), lambda i: (i + first, 0)),
-        pl.BlockSpec((tile, k0), lambda i: (i + first, 0)),
-    ]
+    hbm = pl.BlockSpec(memory_space=pltpu.HBM)
+    specs = [pl.BlockSpec(memory_space=pltpu.VMEM), hbm, hbm]
     args = (solved2, embeddings, factor_cols)
     if aux is not None:
-        specs.append(pl.BlockSpec(memory_space=pl.ANY))
+        specs.append(hbm)
         args += (aux,)
     return pl.pallas_call(
         functools.partial(norms_kernel, first),
-        grid=(last - first,),
         out_shape=jax.ShapeDtypeStruct((rows_here, 128), F32),
         in_specs=specs,
-        out_specs=pl.BlockSpec((tile, 128), lambda i: (i + first, 0)),
+        out_specs=hbm,
+        scratch_shapes=[
+            pltpu.VMEM((rows, dim), BF16),
+            pltpu.VMEM((rows, k0), BF16),
+            pltpu.VMEM((rows, 128), F32),
+            pltpu.SemaphoreType.DMA((2, last - first)),
+            pltpu.SemaphoreType.DMA((last - first,)),
+        ],
         input_output_aliases={} if aux is None else {3: 0},
-        compiler_params=pltpu.CompilerParams(
-            dimension_semantics=("arbitrary",), vmem_limit_bytes=GRANT
-        ),
+        compiler_params=pltpu.CompilerParams(vmem_limit_bytes=GRANT),
         cost_estimate=pl.CostEstimate(
             flops=rows * (dim + k0) * 4, bytes_accessed=rows * (dim + k0) * 2, transcendentals=0
         ),

time: 95.9 us -> 93.5 us (0.975)
  Pallas kernels: 48.6 us -> 46.3 us
    pallas_call x3, Pallas kernels: 18.1 us -> 15.7 us  [norms_part(): pl.pallas_call(functools.partial(norms_kernel, first), out_shape=jax.Shap...]
  transfers between devices with their start and end apart: 10 -> 10, of which waited for: 1 -> 1; matrix products, arithmetic and copies ran while one was open for 0% -> 0% of each run, Pallas kernels for 19% -> 17%
where the time goes in v6:
time: 93.5 us; the launch traced here: 92.8 us
  Pallas kernels  46.3 us (50%)
  blocking collectives  28.5 us (30%)
  starting transfers between devices  13.4 us (14%)
  local copies, waits for them, and re-layouts  1.68 us (2%)
  waiting for transfers between devices  1.42 us (2%)
    pallas_call x1, Pallas kernels, main_call(): pl.pallas_call(main_kernel, out_shape=(jax.ShapeDtypeStruct((rows_here, t...  26 us
    all_to_all x1, blocking collectives, body(): peers = lax.all_to_all(best.reshape(NDEV, 1, 128), AXES, 0, 0)  17.1 us
    pallas_call x3, Pallas kernels, norms_part(): pl.pallas_call(functools.partial(norms_kernel, first), out_shape=jax.Shap...  15.7 us
    all_to_all x1, blocking collectives, body(): lax.all_to_all(send.reshape(CLASSES, 2, width), 'rows', 0, 0)  11.3 us
    ppermute x9, starting transfers between devices, ring(): return [lax.ppermute(v, axis, p) for v, p in zip(values, pairs)]  10.1 us
    pallas_call x1, Pallas kernels, body(): pl.pallas_call(own_kernel, out_shape=(wide(16), jax.ShapeDtypeStruct((2 +...  4.3 us
    ppermute x1, starting transfers between devices, body(): two = lax.ppermute(one, 'rows', swap)  3.31 us
  transfers between devices with their start and end apart: 10, of which 1 were waited for; matrix products, arithmetic and copies ran while one was open for 0% of the time, Pallas kernels for 17%

profile of v6, /device:TPU:1, one launch (start us, length us, event | category | flops | bytes accessed | tf_op | source)
XLA Modules:
  0.0 92.8 jit_solution(17101093440846996199)
XLA Ops:
  0.6 4.3 %own_rows.1 = (bf16[16,1664]{1,0:T(8,128)(2,1)}, s32[18]{0:T(128)}) custom-call(s32[1]{0:T(128)} %bitcast.dev_ref, s32[256]{0:T(256)} %piv_s.1, s32[2,128]{1,0:T(2,128)} %bitcast.13, s32[56,128]{1,0:T(8,128)} %bitcast.8, bf16[7168,1024]{1,0:T(8,128)(2,1)} %emb_hbm.7, bf16[7168,512]{1,0:T(8,128)(2,1)} %fac_hbm.7), custom_call_target="tpu_custom_call" | custom-call | tf_op jit(solution)/shard_map/own_rows/pallas_call | solution.py:452
  4.9 0.8 reshape.34
  5.8 11.3 %all_to_all.10 = bf16[8,2,1664]{2,1,0:T(2,128)(2,1)S(1)} all-to-all(bf16[8,2,1664]{2,1,0:T(2,128)(2,1)S(1)} %reshape.34), channel_id=1, replica_groups=mesh['rows'=8,'cols'=16] {'rows'}, dimensions={0} | all-to-all | bytes 106496 | tf_op jit(solution)/shard_map/all_to_all | solution.py:465
  17.1 2.6 %collective-permute-start.2 = (bf16[16,1664]{1,0:T(8,128)(2,1)S(1)}, bf16[16,1664]{1,0:T(8,128)(2,1)S(1)}, u32[]{:S(2)}, u32[]{:S(2)}) collective-permute-start(bf16[16,1664]{1,0:T(8,128)(2,1)S(1)} %reshape.35.refs_0_), channel_id=1, source_target_pairs={{0,12},{1,13},{2,14},{3,15},{4,8},{5,9},{6,10},{7,11},{8,4},{9,5},... | collective-permute-start | bytes 159752 | tf_op jit(solution)/shard_map/ppermute | solution.py:428
  19.8 0.6 collective-permute-start.1
  20.3 0.1 collective-permute-start
  20.5 5.4 %row_norms.3.refs_0_ = f32[7168,128]{1,0:T(8,128)} custom-call(s32[56,128]{1,0:T(8,128)} %bitcast.9, bf16[7168,1024]{1,0:T(8,128)(2,1)} %emb_hbm.7, bf16[7168,512]{1,0:T(8,128)(2,1)} %fac_hbm.7), custom_call_target="tpu_custom_call" | custom-call | flops 15728640 | bytes 7864320 | tf_op jit(solution)/shard_map/row_norms/pallas_call | solution.py:406
  25.9 0.0 collective-permute-done.2.refs_3_
  25.9 0.0 collective-permute-done.1.refs_2_
  25.9 0.0 collective-permute-done.refs_1_
  26.0 0.3 slots.1
  26.2 2.7 %collective-permute-start.5 = (bf16[32,1664]{1,0:T(8,128)(2,1)S(1)}, bf16[32,1664]{1,0:T(8,128)(2,1)S(1)}, u32[]{:S(2)}, u32[]{:S(2)}) collective-permute-start(bf16[32,1664]{1,0:T(8,128)(2,1)S(1)} %slots.1), channel_id=1, source_target_pairs={{0,3},{1,2},{2,1},{3,0},{4,7},{5,6},{6,5},{7,4},{8,11},{9,10},{10,... | collective-permute-start | bytes 319496 | tf_op jit(solution)/shard_map/ppermute | solution.py:428
  29.0 0.5 collective-permute-start.4
  29.4 0.2 collective-permute-start.3
  29.6 5.4 %row_norms.4.refs_0_ = f32[7168,128]{1,0:T(8,128)} custom-call(s32[56,128]{1,0:T(8,128)} %bitcast.10, bf16[7168,1024]{1,0:T(8,128)(2,1)} %emb_hbm.7, bf16[7168,512]{1,0:T(8,128)(2,1)} %fac_hbm.7, f32[7168,128]{1,0:T(8,128)} %row_norms.3.refs_0_), custom_call_target="tpu_custom_call", output_to_operand_aliasing={{}: (3, {})} | custom-call | flops 15728640 | bytes 7864320 | tf_op jit(solution)/shard_map/row_norms/pallas_call | solution.py:406
  35.1 0.0 collective-permute-done.5
  35.1 0.0 collective-permute-done.4
  35.1 0.0 collective-permute-done.3
  35.1 1.0 %collective-permute-start.8 = (bf16[32,1664]{1,0:T(8,128)(2,1)S(1)}, bf16[32,1664]{1,0:T(8,128)(2,1)S(1)}, u32[]{:S(2)}, u32[]{:S(2)}) collective-permute-start(bf16[32,1664]{1,0:T(8,128)(2,1)S(1)} %add_add_fusion), channel_id=1, source_target_pairs={{0,96},{16,112},{32,64},{48,80},{64,32},{80,48},{96,0},{112,16},{1... | collective-permute-start | bytes 319496 | tf_op jit(solution)/shard_map/ppermute | solution.py:428
  36.1 1.2 %collective-permute-start.7 = (bf16[32,1664]{1,0:T(8,128)(2,1)S(1)}, bf16[32,1664]{1,0:T(8,128)(2,1)S(1)}, u32[]{:S(2)}, u32[]{:S(2)}) collective-permute-start(bf16[32,1664]{1,0:T(8,128)(2,1)S(1)} %add_add_fusion), channel_id=1, source_target_pairs={{0,64},{16,80},{32,96},{48,112},{64,0},{80,16},{96,32},{112,48},{1... | collective-permute-start | bytes 319496 | tf_op jit(solution)/shard_map/ppermute | solution.py:428
  37.3 1.2 %collective-permute-start.6 = (bf16[32,1664]{1,0:T(8,128)(2,1)S(1)}, bf16[32,1664]{1,0:T(8,128)(2,1)S(1)}, u32[]{:S(2)}, u32[]{:S(2)}) collective-permute-start(bf16[32,1664]{1,0:T(8,128)(2,1)S(1)} %add_add_fusion), channel_id=1, source_target_pairs={{0,32},{16,48},{32,0},{48,16},{64,96},{80,112},{96,64},{112,80},{1... | collective-permute-start | bytes 319496 | tf_op jit(solution)/shard_map/ppermute | solution.py:428
  38.5 4.9 %row_norms.5.aux_hbm = f32[7168,128]{1,0:T(8,128)} custom-call(s32[56,128]{1,0:T(8,128)} %bitcast.11, bf16[7168,1024]{1,0:T(8,128)(2,1)} %emb_hbm.7, bf16[7168,512]{1,0:T(8,128)(2,1)} %fac_hbm.7, f32[7168,128]{1,0:T(8,128)} %row_norms.4.refs_0_), custom_call_target="tpu_custom_call", output_to_operand_aliasing={{}: (3, {})} | custom-call | flops 12582912 | bytes 6291456 | tf_op jit(solution)/shard_map/row_norms/pallas_call | solution.py:406
  43.4 0.0 collective-permute-done.8
  43.4 0.0 collective-permute-done.7
  43.4 0.0 collective-permute-done.6
  43.5 0.0 copy-start
  43.5 3.3 %collective-permute-start.9 = (bf16[128,1664]{1,0:T(8,128)(2,1)S(1)}, bf16[128,1664]{1,0:T(8,128)(2,1)S(1)}, u32[]{:S(2)}, u32[]{:S(2)}) collective-permute-start(bf16[128,1664]{1,0:T(8,128)(2,1)S(1)} %constant_dynamic-update-slice_fusion.one_ref), channel_id=1, source_target_pairs={{0,16},{16,0},{32,48},{48,32},{64,80},{80,64},{96,112},{112,96},{1... | collective-permute-start | bytes 1277960 | tf_op jit(solution)/shard_map/ppermute | solution.py:488
  46.8 1.4 %collective-permute-done.9.two_ref = bf16[128,1664]{1,0:T(8,128)(2,1)S(1)} collective-permute-done((bf16[128,1664]{1,0:T(8,128)(2,1)S(1)}, bf16[128,1664]{1,0:T(8,128)(2,1)S(1)}, u32[]{:S(2)}, u32[]{:S(2)}) %collective-permute-start.9) | collective-permute-done | bytes 426016 | tf_op jit(solution)/shard_map/ppermute | solution.py:488
  48.2 0.8 copy-done.1
  48.9 26.0 %panel_factor.1 = (bf16[7168,256]{1,0:T(8,128)(2,1)}, f32[56,128]{1,0:T(8,128)}, f32[128,128]{1,0:T(8,128)}) custom-call(s32[18]{0:T(128)} %get-tuple-element.29.loc_ref, bf16[128,1664]{1,0:T(8,128)(2,1)} %copy-done, bf16[128,1664]{1,0:T(8,128)(2,1)} %copy-done.1, f32[7168,128]{1,0:T(8,128)} %row_norms.5.aux_hbm, bf16[7168,1024]{1,0:T(8,128)(2,1)} %emb_hbm.7, ...), custom_call_target="tpu_custom_call" | custom-call | tf_op jit(solution)/shard_map/panel_factor/pallas_call | solution.py:367
  74.9 17.1 %all_to_all.11 = f32[128,1,128]{2,1,0:T(1,128)S(1)} all-to-all(f32[128,1,128]{2,1,0:T(1,128)} %bitcast.12), channel_id=1, replica_groups=mesh['rows'=8,'cols'=16] {'rows','cols'}, dimensions={0} | all-to-all | bytes 131072 | tf_op jit(solution)/shard_map/all_to_all | solution.py:491
  92.1 0.7 reduce_max.9
  (8 shorter events, 0.1 us)
Async XLA Ops:
  17.1 8.8 %collective-permute-start.2 = (bf16[16,1664]{1,0:T(8,128)(2,1)S(1)}, bf16[16,1664]{1,0:T(8,128)(2,1)S(1)}, u32[]{:S(2)}, u32[]{:S(2)}) collective-permute-start(bf16[16,1664]{1,0:T(8,128)(2,1)S(1)} %reshape.35.refs_0_), channel_id=1, source_target_pairs={{0,12},{1,13},{2,14},{3,15},{4,8},{5,9},{6,10},{7,11},{8,4},{9,5},... | collective-permute-start | bytes 159752 | tf_op jit(solution)/shard_map/ppermute | solution.py:428
  19.8 6.2 %collective-permute-start.1 = (bf16[16,1664]{1,0:T(8,128)(2,1)S(1)}, bf16[16,1664]{1,0:T(8,128)(2,1)S(1)}, u32[]{:S(2)}, u32[]{:S(2)}) collective-permute-start(bf16[16,1664]{1,0:T(8,128)(2,1)S(1)} %reshape.35.refs_0_), channel_id=1, source_target_pairs={{0,8},{1,9},{2,10},{3,11},{4,12},{5,13},{6,14},{7,15},{8,0},{9,1},... | collective-permute-start | bytes 159752 | tf_op jit(solution)/shard_map/ppermute | solution.py:428
  20.3 5.6 %collective-permute-start = (bf16[16,1664]{1,0:T(8,128)(2,1)S(1)}, bf16[16,1664]{1,0:T(8,128)(2,1)S(1)}, u32[]{:S(2)}, u32[]{:S(2)}) collective-permute-start(bf16[16,1664]{1,0:T(8,128)(2,1)S(1)} %reshape.35.refs_0_), channel_id=1, source_target_pairs={{0,4},{1,5},{2,6},{3,7},{4,0},{5,1},{6,2},{7,3},{8,12},{9,13},{10,... | collective-permute-start | bytes 159752 | tf_op jit(solution)/shard_map/ppermute | solution.py:428
  26.2 8.8 %collective-permute-start.5 = (bf16[32,1664]{1,0:T(8,128)(2,1)S(1)}, bf16[32,1664]{1,0:T(8,128)(2,1)S(1)}, u32[]{:S(2)}, u32[]{:S(2)}) collective-permute-start(bf16[32,1664]{1,0:T(8,128)(2,1)S(1)} %slots.1), channel_id=1, source_target_pairs={{0,3},{1,2},{2,1},{3,0},{4,7},{5,6},{6,5},{7,4},{8,11},{9,10},{10,... | collective-permute-start | bytes 319496 | tf_op jit(solution)/shard_map/ppermute | solution.py:428
  29.0 6.1 %collective-permute-start.4 = (bf16[32,1664]{1,0:T(8,128)(2,1)S(1)}, bf16[32,1664]{1,0:T(8,128)(2,1)S(1)}, u32[]{:S(2)}, u32[]{:S(2)}) collective-permute-start(bf16[32,1664]{1,0:T(8,128)(2,1)S(1)} %slots.1), channel_id=1, source_target_pairs={{0,2},{1,3},{2,0},{3,1},{4,6},{5,7},{6,4},{7,5},{8,10},{9,11},{10,... | collective-permute-start | bytes 319496 | tf_op jit(solution)/shard_map/ppermute | solution.py:428
  29.4 5.6 %collective-permute-start.3 = (bf16[32,1664]{1,0:T(8,128)(2,1)S(1)}, bf16[32,1664]{1,0:T(8,128)(2,1)S(1)}, u32[]{:S(2)}, u32[]{:S(2)}) collective-permute-start(bf16[32,1664]{1,0:T(8,128)(2,1)S(1)} %slots.1), channel_id=1, source_target_pairs={{0,1},{1,0},{2,3},{3,2},{4,5},{5,4},{6,7},{7,6},{8,9},{9,8},{10,11... | collective-permute-start | bytes 319496 | tf_op jit(solution)/shard_map/ppermute | solution.py:428
  35.1 8.2 %collective-permute-start.8 = (bf16[32,1664]{1,0:T(8,128)(2,1)S(1)}, bf16[32,1664]{1,0:T(8,128)(2,1)S(1)}, u32[]{:S(2)}, u32[]{:S(2)}) collective-permute-start(bf16[32,1664]{1,0:T(8,128)(2,1)S(1)} %add_add_fusion), channel_id=1, source_target_pairs={{0,96},{16,112},{32,64},{48,80},{64,32},{80,48},{96,0},{112,16},{1... | collective-permute-start | bytes 319496 | tf_op jit(solution)/shard_map/ppermute | solution.py:428
  36.1 7.3 %collective-permute-start.7 = (bf16[32,1664]{1,0:T(8,128)(2,1)S(1)}, bf16[32,1664]{1,0:T(8,128)(2,1)S(1)}, u32[]{:S(2)}, u32[]{:S(2)}) collective-permute-start(bf16[32,1664]{1,0:T(8,128)(2,1)S(1)} %add_add_fusion), channel_id=1, source_target_pairs={{0,64},{16,80},{32,96},{48,112},{64,0},{80,16},{96,32},{112,48},{1... | collective-permute-start | bytes 319496 | tf_op jit(solution)/shard_map/ppermute | solution.py:428
  37.3 6.1 %collective-permute-start.6 = (bf16[32,1664]{1,0:T(8,128)(2,1)S(1)}, bf16[32,1664]{1,0:T(8,128)(2,1)S(1)}, u32[]{:S(2)}, u32[]{:S(2)}) collective-permute-start(bf16[32,1664]{1,0:T(8,128)(2,1)S(1)} %add_add_fusion), channel_id=1, source_target_pairs={{0,32},{16,48},{32,0},{48,16},{64,96},{80,112},{96,64},{112,80},{1... | collective-permute-start | bytes 319496 | tf_op jit(solution)/shard_map/ppermute | solution.py:428
  43.5 4.7 %copy-start = (bf16[128,1664]{1,0:T(8,128)(2,1)}, bf16[128,1664]{1,0:T(8,128)(2,1)S(1)}, u32[]{:S(2)}) copy-start(bf16[128,1664]{1,0:T(8,128)(2,1)S(1)} %constant_dynamic-update-slice_fusion.one_ref) | copy-start | bytes 1277956
  43.5 4.7 %collective-permute-start.9 = (bf16[128,1664]{1,0:T(8,128)(2,1)S(1)}, bf16[128,1664]{1,0:T(8,128)(2,1)S(1)}, u32[]{:S(2)}, u32[]{:S(2)}) collective-permute-start(bf16[128,1664]{1,0:T(8,128)(2,1)S(1)} %constant_dynamic-update-slice_fusion.one_ref), channel_id=1, source_target_pairs={{0,16},{16,0},{32,48},{48,32},{64,80},{80,64},{96,112},{112,96},{1... | collective-permute-start | bytes 1277960 | tf_op jit(solution)/shard_map/ppermute | solution.py:488
  48.2 0.8 copy-start.1

commit v7 on v6

--- a/solution.py
+++ b/solution.py
@@ -163,7 +163,7 @@
     return jnp.broadcast_to(x[k : k + 1, :], x.shape)
 
 
-def eliminate(w):
+def eliminate(w, between):
     rows, width = w.shape
     groups = [
         [w[8 * g : 8 * g + 8, 128 * v : 128 * v + 128] for v in range(width // 128)]
@@ -213,13 +213,14 @@
                     c = c + below[g][k] * inv[j][k]
                 groups[g] = [x - c * sublanes(o, j) for x, o in zip(groups[g], out)]
         done.append(jnp.concatenate(out, axis=1))
+        between(t)
     return jnp.concatenate(done, axis=0)
 
 
 def main_kernel(
     loc_ref, one_ref, two_ref, aux_hbm, emb_hbm, fac_hbm,
     out_hbm, gains_ref, best_ref,
-    piv, pvec, ar, minv, mt, panel, aux_ref, emb_ref, fac_ref, out_ref, sem, out_sem,
+    piv, pvec, ar, minv, mt, panel, aux_ref, emb_ref, fac_ref, out_ref, raw_a, raw_b, sem, out_sem,
 ):
     rows_here, dim = emb_ref.shape
     tile = rows_here // TILES
@@ -272,7 +273,7 @@
     def step(i, carry):
         for c in fetch(i):
             c.wait()
-        for c in range(SUB):
+        def part_of_panel(c):
             w = pl.ds(pl.multiple_of(i * tile + sub * c, 16), sub)
             a = aux_ref[w, 1:2]
             q = aux_ref[w, 2:3]
@@ -291,7 +292,7 @@
         rows = pl.ds(pl.multiple_of(i * BS, BS), BS)
         shift = lax.rem(n - i * BS, n)
         a = pltpu.roll(ar[rows, 0:n], shift, 1)
-        w = eliminate(jnp.concatenate([a, ar[rows, n : 2 * n]], axis=1))
+        w = eliminate(jnp.concatenate([a, ar[rows, n : 2 * n]], axis=1), part_of_panel)
         u = pltpu.roll(w[:, 0:n], i * BS, 1)
         m = w[:, n : 2 * n]
         minv[rows, :] = m
@@ -330,28 +331,47 @@
         w = pl.ds(pl.multiple_of(t * tile, tile), tile)
         return pltpu.make_async_copy(out_ref.at[w, :], out_hbm.at[w, :], out_sem.at[t])
 
-    def solve(t, carry):
-        gs = []
-        part = tile // SOLVE_SUB
+    part = tile // SOLVE_SUB
+    ey = iota((128, 128), 0) == iota((128, 128), 1)
+
+    def product(t, raw):
         for c in range(SOLVE_SUB):
             w = pl.ds(pl.multiple_of(t * tile + part * c, 16), part)
             both = jnp.concatenate([panel[w, :], panel[w, 0:n]], axis=1)
-            full = jnp.dot(both, mt[...], preferred_element_type=F32)
-            out_ref[w, :] = full.astype(BF16)
-            gs.append(aux_ref[w, 0:1] - jnp.sum(full * full, axis=1, keepdims=True))
-        g = jnp.concatenate(gs, axis=0)
-        ey = iota((128, 128), 0) == iota((128, 128), 1)
+            raw[part * c : part * c + part, :] = jnp.dot(
+                both, mt[...], preferred_element_type=F32
+            )
+
+    def finish(t, raw):
         lines = []
         for c in range(nchunk):
-            b = jnp.broadcast_to(g[128 * c : 128 * c + 128, :], (128, 128))
+            full = raw[128 * c : 128 * c + 128, :]
+            w = pl.ds(pl.multiple_of(t * tile + 128 * c, 128), 128)
+            out_ref[w, :] = full.astype(BF16)
+            g = aux_ref[w, 0:1] - jnp.sum(full * full, axis=1, keepdims=True)
+            b = jnp.broadcast_to(g, (128, 128))
             lines.append(jnp.sum(jnp.where(ey, b, 0.0), axis=0, keepdims=True))
         lines = jnp.concatenate(lines, axis=0)
         gains_ref[pl.ds(t * nchunk, nchunk), :] = lines
-        best_ref[...] = jnp.maximum(best_ref[...], jnp.max(lines))
-        store(t).start()
+        best_ref[...] = jnp.maximum(best_ref[...], jnp.max(lines, axis=0, keepdims=True))
+
+    product(0, raw_a)
+
+    def solve(t, carry):
+        product(2 * t + 1, raw_b)
+        finish(2 * t, raw_a)
+        product(2 * t + 2, raw_a)
+        finish(2 * t + 1, raw_b)
+        store(2 * t).start()
+        store(2 * t + 1).start()
         return carry
 
-    lax.fori_loop(0, TILES, solve, 0)
+    lax.fori_loop(0, TILES // 2 - 1, solve, 0)
+    product(TILES - 1, raw_b)
+    finish(TILES - 2, raw_a)
+    store(TILES - 2).start()
+    finish(TILES - 1, raw_b)
+    store(TILES - 1).start()
     for t in range(TILES):
         store(t).wait()
 
@@ -384,6 +404,8 @@
             pltpu.VMEM((rows_here, dim), BF16),
             pltpu.VMEM((rows_here, k0), BF16),
             pltpu.VMEM((rows_here, total), BF16),
+            pltpu.VMEM((tile, total), F32),
+            pltpu.VMEM((tile, total), F32),
             pltpu.SemaphoreType.DMA((3, TILES)),
             pltpu.SemaphoreType.DMA((TILES,)),
         ],

time: 93.5 us -> 90 us (0.963)
  Pallas kernels: 46.3 us -> 42.8 us
    pallas_call x1, Pallas kernels: 26 us -> 22.4 us  [main_call(): pl.pallas_call(main_kernel, out_shape=(jax.ShapeDtypeStruct((rows_here, t...]
  transfers between devices with their start and end apart: 10 -> 10, of which waited for: 1 -> 1; matrix products, arithmetic and copies ran while one was open for 0% -> 0% of each run, Pallas kernels for 17% -> 18%
where the time goes in v7:
time: 90 us; the launch traced here: 89.3 us
  Pallas kernels  42.8 us (48%)
  blocking collectives  28.5 us (32%)
  starting transfers between devices  13.4 us (15%)
  local copies, waits for them, and re-layouts  1.68 us (2%)
  waiting for transfers between devices  1.42 us (2%)
    pallas_call x1, Pallas kernels, main_call(): pl.pallas_call(main_kernel, out_shape=(jax.ShapeDtypeStruct((rows_here, t...  22.4 us
    all_to_all x1, blocking collectives, body(): peers = lax.all_to_all(best.reshape(NDEV, 1, 128), AXES, 0, 0)  17 us
    pallas_call x3, Pallas kernels, norms_part(): pl.pallas_call(functools.partial(norms_kernel, first), out_shape=jax.Shap...  15.7 us
    all_to_all x1, blocking collectives, body(): lax.all_to_all(send.reshape(CLASSES, 2, width), 'rows', 0, 0)  11.5 us
    ppermute x9, starting transfers between devices, ring(): return [lax.ppermute(v, axis, p) for v, p in zip(values, pairs)]  10.1 us
    pallas_call x1, Pallas kernels, body(): pl.pallas_call(own_kernel, out_shape=(wide(16), jax.ShapeDtypeStruct((2 +...  4.3 us
    ppermute x1, starting transfers between devices, body(): two = lax.ppermute(one, 'rows', swap)  3.25 us
  transfers between devices with their start and end apart: 10, of which 1 were waited for; matrix products, arithmetic and copies ran while one was open for 0% of the time, Pallas kernels for 18%

profile of v7, /device:TPU:1, one launch (start us, length us, event | category | flops | bytes accessed | tf_op | source)
XLA Modules:
  0.0 89.3 jit_solution(15699506475339926840)
XLA Ops:
  0.6 4.3 %own_rows.1 = (bf16[16,1664]{1,0:T(8,128)(2,1)}, s32[18]{0:T(128)}) custom-call(s32[1]{0:T(128)} %bitcast.dev_ref, s32[256]{0:T(256)} %piv_s.1, s32[2,128]{1,0:T(2,128)} %bitcast.13, s32[56,128]{1,0:T(8,128)} %bitcast.8, bf16[7168,1024]{1,0:T(8,128)(2,1)} %emb_hbm.7, bf16[7168,512]{1,0:T(8,128)(2,1)} %fac_hbm.7), custom_call_target="tpu_custom_call" | custom-call | tf_op jit(solution)/shard_map/own_rows/pallas_call | solution.py:474
  4.9 0.8 reshape.34
  5.8 11.5 %all_to_all.10 = bf16[8,2,1664]{2,1,0:T(2,128)(2,1)S(1)} all-to-all(bf16[8,2,1664]{2,1,0:T(2,128)(2,1)S(1)} %reshape.34), channel_id=1, replica_groups=mesh['rows'=8,'cols'=16] {'rows'}, dimensions={0} | all-to-all | bytes 106496 | tf_op jit(solution)/shard_map/all_to_all | solution.py:487
  17.3 2.4 %collective-permute-start.2 = (bf16[16,1664]{1,0:T(8,128)(2,1)S(1)}, bf16[16,1664]{1,0:T(8,128)(2,1)S(1)}, u32[]{:S(2)}, u32[]{:S(2)}) collective-permute-start(bf16[16,1664]{1,0:T(8,128)(2,1)S(1)} %reshape.35.refs_0_), channel_id=1, source_target_pairs={{0,12},{1,13},{2,14},{3,15},{4,8},{5,9},{6,10},{7,11},{8,4},{9,5},... | collective-permute-start | bytes 159752 | tf_op jit(solution)/shard_map/ppermute | solution.py:450
  19.7 0.5 collective-permute-start.1
  20.2 0.4 collective-permute-start
  20.6 5.4 %row_norms.3.refs_0_ = f32[7168,128]{1,0:T(8,128)} custom-call(s32[56,128]{1,0:T(8,128)} %bitcast.9, bf16[7168,1024]{1,0:T(8,128)(2,1)} %emb_hbm.7, bf16[7168,512]{1,0:T(8,128)(2,1)} %fac_hbm.7), custom_call_target="tpu_custom_call" | custom-call | flops 15728640 | bytes 7864320 | tf_op jit(solution)/shard_map/row_norms/pallas_call | solution.py:428
  26.0 0.0 collective-permute-done.2.refs_3_
  26.1 0.0 collective-permute-done.1.refs_2_
  26.1 0.0 collective-permute-done.refs_1_
  26.1 0.3 slots.1
  26.4 2.8 %collective-permute-start.5 = (bf16[32,1664]{1,0:T(8,128)(2,1)S(1)}, bf16[32,1664]{1,0:T(8,128)(2,1)S(1)}, u32[]{:S(2)}, u32[]{:S(2)}) collective-permute-start(bf16[32,1664]{1,0:T(8,128)(2,1)S(1)} %slots.1), channel_id=1, source_target_pairs={{0,3},{1,2},{2,1},{3,0},{4,7},{5,6},{6,5},{7,4},{8,11},{9,10},{10,... | collective-permute-start | bytes 319496 | tf_op jit(solution)/shard_map/ppermute | solution.py:450
  29.1 0.3 collective-permute-start.4
  29.5 0.3 collective-permute-start.3
  29.8 5.4 %row_norms.4.refs_0_ = f32[7168,128]{1,0:T(8,128)} custom-call(s32[56,128]{1,0:T(8,128)} %bitcast.10, bf16[7168,1024]{1,0:T(8,128)(2,1)} %emb_hbm.7, bf16[7168,512]{1,0:T(8,128)(2,1)} %fac_hbm.7, f32[7168,128]{1,0:T(8,128)} %row_norms.3.refs_0_), custom_call_target="tpu_custom_call", output_to_operand_aliasing={{}: (3, {})} | custom-call | flops 15728640 | bytes 7864320 | tf_op jit(solution)/shard_map/row_norms/pallas_call | solution.py:428
  35.2 0.0 collective-permute-done.5
  35.3 0.0 collective-permute-done.4
  35.3 0.0 collective-permute-done.3
  35.3 1.0 %collective-permute-start.8 = (bf16[32,1664]{1,0:T(8,128)(2,1)S(1)}, bf16[32,1664]{1,0:T(8,128)(2,1)S(1)}, u32[]{:S(2)}, u32[]{:S(2)}) collective-permute-start(bf16[32,1664]{1,0:T(8,128)(2,1)S(1)} %add_add_fusion), channel_id=1, source_target_pairs={{0,96},{16,112},{32,64},{48,80},{64,32},{80,48},{96,0},{112,16},{1... | collective-permute-start | bytes 319496 | tf_op jit(solution)/shard_map/ppermute | solution.py:450
  36.3 1.2 %collective-permute-start.7 = (bf16[32,1664]{1,0:T(8,128)(2,1)S(1)}, bf16[32,1664]{1,0:T(8,128)(2,1)S(1)}, u32[]{:S(2)}, u32[]{:S(2)}) collective-permute-start(bf16[32,1664]{1,0:T(8,128)(2,1)S(1)} %add_add_fusion), channel_id=1, source_target_pairs={{0,64},{16,80},{32,96},{48,112},{64,0},{80,16},{96,32},{112,48},{1... | collective-permute-start | bytes 319496 | tf_op jit(solution)/shard_map/ppermute | solution.py:450
  37.5 1.2 %collective-permute-start.6 = (bf16[32,1664]{1,0:T(8,128)(2,1)S(1)}, bf16[32,1664]{1,0:T(8,128)(2,1)S(1)}, u32[]{:S(2)}, u32[]{:S(2)}) collective-permute-start(bf16[32,1664]{1,0:T(8,128)(2,1)S(1)} %add_add_fusion), channel_id=1, source_target_pairs={{0,32},{16,48},{32,0},{48,16},{64,96},{80,112},{96,64},{112,80},{1... | collective-permute-start | bytes 319496 | tf_op jit(solution)/shard_map/ppermute | solution.py:450
  38.6 4.9 %row_norms.5.aux_hbm = f32[7168,128]{1,0:T(8,128)} custom-call(s32[56,128]{1,0:T(8,128)} %bitcast.11, bf16[7168,1024]{1,0:T(8,128)(2,1)} %emb_hbm.7, bf16[7168,512]{1,0:T(8,128)(2,1)} %fac_hbm.7, f32[7168,128]{1,0:T(8,128)} %row_norms.4.refs_0_), custom_call_target="tpu_custom_call", output_to_operand_aliasing={{}: (3, {})} | custom-call | flops 12582912 | bytes 6291456 | tf_op jit(solution)/shard_map/row_norms/pallas_call | solution.py:428
  43.5 0.0 collective-permute-done.8
  43.5 0.0 collective-permute-done.7
  43.6 0.0 collective-permute-done.6
  43.6 0.0 copy-start
  43.7 3.3 %collective-permute-start.9 = (bf16[128,1664]{1,0:T(8,128)(2,1)S(1)}, bf16[128,1664]{1,0:T(8,128)(2,1)S(1)}, u32[]{:S(2)}, u32[]{:S(2)}) collective-permute-start(bf16[128,1664]{1,0:T(8,128)(2,1)S(1)} %constant_dynamic-update-slice_fusion.one_ref), channel_id=1, source_target_pairs={{0,16},{16,0},{32,48},{48,32},{64,80},{80,64},{96,112},{112,96},{1... | collective-permute-start | bytes 1277960 | tf_op jit(solution)/shard_map/ppermute | solution.py:510
  46.9 1.4 %collective-permute-done.9.two_ref = bf16[128,1664]{1,0:T(8,128)(2,1)S(1)} collective-permute-done((bf16[128,1664]{1,0:T(8,128)(2,1)S(1)}, bf16[128,1664]{1,0:T(8,128)(2,1)S(1)}, u32[]{:S(2)}, u32[]{:S(2)}) %collective-permute-start.9) | collective-permute-done | bytes 426016 | tf_op jit(solution)/shard_map/ppermute | solution.py:510
  48.3 0.8 copy-done.1
  49.1 22.4 %panel_factor.1 = (bf16[7168,256]{1,0:T(8,128)(2,1)}, f32[56,128]{1,0:T(8,128)}, f32[128,128]{1,0:T(8,128)}) custom-call(s32[18]{0:T(128)} %get-tuple-element.29.loc_ref, bf16[128,1664]{1,0:T(8,128)(2,1)} %copy-done, bf16[128,1664]{1,0:T(8,128)(2,1)} %copy-done.1, f32[7168,128]{1,0:T(8,128)} %row_norms.5.aux_hbm, bf16[7168,1024]{1,0:T(8,128)(2,1)} %emb_hbm.7, ...), custom_call_target="tpu_custom_call" | custom-call | tf_op jit(solution)/shard_map/panel_factor/pallas_call | solution.py:387
  71.5 17.0 %all_to_all.11 = f32[128,1,128]{2,1,0:T(1,128)S(1)} all-to-all(f32[128,1,128]{2,1,0:T(1,128)} %bitcast.12), channel_id=1, replica_groups=mesh['rows'=8,'cols'=16] {'rows','cols'}, dimensions={0} | all-to-all | bytes 131072 | tf_op jit(solution)/shard_map/all_to_all | solution.py:513
  88.5 0.7 reduce_max.9
  (8 shorter events, 0.1 us)
Async XLA Ops:
  17.3 8.8 %collective-permute-start.2 = (bf16[16,1664]{1,0:T(8,128)(2,1)S(1)}, bf16[16,1664]{1,0:T(8,128)(2,1)S(1)}, u32[]{:S(2)}, u32[]{:S(2)}) collective-permute-start(bf16[16,1664]{1,0:T(8,128)(2,1)S(1)} %reshape.35.refs_0_), channel_id=1, source_target_pairs={{0,12},{1,13},{2,14},{3,15},{4,8},{5,9},{6,10},{7,11},{8,4},{9,5},... | collective-permute-start | bytes 159752 | tf_op jit(solution)/shard_map/ppermute | solution.py:450
  19.7 6.4 %collective-permute-start.1 = (bf16[16,1664]{1,0:T(8,128)(2,1)S(1)}, bf16[16,1664]{1,0:T(8,128)(2,1)S(1)}, u32[]{:S(2)}, u32[]{:S(2)}) collective-permute-start(bf16[16,1664]{1,0:T(8,128)(2,1)S(1)} %reshape.35.refs_0_), channel_id=1, source_target_pairs={{0,8},{1,9},{2,10},{3,11},{4,12},{5,13},{6,14},{7,15},{8,0},{9,1},... | collective-permute-start | bytes 159752 | tf_op jit(solution)/shard_map/ppermute | solution.py:450
  20.2 5.8 %collective-permute-start = (bf16[16,1664]{1,0:T(8,128)(2,1)S(1)}, bf16[16,1664]{1,0:T(8,128)(2,1)S(1)}, u32[]{:S(2)}, u32[]{:S(2)}) collective-permute-start(bf16[16,1664]{1,0:T(8,128)(2,1)S(1)} %reshape.35.refs_0_), channel_id=1, source_target_pairs={{0,4},{1,5},{2,6},{3,7},{4,0},{5,1},{6,2},{7,3},{8,12},{9,13},{10,... | collective-permute-start | bytes 159752 | tf_op jit(solution)/shard_map/ppermute | solution.py:450
  26.4 8.9 %collective-permute-start.5 = (bf16[32,1664]{1,0:T(8,128)(2,1)S(1)}, bf16[32,1664]{1,0:T(8,128)(2,1)S(1)}, u32[]{:S(2)}, u32[]{:S(2)}) collective-permute-start(bf16[32,1664]{1,0:T(8,128)(2,1)S(1)} %slots.1), channel_id=1, source_target_pairs={{0,3},{1,2},{2,1},{3,0},{4,7},{5,6},{6,5},{7,4},{8,11},{9,10},{10,... | collective-permute-start | bytes 319496 | tf_op jit(solution)/shard_map/ppermute | solution.py:450
  29.1 6.1 %collective-permute-start.4 = (bf16[32,1664]{1,0:T(8,128)(2,1)S(1)}, bf16[32,1664]{1,0:T(8,128)(2,1)S(1)}, u32[]{:S(2)}, u32[]{:S(2)}) collective-permute-start(bf16[32,1664]{1,0:T(8,128)(2,1)S(1)} %slots.1), channel_id=1, source_target_pairs={{0,2},{1,3},{2,0},{3,1},{4,6},{5,7},{6,4},{7,5},{8,10},{9,11},{10,... | collective-permute-start | bytes 319496 | tf_op jit(solution)/shard_map/ppermute | solution.py:450
  29.5 5.8 %collective-permute-start.3 = (bf16[32,1664]{1,0:T(8,128)(2,1)S(1)}, bf16[32,1664]{1,0:T(8,128)(2,1)S(1)}, u32[]{:S(2)}, u32[]{:S(2)}) collective-permute-start(bf16[32,1664]{1,0:T(8,128)(2,1)S(1)} %slots.1), channel_id=1, source_target_pairs={{0,1},{1,0},{2,3},{3,2},{4,5},{5,4},{6,7},{7,6},{8,9},{9,8},{10,11... | collective-permute-start | bytes 319496 | tf_op jit(solution)/shard_map/ppermute | solution.py:450
  35.3 8.2 %collective-permute-start.8 = (bf16[32,1664]{1,0:T(8,128)(2,1)S(1)}, bf16[32,1664]{1,0:T(8,128)(2,1)S(1)}, u32[]{:S(2)}, u32[]{:S(2)}) collective-permute-start(bf16[32,1664]{1,0:T(8,128)(2,1)S(1)} %add_add_fusion), channel_id=1, source_target_pairs={{0,96},{16,112},{32,64},{48,80},{64,32},{80,48},{96,0},{112,16},{1... | collective-permute-start | bytes 319496 | tf_op jit(solution)/shard_map/ppermute | solution.py:450
  36.3 7.3 %collective-permute-start.7 = (bf16[32,1664]{1,0:T(8,128)(2,1)S(1)}, bf16[32,1664]{1,0:T(8,128)(2,1)S(1)}, u32[]{:S(2)}, u32[]{:S(2)}) collective-permute-start(bf16[32,1664]{1,0:T(8,128)(2,1)S(1)} %add_add_fusion), channel_id=1, source_target_pairs={{0,64},{16,80},{32,96},{48,112},{64,0},{80,16},{96,32},{112,48},{1... | collective-permute-start | bytes 319496 | tf_op jit(solution)/shard_map/ppermute | solution.py:450
  37.5 6.1 %collective-permute-start.6 = (bf16[32,1664]{1,0:T(8,128)(2,1)S(1)}, bf16[32,1664]{1,0:T(8,128)(2,1)S(1)}, u32[]{:S(2)}, u32[]{:S(2)}) collective-permute-start(bf16[32,1664]{1,0:T(8,128)(2,1)S(1)} %add_add_fusion), channel_id=1, source_target_pairs={{0,32},{16,48},{32,0},{48,16},{64,96},{80,112},{96,64},{112,80},{1... | collective-permute-start | bytes 319496 | tf_op jit(solution)/shard_map/ppermute | solution.py:450
  43.6 4.7 %copy-start = (bf16[128,1664]{1,0:T(8,128)(2,1)}, bf16[128,1664]{1,0:T(8,128)(2,1)S(1)}, u32[]{:S(2)}) copy-start(bf16[128,1664]{1,0:T(8,128)(2,1)S(1)} %constant_dynamic-update-slice_fusion.one_ref) | copy-start | bytes 1277956
  43.7 4.6 %collective-permute-start.9 = (bf16[128,1664]{1,0:T(8,128)(2,1)S(1)}, bf16[128,1664]{1,0:T(8,128)(2,1)S(1)}, u32[]{:S(2)}, u32[]{:S(2)}) collective-permute-start(bf16[128,1664]{1,0:T(8,128)(2,1)S(1)} %constant_dynamic-update-slice_fusion.one_ref), channel_id=1, source_target_pairs={{0,16},{16,0},{32,48},{48,32},{64,80},{80,64},{96,112},{112,96},{1... | collective-permute-start | bytes 1277960 | tf_op jit(solution)/shard_map/ppermute | solution.py:510
  48.3 0.8 copy-start.1

commit v8 on v7

--- a/solution.py
+++ b/solution.py
@@ -79,9 +79,11 @@
     hot = hot.astype(BF16)
     for c in copies:
         c.wait()
-    send_ref[:, 0:dim] = jnp.dot(hot, ebuf[...], preferred_element_type=F32).astype(BF16)
-    send_ref[:, dim : dim + k0] = jnp.dot(hot, fbuf[...], preferred_element_type=F32).astype(BF16)
-    send_ref[:, dim + k0 :] = tag.astype(BF16)
+    e = jnp.dot(hot, ebuf[...], preferred_element_type=F32)
+    f = jnp.dot(hot, fbuf[...], preferred_element_type=F32)
+    row = jnp.concatenate([e, f, tag], axis=1)
+    for k in range(CLASSES):
+        send_ref[k, :, :] = row[2 * k : 2 * k + 2, :].astype(BF16)
 
 
 def slots_kernel(cls_ref, *refs):
@@ -409,7 +411,7 @@
             pltpu.SemaphoreType.DMA((3, TILES)),
             pltpu.SemaphoreType.DMA((TILES,)),
         ],
-        compiler_params=pltpu.CompilerParams(vmem_limit_bytes=GRANT),
+        compiler_params=pltpu.CompilerParams(vmem_limit_bytes=50 << 20),
         name="panel_factor",
     )(loc, one, two, aux, embeddings, factor_cols)
 
@@ -473,7 +475,10 @@
 
     send, loc = pl.pallas_call(
         own_kernel,
-        out_shape=(wide(16), jax.ShapeDtypeStruct((2 + PMAX,), jnp.int32)),
+        out_shape=(
+            jax.ShapeDtypeStruct((CLASSES, 2, width), BF16),
+            jax.ShapeDtypeStruct((2 + PMAX,), jnp.int32),
+        ),
         in_specs=[smem, smem, vmem, smem, hbm, hbm],
         out_specs=(vmem, smem),
         scratch_shapes=[
@@ -484,7 +489,7 @@
         compiler_params=pltpu.CompilerParams(vmem_limit_bytes=GRANT),
         name="own_rows",
     )(dev, pivots, piv2, solved2, embeddings, factor_cols)
-    mine = lax.all_to_all(send.reshape(CLASSES, 2, width), "rows", 0, 0).reshape(16, width)
+    mine = lax.all_to_all(send, "rows", 0, 0).reshape(16, width)
     counts, mine = lax.optimization_barrier((solved2, mine))
     got = [mine] + ring([mine] * 3, "cols", xs)
     aux = norms_part(counts, embeddings, factor_cols, 0, 5, None)

time: 90 us -> 88 us (0.978)
  local copies, waits for them, and re-layouts: 1.68 us -> 0.09 us
where the time goes in v8:
time: 88 us; the launch traced here: 87.3 us
  Pallas kernels  42.5 us (48%)
  blocking collectives  28.4 us (32%)
  starting transfers between devices  13.4 us (15%)
  waiting for transfers between devices  1.42 us (2%)
    pallas_call x1, Pallas kernels, main_call(): pl.pallas_call(main_kernel, out_shape=(jax.ShapeDtypeStruct((rows_here, t...  22.2 us
    all_to_all x1, blocking collectives, body(): peers = lax.all_to_all(best.reshape(NDEV, 1, 128), AXES, 0, 0)  16.8 us
    pallas_call x3, Pallas kernels, norms_part(): pl.pallas_call(functools.partial(norms_kernel, first), out_shape=jax.Shap...  15.7 us
    all_to_all x1, blocking collectives, body(): mine = lax.all_to_all(send, 'rows', 0, 0).reshape(16, width)  11.6 us
    ppermute x9, starting transfers between devices, ring(): return [lax.ppermute(v, axis, p) for v, p in zip(values, pairs)]  10.2 us
    pallas_call x1, Pallas kernels, body(): pl.pallas_call(own_kernel, out_shape=(jax.ShapeDtypeStruct((CLASSES, 2, w...  4.29 us
    ppermute x1, starting transfers between devices, body(): two = lax.ppermute(one, 'rows', swap)  3.19 us
  transfers between devices with their start and end apart: 10, of which 1 were waited for; matrix products, arithmetic and copies ran while one was open for 0% of the time, Pallas kernels for 18%

profile of v8, /device:TPU:1, one launch (start us, length us, event | category | flops | bytes accessed | tf_op | source)
XLA Modules:
  0.0 87.3 jit_solution(2938624927556367288)
XLA Ops:
  0.6 4.3 %own_rows.1 = (bf16[8,2,1664]{2,1,0:T(2,128)(2,1)}, s32[18]{0:T(128)}) custom-call(s32[1]{0:T(128)} %bitcast.dev_ref, s32[256]{0:T(256)} %piv_s.1, s32[2,128]{1,0:T(2,128)} %bitcast.13, s32[56,128]{1,0:T(8,128)} %bitcast.9, bf16[7168,1024]{1,0:T(8,128)(2,1)} %emb_hbm.7, bf16[7168,512]{1,0:T(8,128)(2,1)} %fac_hbm.7), custom_call_target="tpu_custom_call" | custom-call | tf_op jit(solution)/shard_map/own_rows/pallas_call | solution.py:476
  4.9 11.6 %all_to_all.10 = bf16[8,2,1664]{2,1,0:T(2,128)(2,1)S(1)} all-to-all(bf16[8,2,1664]{2,1,0:T(2,128)(2,1)} %get-tuple-element.30), channel_id=1, replica_groups=mesh['rows'=8,'cols'=16] {'rows'}, dimensions={0} | all-to-all | bytes 106496 | tf_op jit(solution)/shard_map/all_to_all | solution.py:492
  16.5 2.6 %collective-permute-start.2 = (bf16[16,1664]{1,0:T(8,128)(2,1)S(1)}, bf16[16,1664]{1,0:T(8,128)(2,1)S(1)}, u32[]{:S(2)}, u32[]{:S(2)}) collective-permute-start(bf16[16,1664]{1,0:T(8,128)(2,1)S(1)} %reshape.31.refs_0_), channel_id=1, source_target_pairs={{0,12},{1,13},{2,14},{3,15},{4,8},{5,9},{6,10},{7,11},{8,4},{9,5},... | collective-permute-start | bytes 159752 | tf_op jit(solution)/shard_map/ppermute | solution.py:452
  19.1 0.6 collective-permute-start.1
  19.7 0.2 collective-permute-start
  19.8 5.4 %row_norms.3.refs_0_ = f32[7168,128]{1,0:T(8,128)} custom-call(s32[56,128]{1,0:T(8,128)} %bitcast.10, bf16[7168,1024]{1,0:T(8,128)(2,1)} %emb_hbm.7, bf16[7168,512]{1,0:T(8,128)(2,1)} %fac_hbm.7), custom_call_target="tpu_custom_call" | custom-call | flops 15728640 | bytes 7864320 | tf_op jit(solution)/shard_map/row_norms/pallas_call | solution.py:430
  25.3 0.0 collective-permute-done.2.refs_3_
  25.3 0.0 collective-permute-done.1.refs_2_
  25.3 0.0 collective-permute-done.refs_1_
  25.3 0.3 slots.1
  25.6 2.8 %collective-permute-start.5 = (bf16[32,1664]{1,0:T(8,128)(2,1)S(1)}, bf16[32,1664]{1,0:T(8,128)(2,1)S(1)}, u32[]{:S(2)}, u32[]{:S(2)}) collective-permute-start(bf16[32,1664]{1,0:T(8,128)(2,1)S(1)} %slots.1), channel_id=1, source_target_pairs={{0,3},{1,2},{2,1},{3,0},{4,7},{5,6},{6,5},{7,4},{8,11},{9,10},{10,... | collective-permute-start | bytes 319496 | tf_op jit(solution)/shard_map/ppermute | solution.py:452
  28.5 0.3 collective-permute-start.4
  28.7 0.4 collective-permute-start.3
  29.1 5.4 %row_norms.4.refs_0_ = f32[7168,128]{1,0:T(8,128)} custom-call(s32[56,128]{1,0:T(8,128)} %bitcast.11, bf16[7168,1024]{1,0:T(8,128)(2,1)} %emb_hbm.7, bf16[7168,512]{1,0:T(8,128)(2,1)} %fac_hbm.7, f32[7168,128]{1,0:T(8,128)} %row_norms.3.refs_0_), custom_call_target="tpu_custom_call", output_to_operand_aliasing={{}: (3, {})} | custom-call | flops 15728640 | bytes 7864320 | tf_op jit(solution)/shard_map/row_norms/pallas_call | solution.py:430
  34.6 0.0 collective-permute-done.5
  34.6 0.0 collective-permute-done.4
  34.6 0.0 collective-permute-done.3
  34.6 0.0 copy-start
  34.6 1.0 %collective-permute-start.8 = (bf16[32,1664]{1,0:T(8,128)(2,1)S(1)}, bf16[32,1664]{1,0:T(8,128)(2,1)S(1)}, u32[]{:S(2)}, u32[]{:S(2)}) collective-permute-start(bf16[32,1664]{1,0:T(8,128)(2,1)S(1)} %add_add_fusion), channel_id=1, source_target_pairs={{0,96},{16,112},{32,64},{48,80},{64,32},{80,48},{96,0},{112,16},{1... | collective-permute-start | bytes 319496 | tf_op jit(solution)/shard_map/ppermute | solution.py:452
  35.6 1.2 %collective-permute-start.7 = (bf16[32,1664]{1,0:T(8,128)(2,1)S(1)}, bf16[32,1664]{1,0:T(8,128)(2,1)S(1)}, u32[]{:S(2)}, u32[]{:S(2)}) collective-permute-start(bf16[32,1664]{1,0:T(8,128)(2,1)S(1)} %add_add_fusion), channel_id=1, source_target_pairs={{0,64},{16,80},{32,96},{48,112},{64,0},{80,16},{96,32},{112,48},{1... | collective-permute-start | bytes 319496 | tf_op jit(solution)/shard_map/ppermute | solution.py:452
  36.8 1.2 %collective-permute-start.6 = (bf16[32,1664]{1,0:T(8,128)(2,1)S(1)}, bf16[32,1664]{1,0:T(8,128)(2,1)S(1)}, u32[]{:S(2)}, u32[]{:S(2)}) collective-permute-start(bf16[32,1664]{1,0:T(8,128)(2,1)S(1)} %add_add_fusion), channel_id=1, source_target_pairs={{0,32},{16,48},{32,0},{48,16},{64,96},{80,112},{96,64},{112,80},{1... | collective-permute-start | bytes 319496 | tf_op jit(solution)/shard_map/ppermute | solution.py:452
  38.0 4.9 %row_norms.5.aux_hbm = f32[7168,128]{1,0:T(8,128)} custom-call(s32[56,128]{1,0:T(8,128)} %bitcast.12, bf16[7168,1024]{1,0:T(8,128)(2,1)} %emb_hbm.7, bf16[7168,512]{1,0:T(8,128)(2,1)} %fac_hbm.7, f32[7168,128]{1,0:T(8,128)} %row_norms.4.refs_0_), custom_call_target="tpu_custom_call", output_to_operand_aliasing={{}: (3, {})} | custom-call | flops 12582912 | bytes 6291456 | tf_op jit(solution)/shard_map/row_norms/pallas_call | solution.py:430
  42.9 0.0 collective-permute-done.8
  42.9 0.0 collective-permute-done.7
  42.9 0.0 collective-permute-done.6
  43.0 3.2 %collective-permute-start.9 = (bf16[128,1664]{1,0:T(8,128)(2,1)S(1)}, bf16[128,1664]{1,0:T(8,128)(2,1)S(1)}, u32[]{:S(2)}, u32[]{:S(2)}) collective-permute-start(bf16[128,1664]{1,0:T(8,128)(2,1)S(1)} %constant_dynamic-update-slice_fusion.one_ref), channel_id=1, source_target_pairs={{0,16},{16,0},{32,48},{48,32},{64,80},{80,64},{96,112},{112,96},{1... | collective-permute-start | bytes 1277960 | tf_op jit(solution)/shard_map/ppermute | solution.py:515
  46.2 1.4 %collective-permute-done.9.two_ref = bf16[128,1664]{1,0:T(8,128)(2,1)S(1)} collective-permute-done((bf16[128,1664]{1,0:T(8,128)(2,1)S(1)}, bf16[128,1664]{1,0:T(8,128)(2,1)S(1)}, u32[]{:S(2)}, u32[]{:S(2)}) %collective-permute-start.9) | collective-permute-done | bytes 426016 | tf_op jit(solution)/shard_map/ppermute | solution.py:515
  47.5 0.0 copy-done
  47.6 22.2 %panel_factor.1 = (bf16[7168,256]{1,0:T(8,128)(2,1)}, f32[56,128]{1,0:T(8,128)}, f32[128,128]{1,0:T(8,128)S(1)}) custom-call(s32[18]{0:T(128)S(1)} %copy-done, bf16[128,1664]{1,0:T(8,128)(2,1)S(1)} %constant_dynamic-update-slice_fusion.one_ref, bf16[128,1664]{1,0:T(8,128)(2,1)S(1)} %collective-permute-done.9.two_ref, f32[7168,128]{1,0:T(8,128)} %row_norms.5.aux_hbm, ...), custom_call_target="tpu_custom_call" | custom-call | tf_op jit(solution)/shard_map/panel_factor/pallas_call | solution.py:389
  69.8 16.8 %all_to_all.11 = f32[128,1,128]{2,1,0:T(1,128)S(1)} all-to-all(f32[128,1,128]{2,1,0:T(1,128)S(1)} %bitcast.8), channel_id=1, replica_groups=mesh['rows'=8,'cols'=16] {'rows','cols'}, dimensions={0} | all-to-all | bytes 131072 | tf_op jit(solution)/shard_map/all_to_all | solution.py:518
  86.6 0.7 reduce_max.9
  (6 shorter events, 0.1 us)
Async XLA Ops:
  16.5 8.8 %collective-permute-start.2 = (bf16[16,1664]{1,0:T(8,128)(2,1)S(1)}, bf16[16,1664]{1,0:T(8,128)(2,1)S(1)}, u32[]{:S(2)}, u32[]{:S(2)}) collective-permute-start(bf16[16,1664]{1,0:T(8,128)(2,1)S(1)} %reshape.31.refs_0_), channel_id=1, source_target_pairs={{0,12},{1,13},{2,14},{3,15},{4,8},{5,9},{6,10},{7,11},{8,4},{9,5},... | collective-permute-start | bytes 159752 | tf_op jit(solution)/shard_map/ppermute | solution.py:452
  19.1 6.2 %collective-permute-start.1 = (bf16[16,1664]{1,0:T(8,128)(2,1)S(1)}, bf16[16,1664]{1,0:T(8,128)(2,1)S(1)}, u32[]{:S(2)}, u32[]{:S(2)}) collective-permute-start(bf16[16,1664]{1,0:T(8,128)(2,1)S(1)} %reshape.31.refs_0_), channel_id=1, source_target_pairs={{0,8},{1,9},{2,10},{3,11},{4,12},{5,13},{6,14},{7,15},{8,0},{9,1},... | collective-permute-start | bytes 159752 | tf_op jit(solution)/shard_map/ppermute | solution.py:452
  19.7 5.7 %collective-permute-start = (bf16[16,1664]{1,0:T(8,128)(2,1)S(1)}, bf16[16,1664]{1,0:T(8,128)(2,1)S(1)}, u32[]{:S(2)}, u32[]{:S(2)}) collective-permute-start(bf16[16,1664]{1,0:T(8,128)(2,1)S(1)} %reshape.31.refs_0_), channel_id=1, source_target_pairs={{0,4},{1,5},{2,6},{3,7},{4,0},{5,1},{6,2},{7,3},{8,12},{9,13},{10,... | collective-permute-start | bytes 159752 | tf_op jit(solution)/shard_map/ppermute | solution.py:452
  25.6 9.0 %collective-permute-start.5 = (bf16[32,1664]{1,0:T(8,128)(2,1)S(1)}, bf16[32,1664]{1,0:T(8,128)(2,1)S(1)}, u32[]{:S(2)}, u32[]{:S(2)}) collective-permute-start(bf16[32,1664]{1,0:T(8,128)(2,1)S(1)} %slots.1), channel_id=1, source_target_pairs={{0,3},{1,2},{2,1},{3,0},{4,7},{5,6},{6,5},{7,4},{8,11},{9,10},{10,... | collective-permute-start | bytes 319496 | tf_op jit(solution)/shard_map/ppermute | solution.py:452
  28.5 6.1 %collective-permute-start.4 = (bf16[32,1664]{1,0:T(8,128)(2,1)S(1)}, bf16[32,1664]{1,0:T(8,128)(2,1)S(1)}, u32[]{:S(2)}, u32[]{:S(2)}) collective-permute-start(bf16[32,1664]{1,0:T(8,128)(2,1)S(1)} %slots.1), channel_id=1, source_target_pairs={{0,2},{1,3},{2,0},{3,1},{4,6},{5,7},{6,4},{7,5},{8,10},{9,11},{10,... | collective-permute-start | bytes 319496 | tf_op jit(solution)/shard_map/ppermute | solution.py:452
  28.7 5.8 %collective-permute-start.3 = (bf16[32,1664]{1,0:T(8,128)(2,1)S(1)}, bf16[32,1664]{1,0:T(8,128)(2,1)S(1)}, u32[]{:S(2)}, u32[]{:S(2)}) collective-permute-start(bf16[32,1664]{1,0:T(8,128)(2,1)S(1)} %slots.1), channel_id=1, source_target_pairs={{0,1},{1,0},{2,3},{3,2},{4,5},{5,4},{6,7},{7,6},{8,9},{9,8},{10,11... | collective-permute-start | bytes 319496 | tf_op jit(solution)/shard_map/ppermute | solution.py:452
  34.6 12.9 %copy-start = (s32[18]{0:T(128)S(1)}, s32[18]{0:T(128)}, u32[]{:S(2)}) copy-start(s32[18]{0:T(128)} %get-tuple-element.29.loc_ref) | copy-start | bytes 220
  34.6 8.2 %collective-permute-start.8 = (bf16[32,1664]{1,0:T(8,128)(2,1)S(1)}, bf16[32,1664]{1,0:T(8,128)(2,1)S(1)}, u32[]{:S(2)}, u32[]{:S(2)}) collective-permute-start(bf16[32,1664]{1,0:T(8,128)(2,1)S(1)} %add_add_fusion), channel_id=1, source_target_pairs={{0,96},{16,112},{32,64},{48,80},{64,32},{80,48},{96,0},{112,16},{1... | collective-permute-start | bytes 319496 | tf_op jit(solution)/shard_map/ppermute | solution.py:452
  35.6 7.3 %collective-permute-start.7 = (bf16[32,1664]{1,0:T(8,128)(2,1)S(1)}, bf16[32,1664]{1,0:T(8,128)(2,1)S(1)}, u32[]{:S(2)}, u32[]{:S(2)}) collective-permute-start(bf16[32,1664]{1,0:T(8,128)(2,1)S(1)} %add_add_fusion), channel_id=1, source_target_pairs={{0,64},{16,80},{32,96},{48,112},{64,0},{80,16},{96,32},{112,48},{1... | collective-permute-start | bytes 319496 | tf_op jit(solution)/shard_map/ppermute | solution.py:452
  36.8 6.1 %collective-permute-start.6 = (bf16[32,1664]{1,0:T(8,128)(2,1)S(1)}, bf16[32,1664]{1,0:T(8,128)(2,1)S(1)}, u32[]{:S(2)}, u32[]{:S(2)}) collective-permute-start(bf16[32,1664]{1,0:T(8,128)(2,1)S(1)} %add_add_fusion), channel_id=1, source_target_pairs={{0,32},{16,48},{32,0},{48,16},{64,96},{80,112},{96,64},{112,80},{1... | collective-permute-start | bytes 319496 | tf_op jit(solution)/shard_map/ppermute | solution.py:452
  43.0 4.6 %collective-permute-start.9 = (bf16[128,1664]{1,0:T(8,128)(2,1)S(1)}, bf16[128,1664]{1,0:T(8,128)(2,1)S(1)}, u32[]{:S(2)}, u32[]{:S(2)}) collective-permute-start(bf16[128,1664]{1,0:T(8,128)(2,1)S(1)} %constant_dynamic-update-slice_fusion.one_ref), channel_id=1, source_target_pairs={{0,16},{16,0},{32,48},{48,32},{64,80},{80,64},{96,112},{112,96},{1... | collective-permute-start | bytes 1277960 | tf_op jit(solution)/shard_map/ppermute | solution.py:515

commit v9 on v8

--- a/solution.py
+++ b/solution.py
@@ -74,7 +74,9 @@
         j = before + s
         row = jnp.where(s < mine, 2 * lax.rem(j, CLASSES) + s // CLASSES, -1)
         hot = jnp.where((r == row) & (q == 16 * s + lax.rem(idx[s], 16)), 1.0, hot)
-        c = solved_ref[idx[s] // 128, lax.rem(idx[s], 128)].astype(F32)
+        line = solved_ref[pl.ds(idx[s] // 128, 1), :].astype(F32)
+        here = iota((1, 128), 1) == lax.rem(idx[s], 128)
+        c = jnp.sum(jnp.where(here, line, 0.0), axis=1, keepdims=True)
         tag = jnp.where(rc == row, jnp.where(lane == 0, c, (j + 1).astype(F32)), tag)
     hot = hot.astype(BF16)
     for c in copies:
@@ -479,7 +481,7 @@
             jax.ShapeDtypeStruct((CLASSES, 2, width), BF16),
             jax.ShapeDtypeStruct((2 + PMAX,), jnp.int32),
         ),
-        in_specs=[smem, smem, vmem, smem, hbm, hbm],
+        in_specs=[smem, smem, vmem, vmem, hbm, hbm],
         out_specs=(vmem, smem),
         scratch_shapes=[
             pltpu.VMEM((16 * PMAX, dim), BF16),

time: 88 us -> 87.5 us (level)
  no operation moved by 1% of the time
where the time goes in v9:
time: 87.5 us; the launch traced here: 86.9 us
  Pallas kernels  41.9 us (48%)
  blocking collectives  28.5 us (33%)
  starting transfers between devices  13.4 us (15%)
  waiting for transfers between devices  1.42 us (2%)
    pallas_call x1, Pallas kernels, main_call(): pl.pallas_call(main_kernel, out_shape=(jax.ShapeDtypeStruct((rows_here, t...  22.2 us
    all_to_all x1, blocking collectives, body(): peers = lax.all_to_all(best.reshape(NDEV, 1, 128), AXES, 0, 0)  16.7 us
    pallas_call x3, Pallas kernels, norms_part(): pl.pallas_call(functools.partial(norms_kernel, first), out_shape=jax.Shap...  15.7 us
    all_to_all x1, blocking collectives, body(): mine = lax.all_to_all(send, 'rows', 0, 0).reshape(16, width)  11.8 us
    ppermute x9, starting transfers between devices, ring(): return [lax.ppermute(v, axis, p) for v, p in zip(values, pairs)]  10 us
    pallas_call x1, Pallas kernels, body(): pl.pallas_call(own_kernel, out_shape=(jax.ShapeDtypeStruct((CLASSES, 2, w...  3.66 us
    ppermute x1, starting transfers between devices, body(): two = lax.ppermute(one, 'rows', swap)  3.36 us
  transfers between devices with their start and end apart: 10, of which 1 were waited for; matrix products, arithmetic and copies ran while one was open for 0% of the time, Pallas kernels for 18%

profile of v9, /device:TPU:1, one launch (start us, length us, event | category | flops | bytes accessed | tf_op | source)
XLA Modules:
  0.0 86.9 jit_solution(529951139350936967)
XLA Ops:
  0.6 3.7 %own_rows.1 = (bf16[8,2,1664]{2,1,0:T(2,128)(2,1)}, s32[18]{0:T(128)}) custom-call(s32[1]{0:T(128)} %bitcast.dev_ref, s32[256]{0:T(256)} %piv_s.1, s32[2,128]{1,0:T(2,128)} %bitcast.13, s32[56,128]{1,0:T(8,128)} %bitcast.9, bf16[7168,1024]{1,0:T(8,128)(2,1)} %emb_hbm.7, bf16[7168,512]{1,0:T(8,128)(2,1)} %fac_hbm.7), custom_call_target="tpu_custom_call" | custom-call | tf_op jit(solution)/shard_map/own_rows/pallas_call | solution.py:478
  4.3 11.8 %all_to_all.10 = bf16[8,2,1664]{2,1,0:T(2,128)(2,1)S(1)} all-to-all(bf16[8,2,1664]{2,1,0:T(2,128)(2,1)} %get-tuple-element.30), channel_id=1, replica_groups=mesh['rows'=8,'cols'=16] {'rows'}, dimensions={0} | all-to-all | bytes 106496 | tf_op jit(solution)/shard_map/all_to_all | solution.py:494
  16.1 2.4 %collective-permute-start.2 = (bf16[16,1664]{1,0:T(8,128)(2,1)S(1)}, bf16[16,1664]{1,0:T(8,128)(2,1)S(1)}, u32[]{:S(2)}, u32[]{:S(2)}) collective-permute-start(bf16[16,1664]{1,0:T(8,128)(2,1)S(1)} %reshape.31.refs_0_), channel_id=1, source_target_pairs={{0,12},{1,13},{2,14},{3,15},{4,8},{5,9},{6,10},{7,11},{8,4},{9,5},... | collective-permute-start | bytes 159752 | tf_op jit(solution)/shard_map/ppermute | solution.py:454
  18.5 0.5 collective-permute-start.1
  19.0 0.4 collective-permute-start
  19.5 5.4 %row_norms.3.refs_0_ = f32[7168,128]{1,0:T(8,128)} custom-call(s32[56,128]{1,0:T(8,128)} %bitcast.10, bf16[7168,1024]{1,0:T(8,128)(2,1)} %emb_hbm.7, bf16[7168,512]{1,0:T(8,128)(2,1)} %fac_hbm.7), custom_call_target="tpu_custom_call" | custom-call | flops 15728640 | bytes 7864320 | tf_op jit(solution)/shard_map/row_norms/pallas_call | solution.py:432
  24.9 0.0 collective-permute-done.2.refs_3_
  24.9 0.0 collective-permute-done.1.refs_2_
  24.9 0.0 collective-permute-done.refs_1_
  25.0 0.3 slots.1
  25.2 2.7 %collective-permute-start.5 = (bf16[32,1664]{1,0:T(8,128)(2,1)S(1)}, bf16[32,1664]{1,0:T(8,128)(2,1)S(1)}, u32[]{:S(2)}, u32[]{:S(2)}) collective-permute-start(bf16[32,1664]{1,0:T(8,128)(2,1)S(1)} %slots.1), channel_id=1, source_target_pairs={{0,3},{1,2},{2,1},{3,0},{4,7},{5,6},{6,5},{7,4},{8,11},{9,10},{10,... | collective-permute-start | bytes 319496 | tf_op jit(solution)/shard_map/ppermute | solution.py:454
  27.9 0.4 collective-permute-start.4
  28.3 0.3 collective-permute-start.3
  28.6 5.4 %row_norms.4.refs_0_ = f32[7168,128]{1,0:T(8,128)} custom-call(s32[56,128]{1,0:T(8,128)} %bitcast.11, bf16[7168,1024]{1,0:T(8,128)(2,1)} %emb_hbm.7, bf16[7168,512]{1,0:T(8,128)(2,1)} %fac_hbm.7, f32[7168,128]{1,0:T(8,128)} %row_norms.3.refs_0_), custom_call_target="tpu_custom_call", output_to_operand_aliasing={{}: (3, {})} | custom-call | flops 15728640 | bytes 7864320 | tf_op jit(solution)/shard_map/row_norms/pallas_call | solution.py:432
  34.0 0.0 collective-permute-done.5
  34.0 0.0 collective-permute-done.4
  34.0 0.0 collective-permute-done.3
  34.1 0.0 copy-start
  34.1 1.0 %collective-permute-start.8 = (bf16[32,1664]{1,0:T(8,128)(2,1)S(1)}, bf16[32,1664]{1,0:T(8,128)(2,1)S(1)}, u32[]{:S(2)}, u32[]{:S(2)}) collective-permute-start(bf16[32,1664]{1,0:T(8,128)(2,1)S(1)} %add_add_fusion), channel_id=1, source_target_pairs={{0,96},{16,112},{32,64},{48,80},{64,32},{80,48},{96,0},{112,16},{1... | collective-permute-start | bytes 319496 | tf_op jit(solution)/shard_map/ppermute | solution.py:454
  35.1 1.2 %collective-permute-start.7 = (bf16[32,1664]{1,0:T(8,128)(2,1)S(1)}, bf16[32,1664]{1,0:T(8,128)(2,1)S(1)}, u32[]{:S(2)}, u32[]{:S(2)}) collective-permute-start(bf16[32,1664]{1,0:T(8,128)(2,1)S(1)} %add_add_fusion), channel_id=1, source_target_pairs={{0,64},{16,80},{32,96},{48,112},{64,0},{80,16},{96,32},{112,48},{1... | collective-permute-start | bytes 319496 | tf_op jit(solution)/shard_map/ppermute | solution.py:454
  36.3 1.2 %collective-permute-start.6 = (bf16[32,1664]{1,0:T(8,128)(2,1)S(1)}, bf16[32,1664]{1,0:T(8,128)(2,1)S(1)}, u32[]{:S(2)}, u32[]{:S(2)}) collective-permute-start(bf16[32,1664]{1,0:T(8,128)(2,1)S(1)} %add_add_fusion), channel_id=1, source_target_pairs={{0,32},{16,48},{32,0},{48,16},{64,96},{80,112},{96,64},{112,80},{1... | collective-permute-start | bytes 319496 | tf_op jit(solution)/shard_map/ppermute | solution.py:454
  37.4 4.9 %row_norms.5.aux_hbm = f32[7168,128]{1,0:T(8,128)} custom-call(s32[56,128]{1,0:T(8,128)} %bitcast.12, bf16[7168,1024]{1,0:T(8,128)(2,1)} %emb_hbm.7, bf16[7168,512]{1,0:T(8,128)(2,1)} %fac_hbm.7, f32[7168,128]{1,0:T(8,128)} %row_norms.4.refs_0_), custom_call_target="tpu_custom_call", output_to_operand_aliasing={{}: (3, {})} | custom-call | flops 12582912 | bytes 6291456 | tf_op jit(solution)/shard_map/row_norms/pallas_call | solution.py:432
  42.3 0.0 collective-permute-done.8
  42.3 0.0 collective-permute-done.7
  42.3 0.0 collective-permute-done.6
  42.4 3.4 %collective-permute-start.9 = (bf16[128,1664]{1,0:T(8,128)(2,1)S(1)}, bf16[128,1664]{1,0:T(8,128)(2,1)S(1)}, u32[]{:S(2)}, u32[]{:S(2)}) collective-permute-start(bf16[128,1664]{1,0:T(8,128)(2,1)S(1)} %constant_dynamic-update-slice_fusion.one_ref), channel_id=1, source_target_pairs={{0,16},{16,0},{32,48},{48,32},{64,80},{80,64},{96,112},{112,96},{1... | collective-permute-start | bytes 1277960 | tf_op jit(solution)/shard_map/ppermute | solution.py:517
  45.8 1.4 %collective-permute-done.9.two_ref = bf16[128,1664]{1,0:T(8,128)(2,1)S(1)} collective-permute-done((bf16[128,1664]{1,0:T(8,128)(2,1)S(1)}, bf16[128,1664]{1,0:T(8,128)(2,1)S(1)}, u32[]{:S(2)}, u32[]{:S(2)}) %collective-permute-start.9) | collective-permute-done | bytes 426016 | tf_op jit(solution)/shard_map/ppermute | solution.py:517
  47.2 0.0 copy-done
  47.2 22.2 %panel_factor.1 = (bf16[7168,256]{1,0:T(8,128)(2,1)}, f32[56,128]{1,0:T(8,128)}, f32[128,128]{1,0:T(8,128)S(1)}) custom-call(s32[18]{0:T(128)S(1)} %copy-done, bf16[128,1664]{1,0:T(8,128)(2,1)S(1)} %constant_dynamic-update-slice_fusion.one_ref, bf16[128,1664]{1,0:T(8,128)(2,1)S(1)} %collective-permute-done.9.two_ref, f32[7168,128]{1,0:T(8,128)} %row_norms.5.aux_hbm, ...), custom_call_target="tpu_custom_call" | custom-call | tf_op jit(solution)/shard_map/panel_factor/pallas_call | solution.py:391
  69.4 16.7 %all_to_all.11 = f32[128,1,128]{2,1,0:T(1,128)S(1)} all-to-all(f32[128,1,128]{2,1,0:T(1,128)S(1)} %bitcast.8), channel_id=1, replica_groups=mesh['rows'=8,'cols'=16] {'rows','cols'}, dimensions={0} | all-to-all | bytes 131072 | tf_op jit(solution)/shard_map/all_to_all | solution.py:520
  86.1 0.7 reduce_max.9
  (6 shorter events, 0.1 us)
Async XLA Ops:
  16.1 8.8 %collective-permute-start.2 = (bf16[16,1664]{1,0:T(8,128)(2,1)S(1)}, bf16[16,1664]{1,0:T(8,128)(2,1)S(1)}, u32[]{:S(2)}, u32[]{:S(2)}) collective-permute-start(bf16[16,1664]{1,0:T(8,128)(2,1)S(1)} %reshape.31.refs_0_), channel_id=1, source_target_pairs={{0,12},{1,13},{2,14},{3,15},{4,8},{5,9},{6,10},{7,11},{8,4},{9,5},... | collective-permute-start | bytes 159752 | tf_op jit(solution)/shard_map/ppermute | solution.py:454
  18.5 6.4 %collective-permute-start.1 = (bf16[16,1664]{1,0:T(8,128)(2,1)S(1)}, bf16[16,1664]{1,0:T(8,128)(2,1)S(1)}, u32[]{:S(2)}, u32[]{:S(2)}) collective-permute-start(bf16[16,1664]{1,0:T(8,128)(2,1)S(1)} %reshape.31.refs_0_), channel_id=1, source_target_pairs={{0,8},{1,9},{2,10},{3,11},{4,12},{5,13},{6,14},{7,15},{8,0},{9,1},... | collective-permute-start | bytes 159752 | tf_op jit(solution)/shard_map/ppermute | solution.py:454
  19.0 5.9 %collective-permute-start = (bf16[16,1664]{1,0:T(8,128)(2,1)S(1)}, bf16[16,1664]{1,0:T(8,128)(2,1)S(1)}, u32[]{:S(2)}, u32[]{:S(2)}) collective-permute-start(bf16[16,1664]{1,0:T(8,128)(2,1)S(1)} %reshape.31.refs_0_), channel_id=1, source_target_pairs={{0,4},{1,5},{2,6},{3,7},{4,0},{5,1},{6,2},{7,3},{8,12},{9,13},{10,... | collective-permute-start | bytes 159752 | tf_op jit(solution)/shard_map/ppermute | solution.py:454
  25.2 8.8 %collective-permute-start.5 = (bf16[32,1664]{1,0:T(8,128)(2,1)S(1)}, bf16[32,1664]{1,0:T(8,128)(2,1)S(1)}, u32[]{:S(2)}, u32[]{:S(2)}) collective-permute-start(bf16[32,1664]{1,0:T(8,128)(2,1)S(1)} %slots.1), channel_id=1, source_target_pairs={{0,3},{1,2},{2,1},{3,0},{4,7},{5,6},{6,5},{7,4},{8,11},{9,10},{10,... | collective-permute-start | bytes 319496 | tf_op jit(solution)/shard_map/ppermute | solution.py:454
  27.9 6.1 %collective-permute-start.4 = (bf16[32,1664]{1,0:T(8,128)(2,1)S(1)}, bf16[32,1664]{1,0:T(8,128)(2,1)S(1)}, u32[]{:S(2)}, u32[]{:S(2)}) collective-permute-start(bf16[32,1664]{1,0:T(8,128)(2,1)S(1)} %slots.1), channel_id=1, source_target_pairs={{0,2},{1,3},{2,0},{3,1},{4,6},{5,7},{6,4},{7,5},{8,10},{9,11},{10,... | collective-permute-start | bytes 319496 | tf_op jit(solution)/shard_map/ppermute | solution.py:454
  28.3 5.8 %collective-permute-start.3 = (bf16[32,1664]{1,0:T(8,128)(2,1)S(1)}, bf16[32,1664]{1,0:T(8,128)(2,1)S(1)}, u32[]{:S(2)}, u32[]{:S(2)}) collective-permute-start(bf16[32,1664]{1,0:T(8,128)(2,1)S(1)} %slots.1), channel_id=1, source_target_pairs={{0,1},{1,0},{2,3},{3,2},{4,5},{5,4},{6,7},{7,6},{8,9},{9,8},{10,11... | collective-permute-start | bytes 319496 | tf_op jit(solution)/shard_map/ppermute | solution.py:454
  34.1 13.1 %copy-start = (s32[18]{0:T(128)S(1)}, s32[18]{0:T(128)}, u32[]{:S(2)}) copy-start(s32[18]{0:T(128)} %get-tuple-element.29.loc_ref) | copy-start | bytes 220
  34.1 8.2 %collective-permute-start.8 = (bf16[32,1664]{1,0:T(8,128)(2,1)S(1)}, bf16[32,1664]{1,0:T(8,128)(2,1)S(1)}, u32[]{:S(2)}, u32[]{:S(2)}) collective-permute-start(bf16[32,1664]{1,0:T(8,128)(2,1)S(1)} %add_add_fusion), channel_id=1, source_target_pairs={{0,96},{16,112},{32,64},{48,80},{64,32},{80,48},{96,0},{112,16},{1... | collective-permute-start | bytes 319496 | tf_op jit(solution)/shard_map/ppermute | solution.py:454
  35.1 7.3 %collective-permute-start.7 = (bf16[32,1664]{1,0:T(8,128)(2,1)S(1)}, bf16[32,1664]{1,0:T(8,128)(2,1)S(1)}, u32[]{:S(2)}, u32[]{:S(2)}) collective-permute-start(bf16[32,1664]{1,0:T(8,128)(2,1)S(1)} %add_add_fusion), channel_id=1, source_target_pairs={{0,64},{16,80},{32,96},{48,112},{64,0},{80,16},{96,32},{112,48},{1... | collective-permute-start | bytes 319496 | tf_op jit(solution)/shard_map/ppermute | solution.py:454
  36.3 6.1 %collective-permute-start.6 = (bf16[32,1664]{1,0:T(8,128)(2,1)S(1)}, bf16[32,1664]{1,0:T(8,128)(2,1)S(1)}, u32[]{:S(2)}, u32[]{:S(2)}) collective-permute-start(bf16[32,1664]{1,0:T(8,128)(2,1)S(1)} %add_add_fusion), channel_id=1, source_target_pairs={{0,32},{16,48},{32,0},{48,16},{64,96},{80,112},{96,64},{112,80},{1... | collective-permute-start | bytes 319496 | tf_op jit(solution)/shard_map/ppermute | solution.py:454
  42.4 4.8 %collective-permute-start.9 = (bf16[128,1664]{1,0:T(8,128)(2,1)S(1)}, bf16[128,1664]{1,0:T(8,128)(2,1)S(1)}, u32[]{:S(2)}, u32[]{:S(2)}) collective-permute-start(bf16[128,1664]{1,0:T(8,128)(2,1)S(1)} %constant_dynamic-update-slice_fusion.one_ref), channel_id=1, source_target_pairs={{0,16},{16,0},{32,48},{48,32},{64,80},{80,64},{96,112},{112,96},{1... | collective-permute-start | bytes 1277960 | tf_op jit(solution)/shard_map/ppermute | solution.py:517
